TPU v7x, 32 devices: a whole 2x2x4 slice. The times are simulated.
32 devices in a mesh: seq: 32 (over z, y, x, core).
Axes of the slice: x: 2, y: 2, z: 4, core: 2. Of those that a mesh axis runs over, the one named last changes fastest.
Arguments:
- tokens: bfloat16 [2, 8192, 1024], P(None, 'seq'), may hold values from -6 to 6
- ln1_gain: bfloat16 [1024], P('seq'), may hold values from 0.5 to 1.5
- ln1_bias: bfloat16 [1024], P('seq'), may hold values from -1.75 to 1.75
- qkv_weight: bfloat16 [1024, 3072], P('seq'), may hold values from -0.1875 to 0.1875
- q_bias: bfloat16 [1024], P('seq'), may hold values from -1.75 to 1.75
- v_bias: bfloat16 [1024], P('seq'), may hold values from -1.75 to 1.75
- out_weight: bfloat16 [1024, 1024], P('seq'), may hold values from -4 to 4
- out_bias: bfloat16 [1024], P('seq'), may hold values from -1.75 to 1.75
- ln2_gain: bfloat16 [1024], P('seq'), may hold values from 0.5 to 1.5
- ln2_bias: bfloat16 [1024], P('seq'), may hold values from -1.75 to 1.75
- fc1_weight: bfloat16 [1024, 4096], P('seq'), may hold values from -0.1875 to 0.1875
- fc1_bias: bfloat16 [4096], P('seq'), may hold values from -3 to 3
- fc2_weight: bfloat16 [4096, 1024], P('seq'), may hold values from -0.125 to 0.125
- fc2_bias: bfloat16 [1024], P('seq'), may hold values from -1.75 to 1.75
- image_ids: int32 [2, 8192], P(None, 'seq'), may hold values from 0 to 14, as said below
- image_starts: int32 [2, 15], replicated, may hold values from 0 to 8191, as said below
- cotangent: bfloat16 [2, 8192, 1024], P(None, 'seq'), may hold values from -6 to 6
Outputs:
- out: bfloat16 [2, 8192, 1024], P(None, 'seq')
- input_grad: bfloat16 [2, 8192, 1024], P(None, 'seq')
- ln1_gain_grad: float32 [1024], P('seq')
- ln1_bias_grad: float32 [1024], P('seq')
- qkv_weight_grad: float32 [1024, 3072], P('seq')
- q_bias_grad: float32 [1024], P('seq')
- v_bias_grad: float32 [1024], P('seq')
- out_weight_grad: float32 [1024, 1024], P('seq')
- out_bias_grad: float32 [1024], P('seq')
- ln2_gain_grad: float32 [1024], P('seq')
- ln2_bias_grad: float32 [1024], P('seq')
- fc1_weight_grad: float32 [1024, 4096], P('seq')
- fc1_bias_grad: float32 [4096], P('seq')
- fc2_weight_grad: float32 [4096, 1024], P('seq')
- fc2_bias_grad: float32 [1024], P('seq')
Inputs may be any that keep to these rules, and one draw needn't show every extreme that they name: In micro-batch m the images are contiguous runs in order: image i covers positions image_starts[m, i] to image_starts[m, i + 1] - 1 (the last one to 8191) and image_ids[m, t] names the image of position t; every image has exactly 577 tokens except one padding run, at a place drawn from the seed, of 8192 % 577 tokens. image_starts[m, 0] = 0 and the starts rise strictly; every start is a position of the stream.
All inputs are finite; a program needn't handle non-finite values.
Results may differ from a plain program's by a relative error of at most 0.013.
Values may be sent and summed in bfloat16 or wider, within the bound.
No kernel may reach another device: no remote copies, remote signals or barrier semaphores. Data moves between devices by JAX's collectives and lax.ppermute only.
A program may use at most 256 MiB of HBM per device.

v0:
```python
import jax
import jax.numpy as jnp
from jax import lax
from jax.sharding import PartitionSpec as P

HEAD_DIM = 64
IMG_TOK = 577


epsilon = 1e-05
negative_fill = -1e30


def passed_along(block, axis, distance):
    devices = range(lax.axis_size(axis))
    route = [(i - distance, i) for i in devices if i - distance in devices]
    return lax.ppermute(block, axis, route)


def product(left, right):
    return jnp.dot(left, right, preferred_element_type=jnp.float32)


def product_tn(left, right):
    return lax.dot_general(
        left, right, (((0,), (0,)), ((), ())), preferred_element_type=jnp.float32
    )


def product_nt(left, right):
    return lax.dot_general(
        left, right, (((1,), (1,)), ((), ())), preferred_element_type=jnp.float32
    )


def layer_norm_parts(values, gain, shift):
    center = values - jnp.mean(values, axis=-1, keepdims=True)
    inverse = lax.rsqrt(jnp.mean(center * center, axis=-1, keepdims=True) + epsilon)
    normal = center * inverse
    return (normal * gain + shift, normal, inverse)


def layer_norm_back(grad_normed, normal, inverse, gain):
    scaled = grad_normed * gain
    centered = scaled - jnp.mean(scaled, axis=-1, keepdims=True)
    return inverse * (centered - normal * jnp.mean(scaled * normal, axis=-1, keepdims=True))


def allowed_keys(ids_row, starts_row, stream_len, key_places):
    image_count = starts_row.shape[0]
    finish = jnp.concatenate([starts_row[1:], jnp.full((1,), stream_len, jnp.int32)])
    picked = ids_row[:, None] == jnp.arange(image_count, dtype=jnp.int32)[None, :]
    low_bound = jnp.sum(jnp.where(picked, starts_row[None, :], 0), axis=1)
    high_bound = jnp.sum(jnp.where(picked, finish[None, :], 0), axis=1)
    return (key_places[None, :] >= low_bound[:, None]) & (key_places[None, :] < high_bound[:, None])


def head_parts(queries, window, index):
    tok_dev, model_width = queries.shape
    key_span = window.shape[0]
    pair_width = 2 * HEAD_DIM
    column = index * pair_width
    query_part = lax.dynamic_slice_in_dim(queries, column, pair_width, 1).reshape(
        tok_dev, 2, HEAD_DIM
    )
    key_part = lax.dynamic_slice_in_dim(window, column, pair_width, 1).reshape(
        key_span, 2, HEAD_DIM
    )
    value_part = lax.dynamic_slice_in_dim(window, model_width + column, pair_width, 1).reshape(
        key_span, 2, HEAD_DIM
    )
    return (query_part, key_part, value_part)


def masked_scores(query_part, key_part, allowed, score_scale):
    scores = (
        jnp.einsum("thd,shd->hts", query_part, key_part, preferred_element_type=jnp.float32)
        * score_scale
    )
    return jnp.where(allowed[None], scores, negative_fill)


def attend_forward(queries, window, allowed, score_scale):
    tok_dev, model_width = queries.shape
    pair_width = 2 * HEAD_DIM

    def one_group(index):
        query_part, key_part, value_part = head_parts(queries, window, index)
        scores = masked_scores(query_part, key_part, allowed, score_scale)
        peak = jnp.max(scores, axis=-1, keepdims=True)
        exponent = jnp.exp(scores - peak)
        totals = jnp.sum(exponent, axis=-1, keepdims=True)
        share_low = (exponent / totals).astype(jnp.bfloat16)
        mixed = jnp.einsum(
            "hts,shd->thd", share_low, value_part, preferred_element_type=jnp.float32
        )
        return (mixed.reshape(tok_dev, pair_width), peak[..., 0], totals[..., 0])

    mixed, peaks, totals = lax.map(
        one_group, jnp.arange(model_width // pair_width, dtype=jnp.int32)
    )
    mixed = jnp.moveaxis(mixed, 0, 1).reshape(tok_dev, model_width)
    return (mixed.astype(jnp.bfloat16), peaks, totals)


def attend_backward(queries, window, allowed, peaks, totals, grad_mixed, score_scale):
    tok_dev, model_width = queries.shape
    key_span = window.shape[0]
    pair_width = 2 * HEAD_DIM

    def one_group(inputs):
        index, peak, total = inputs
        query_part, key_part, value_part = head_parts(queries, window, index)
        scores = masked_scores(query_part, key_part, allowed, score_scale)
        shares = jnp.exp(scores - peak[..., None]) / total[..., None]
        share_low = shares.astype(jnp.bfloat16)
        grad_part = lax.dynamic_slice_in_dim(grad_mixed, index * pair_width, pair_width, 1).reshape(
            tok_dev, 2, HEAD_DIM
        )
        grad_value = jnp.einsum(
            "hts,thd->shd", share_low, grad_part, preferred_element_type=jnp.float32
        )
        grad_share = jnp.einsum(
            "thd,shd->hts", grad_part, value_part, preferred_element_type=jnp.float32
        )
        row_dot = jnp.sum(grad_share * shares, axis=-1, keepdims=True)
        grad_scores = (shares * (grad_share - row_dot)).astype(jnp.bfloat16)
        grad_query = (
            jnp.einsum("hts,shd->thd", grad_scores, key_part, preferred_element_type=jnp.float32)
            * score_scale
        )
        grad_key = (
            jnp.einsum("hts,thd->shd", grad_scores, query_part, preferred_element_type=jnp.float32)
            * score_scale
        )
        return (
            grad_query.reshape(tok_dev, pair_width),
            grad_key.reshape(key_span, pair_width),
            grad_value.reshape(key_span, pair_width),
        )

    group_index = jnp.arange(model_width // pair_width, dtype=jnp.int32)
    grad_query, grad_key, grad_value = lax.map(one_group, (group_index, peaks, totals))
    grad_query = jnp.moveaxis(grad_query, 0, 1).reshape(tok_dev, model_width)
    grad_key = jnp.moveaxis(grad_key, 0, 1).reshape(key_span, model_width)
    grad_value = jnp.moveaxis(grad_value, 0, 1).reshape(key_span, model_width)
    return (grad_query, jnp.concatenate([grad_key, grad_value], axis=1))


def forward_micro(weights_full, stream_low, allowed, reach_blocks, offsets, score_scale):
    (
        gain_one,
        shift_one,
        qkv_full,
        q_shift,
        v_shift,
        out_full,
        out_shift,
        gain_two,
        shift_two,
        up_full,
        up_shift,
        down_full,
        down_shift,
    ) = weights_full
    model_width = stream_low.shape[1]
    stream = stream_low.astype(jnp.float32)
    normed, normal_one, inverse_one = layer_norm_parts(
        stream, gain_one.astype(jnp.float32), shift_one.astype(jnp.float32)
    )
    normed_low = normed.astype(jnp.bfloat16)
    joined = product(normed_low, qkv_full)
    queries = (joined[:, :model_width] + q_shift.astype(jnp.float32)).astype(jnp.bfloat16)
    key_low = joined[:, model_width : 2 * model_width].astype(jnp.bfloat16)
    value_low = (joined[:, 2 * model_width :] + v_shift.astype(jnp.float32)).astype(jnp.bfloat16)
    own_pairs = jnp.concatenate([key_low, value_low], axis=1)
    received = [passed_along(own_pairs, "seq", offset) for offset in offsets]
    window = jnp.concatenate(
        received[:reach_blocks] + [own_pairs] + received[reach_blocks:], axis=0
    )
    mixed_low, peaks, totals = attend_forward(queries, window, allowed, score_scale)
    middle = stream + product(mixed_low, out_full) + out_shift.astype(jnp.float32)
    normed_two, normal_two, inverse_two = layer_norm_parts(
        middle, gain_two.astype(jnp.float32), shift_two.astype(jnp.float32)
    )
    normed_two_low = normed_two.astype(jnp.bfloat16)
    hidden = product(normed_two_low, up_full) + up_shift.astype(jnp.float32)
    active_low = (hidden * jax.nn.sigmoid(1.702 * hidden)).astype(jnp.bfloat16)
    result = middle + product(active_low, down_full) + down_shift.astype(jnp.float32)
    saved = (
        normal_one,
        inverse_one,
        normed_low,
        queries,
        window,
        peaks,
        totals,
        mixed_low,
        normal_two,
        inverse_two,
        normed_two_low,
        hidden,
        active_low,
    )
    return (result.astype(jnp.bfloat16), saved)


def backward_micro(weights_back, saved, cotangent_row, allowed, reach_blocks, offsets, score_scale):
    (
        gain_one,
        shift_one,
        qkv_full,
        q_shift,
        v_shift,
        out_full,
        out_shift,
        gain_two,
        shift_two,
        up_full,
        up_shift,
        down_full,
        down_shift,
    ) = weights_back
    (
        normal_one,
        inverse_one,
        normed_low,
        queries,
        window,
        peaks,
        totals,
        mixed_low,
        normal_two,
        inverse_two,
        normed_two_low,
        hidden,
        active_low,
    ) = saved
    tok_dev, model_width = queries.shape
    grad_output = cotangent_row.astype(jnp.float32)
    grad_down = product_tn(active_low, cotangent_row)
    grad_down_shift = jnp.sum(cotangent_row.astype(jnp.float32), axis=0)
    grad_active = product_nt(cotangent_row, down_full)
    gate = jax.nn.sigmoid(1.702 * hidden)
    grad_hidden_low = (grad_active * (gate + 1.702 * hidden * gate * (1.0 - gate))).astype(
        jnp.bfloat16
    )
    grad_up = product_tn(normed_two_low, grad_hidden_low)
    grad_up_shift = jnp.sum(grad_hidden_low.astype(jnp.float32), axis=0)
    grad_normed_two = product_nt(grad_hidden_low, up_full)
    grad_gain_two = jnp.sum(grad_normed_two * normal_two, axis=0)
    grad_shift_two = jnp.sum(grad_normed_two, axis=0)
    grad_middle = grad_output + layer_norm_back(
        grad_normed_two, normal_two, inverse_two, gain_two.astype(jnp.float32)
    )
    grad_branch_low = grad_middle.astype(jnp.bfloat16)
    grad_out_weight = product_tn(mixed_low, grad_branch_low)
    grad_out_shift = jnp.sum(grad_branch_low.astype(jnp.float32), axis=0)
    grad_mixed_low = product_nt(grad_branch_low, out_full).astype(jnp.bfloat16)
    grad_query, grad_window = attend_backward(
        queries, window, allowed, peaks, totals, grad_mixed_low, score_scale
    )
    collected = grad_window[reach_blocks * tok_dev : (reach_blocks + 1) * tok_dev]
    for offset in offsets:
        block_index = reach_blocks - offset
        piece = grad_window[block_index * tok_dev : (block_index + 1) * tok_dev]
        collected = collected + passed_along(piece.astype(jnp.bfloat16), "seq", -offset).astype(
            piece.dtype
        )
    grad_key_low = collected[:, :model_width].astype(jnp.bfloat16)
    grad_value_low = collected[:, model_width:].astype(jnp.bfloat16)
    grad_query_low = grad_query.astype(jnp.bfloat16)
    grad_joined = jnp.concatenate([grad_query_low, grad_key_low, grad_value_low], axis=1)
    grad_qkv = product_tn(normed_low, grad_joined)
    grad_q_shift = jnp.sum(grad_query_low.astype(jnp.float32), axis=0)
    grad_v_shift = jnp.sum(grad_value_low.astype(jnp.float32), axis=0)
    grad_normed = product_nt(grad_joined, qkv_full)
    grad_gain_one = jnp.sum(grad_normed * normal_one, axis=0)
    grad_shift_one = jnp.sum(grad_normed, axis=0)
    grad_stream = grad_middle + layer_norm_back(
        grad_normed, normal_one, inverse_one, gain_one.astype(jnp.float32)
    )
    grads = (
        grad_gain_one,
        grad_shift_one,
        grad_qkv,
        grad_q_shift,
        grad_v_shift,
        grad_out_weight,
        grad_out_shift,
        grad_gain_two,
        grad_shift_two,
        grad_up,
        grad_up_shift,
        grad_down,
        grad_down_shift,
    )
    return (grad_stream.astype(jnp.bfloat16), grads)


def body(
    tokens,
    ln1_gain,
    ln1_bias,
    qkv_weight,
    q_bias,
    v_bias,
    out_weight,
    out_bias,
    ln2_gain,
    ln2_bias,
    fc1_weight,
    fc1_bias,
    fc2_weight,
    fc2_bias,
    image_ids,
    image_starts,
    cotangent,
):
    micro_count, tok_dev, model_width = tokens.shape
    stream_len = tok_dev * lax.axis_size("seq")
    reach_blocks = (IMG_TOK + tok_dev - 2) // tok_dev
    key_span = (2 * reach_blocks + 1) * tok_dev
    score_scale = HEAD_DIM ** (-0.5)
    own_start = lax.axis_index("seq") * tok_dev
    key_places = own_start - reach_blocks * tok_dev + jnp.arange(key_span, dtype=jnp.int32)
    offsets = list(range(reach_blocks, 0, -1)) + list(range(-1, -reach_blocks - 1, -1))
    weights_full = (
        lax.all_gather(ln1_gain, "seq", axis=0, tiled=True),
        lax.all_gather(ln1_bias, "seq", axis=0, tiled=True),
        lax.all_gather(qkv_weight, "seq", axis=0, tiled=True),
        lax.all_gather(q_bias, "seq", axis=0, tiled=True),
        lax.all_gather(v_bias, "seq", axis=0, tiled=True),
        lax.all_gather(out_weight, "seq", axis=0, tiled=True),
        lax.all_gather(out_bias, "seq", axis=0, tiled=True),
        lax.all_gather(ln2_gain, "seq", axis=0, tiled=True),
        lax.all_gather(ln2_bias, "seq", axis=0, tiled=True),
        lax.all_gather(fc1_weight, "seq", axis=0, tiled=True),
        lax.all_gather(fc1_bias, "seq", axis=0, tiled=True),
        lax.all_gather(fc2_weight, "seq", axis=0, tiled=True),
        lax.all_gather(fc2_bias, "seq", axis=0, tiled=True),
    )
    outputs = []
    saved_all = []
    masks = []
    for micro_index in range(micro_count):
        allowed = allowed_keys(
            image_ids[micro_index], image_starts[micro_index], stream_len, key_places
        )
        result, saved = forward_micro(
            weights_full, tokens[micro_index], allowed, reach_blocks, offsets, score_scale
        )
        outputs.append(result)
        saved_all.append(saved)
        masks.append(allowed)
    weights_back = (
        lax.all_gather(ln1_gain, "seq", axis=0, tiled=True),
        lax.all_gather(ln1_bias, "seq", axis=0, tiled=True),
        lax.all_gather(qkv_weight, "seq", axis=0, tiled=True),
        lax.all_gather(q_bias, "seq", axis=0, tiled=True),
        lax.all_gather(v_bias, "seq", axis=0, tiled=True),
        lax.all_gather(out_weight, "seq", axis=0, tiled=True),
        lax.all_gather(out_bias, "seq", axis=0, tiled=True),
        lax.all_gather(ln2_gain, "seq", axis=0, tiled=True),
        lax.all_gather(ln2_bias, "seq", axis=0, tiled=True),
        lax.all_gather(fc1_weight, "seq", axis=0, tiled=True),
        lax.all_gather(fc1_bias, "seq", axis=0, tiled=True),
        lax.all_gather(fc2_weight, "seq", axis=0, tiled=True),
        lax.all_gather(fc2_bias, "seq", axis=0, tiled=True),
    )
    grad_inputs = []
    sums = None
    for micro_index in range(micro_count):
        grad_stream, grads = backward_micro(
            weights_back,
            saved_all[micro_index],
            cotangent[micro_index],
            masks[micro_index],
            reach_blocks,
            offsets,
            score_scale,
        )
        grad_inputs.append(grad_stream)
        if micro_index == 0:
            sums = tuple(grads)
        else:
            sums = tuple(jax.tree.map(jnp.add, list(sums), list(grads)))
    owned = (
        lax.psum_scatter(sums[0], "seq", scatter_dimension=0, tiled=True),
        lax.psum_scatter(sums[1], "seq", scatter_dimension=0, tiled=True),
        lax.psum_scatter(sums[2], "seq", scatter_dimension=0, tiled=True),
        lax.psum_scatter(sums[3], "seq", scatter_dimension=0, tiled=True),
        lax.psum_scatter(sums[4], "seq", scatter_dimension=0, tiled=True),
        lax.psum_scatter(sums[5], "seq", scatter_dimension=0, tiled=True),
        lax.psum_scatter(sums[6], "seq", scatter_dimension=0, tiled=True),
        lax.psum_scatter(sums[7], "seq", scatter_dimension=0, tiled=True),
        lax.psum_scatter(sums[8], "seq", scatter_dimension=0, tiled=True),
        lax.psum_scatter(sums[9], "seq", scatter_dimension=0, tiled=True),
        lax.psum_scatter(sums[10], "seq", scatter_dimension=0, tiled=True),
        lax.psum_scatter(sums[11], "seq", scatter_dimension=0, tiled=True),
        lax.psum_scatter(sums[12], "seq", scatter_dimension=0, tiled=True),
    )
    return (
        jnp.stack(outputs),
        jnp.stack(grad_inputs),
        owned[0],
        owned[1],
        owned[2],
        owned[3],
        owned[4],
        owned[5],
        owned[6],
        owned[7],
        owned[8],
        owned[9],
        owned[10],
        owned[11],
        owned[12],
    )


def solution(mesh):
    return jax.shard_map(
        body,
        mesh=mesh,
        in_specs=(
            P(None, "seq", None),
            P("seq"),
            P("seq"),
            P("seq", None),
            P("seq"),
            P("seq"),
            P("seq", None),
            P("seq"),
            P("seq"),
            P("seq"),
            P("seq", None),
            P("seq"),
            P("seq", None),
            P("seq"),
            P(None, "seq"),
            P(),
            P(None, "seq", None),
        ),
        out_specs=(
            P(None, "seq", None),
            P(None, "seq", None),
            P("seq"),
            P("seq"),
            P("seq", None),
            P("seq"),
            P("seq"),
            P("seq", None),
            P("seq"),
            P("seq"),
            P("seq"),
            P("seq", None),
            P("seq"),
            P("seq", None),
            P("seq"),
        ),
        check_vma=False,
    )
```

profile of v0, /device:TPU:0, one launch (start us, length us, event | category | flops | bytes accessed | tf_op | source)
XLA Modules:
  0.0 1591.2 jit_solution(13706599040672827298)
XLA Ops:
  19.8 42.6 %all-reduce.18 = (bf16[1024]{0:T(1024)(128)(2,1)S(1)}, bf16[1024]{0:T(1024)(128)(2,1)S(1)}, bf16[1024]{0:T(1024)(128)(2,1)S(1)}, bf16[1024]{0:T(1024)(128)(2,1)S...) all-reduce(bf16[1024]{0:T(1024)(128)(2,1)S(1)} %dynamic-update-slic, ...), channel_id=1, replica_groups=mesh['seq'=32] {'seq'}, use_global_device_ids=true, to_apply=%add.1 | all-reduce | flops 8192 | bytes 32768
  63.3 20.0 %all-gather.6.cloned.1.call-done = bf16[1024,3072]{1,0:T(8,128)(2,1)} async-done(((bf16[32,3072]{1,0:T(8,128)(2,1)}), bf16[1024,3072]{1,0:T(8,128)(2,1)}) %all-gather.6.cloned.1.call-update) | async-done | bytes 6291472 | tf_op jit(solution)/shard_map/all_gather | solution.py:331
  97.3 51.8 %all-gather = bf16[32,1,128]{2,1,0:T(2,128)(2,1)S(1)} all-gather(bf16[1,1,128]{2,1,0:T(2,128)(2,1)S(1)} %bitcast.420), channel_id=1, replica_groups=mesh['seq'=32] {'seq'}, dimensions={0}, use_global_device_ids=true | all-gather | bytes 8448 | tf_op jit(solution)/shard_map/all_gather | solution.py:339
  172.4 60.0 %collective-permute-done.7 = bf16[256,2048]{1,0:T(8,128)(2,1)} collective-permute-done((bf16[256,2048]{1,0:T(8,128)(2,1)}, bf16[256,2048]{1,0:T(8,128)(2,1)}, u32[]{:S(2)}, u32[]{:S(2)}) %collective-permute-start.7) | collective-permute-done | bytes 1048608 | tf_op jit(solution)/shard_map/ppermute | solution.py:17
  238.5 22.3 %collective-permute-start.1 = (bf16[256,2048]{1,0:T(8,128)(2,1)}, bf16[256,2048]{1,0:T(8,128)(2,1)}, u32[]{:S(2)}, u32[]{:S(2)}) collective-permute-start(bf16[256,2048]{1,0:T(8,128)(2,1)} %pad_maximum_fusion.4), channel_id=1, source_target_pairs={{0,2},{1,3},{2,4},{3,5},{4,6},{5,7},{6,8},{7,9},{8,10},{9,11},{10,... | collective-permute-start | bytes 3145736 | tf_op jit(solution)/shard_map/ppermute | solution.py:17
  275.0 10.0 copy.54
  285.1 51.3 %while.69 = (s32[]{:T(128)}, bf16[8,256,128]{1,2,0:T(8,128)(2,1)S(1)}, f32[8,2,256]{2,1,0:T(2,128)S(1)}, f32[8,2,256]{2,1,0:T(2,128)S(1)}, s32[8]{0:T(128)S(1)},...) while((s32[]{:T(128)}, ...), condition=%wide.region_17.18_spmd.clone, body=%wide.region_14.17_spmd.clone.sunk | while | flops 243596288 | bytes 15101222 | solution.py:99
  357.8 10.1 copy.52
  370.1 61.3 %while.68 = (s32[]{:T(128)}, bf16[8,256,128]{1,2,0:T(8,128)(2,1)S(1)}, f32[8,2,256]{2,1,0:T(2,128)}, f32[8,2,256]{2,1,0:T(2,128)}, s32[8]{0:T(128)S(1)}, /*index...) while((s32[]{:T(128)}, ...), condition=%wide.region_7.8_spmd.clone, body=%wide.region_4.7_spmd.clone.sunk | while | flops 243596288 | bytes 15101534 | solution.py:99
  434.9 8.4 convolution_add_fusion.3
  447.7 8.8 convert_reduce_fusion
  470.1 7.8 multiply_reduce_fusion.3
  490.3 129.4 %while.71 = (s32[]{:T(128)}, bf16[8,256,128]{1,2,0:T(8,128)(2,1)}, f32[8,1792,128]{1,2,0:T(8,128)}, f32[8,1792,128]{1,2,0:T(8,128)}, s32[8]{0:T(128)S(1)}, /*ind...) while((s32[]{:T(128)}, bf16[8,256,128]{1,2,0:T(8,128)(2,1)}, ...), condition=%wide.region_31.32_spmd.clone, body=%wide.region_29.31_spmd.clone.sunk | while | flops 598048256 | bytes 52716900 | solution.py:143
  628.8 20.0 %collective-permute-start.23 = (bf16[256,2048]{0,1:T(8,128)(2,1)}, bf16[256,2048]{0,1:T(8,128)(2,1)}, u32[]{:S(2)}, u32[]{:S(2)}) collective-permute-start(bf16[256,2048]{0,1:T(8,128)(2,1)} %get-tuple-element.933), channel_id=1, source_target_pairs={{0,3},{1,4},{2,5},{3,6},{4,7},{5,8},{6,9},{7,10},{8,11},{9,12},{10... | collective-permute-start | bytes 3145736 | tf_op jit(solution)/shard_map/ppermute | solution.py:17
  662.6 124.9 %while.70 = (s32[]{:T(128)}, bf16[8,256,128]{1,2,0:T(8,128)(2,1)S(1)}, f32[8,1792,128]{1,2,0:T(8,128)}, f32[8,1792,128]{1,2,0:T(8,128)}, s32[8]{0:T(128)S(1)}, /...) while((s32[]{:T(128)}, ...), condition=%wide.region_24.25_spmd.clone, body=%wide.region_22.24_spmd.clone.sunk | while | flops 598048256 | bytes 52716900 | solution.py:143
  787.6 7.5 fusion.21
  796.5 9.5 collective-permute-start.17
  812.8 23.2 %collective-permute-done.17 = bf16[256,2048]{0,1:T(8,128)(2,1)S(1)} collective-permute-done((bf16[256,2048]{0,1:T(8,128)(2,1)}, bf16[256,2048]{0,1:T(8,128)(2,1)S(1)}, u32[]{:S(2)}, u32[]{:S(2)}) %collective-permute-start.17) | collective-permute-done | bytes 1048608 | tf_op jit(solution)/shard_map/ppermute | solution.py:17
  837.3 21.6 %collective-permute-done.16 = bf16[256,2048]{0,1:T(8,128)(2,1)S(1)} collective-permute-done((bf16[256,2048]{0,1:T(8,128)(2,1)S(1)}, bf16[256,2048]{0,1:T(8,128)(2,1)S(1)}, u32[]{:S(2)}, u32[]{:S(2)}) %collective-permute-start.16) | collective-permute-done | bytes 1048608 | tf_op jit(solution)/shard_map/ppermute | solution.py:17
  869.2 30.4 %collective-permute-done.13 = bf16[256,2048]{0,1:T(8,128)(2,1)S(1)} collective-permute-done((bf16[256,2048]{0,1:T(8,128)(2,1)S(1)}, bf16[256,2048]{0,1:T(8,128)(2,1)S(1)}, u32[]{:S(2)}, u32[]{:S(2)}) %collective-permute-start.13) | collective-permute-done | bytes 1048608 | tf_op jit(solution)/shard_map/ppermute | solution.py:17
  900.8 12.7 collective-permute-done.12
  919.0 10.0 collective-permute-done.22
  929.0 41.1 %collective-permute-done.19 = bf16[256,2048]{0,1:T(8,128)(2,1)} collective-permute-done((bf16[256,2048]{0,1:T(8,128)(2,1)}, bf16[256,2048]{0,1:T(8,128)(2,1)}, u32[]{:S(2)}, u32[]{:S(2)}) %collective-permute-start.19) | collective-permute-done | bytes 1048608 | tf_op jit(solution)/shard_map/ppermute | solution.py:17
  970.1 18.2 %collective-permute-done.18 = bf16[256,2048]{0,1:T(8,128)(2,1)} collective-permute-done((bf16[256,2048]{0,1:T(8,128)(2,1)S(1)}, bf16[256,2048]{0,1:T(8,128)(2,1)}, u32[]{:S(2)}, u32[]{:S(2)}) %collective-permute-start.18) | collective-permute-done | bytes 1048608 | tf_op jit(solution)/shard_map/ppermute | solution.py:17
  1004.9 10.2 convolution_add_fusion.1
  1015.2 10.7 fusion.91
  1025.9 10.8 convolution_add_fusion
  1038.1 7.3 fusion.60
  1058.5 103.7 %all-reduce.17 = (f32[1024]{0:T(1024)S(1)}, f32[1024]{0:T(1024)S(1)}, f32[1024]{0:T(1024)S(1)}, f32[1024]{0:T(1024)S(1)}, f32[1024]{0:T(1024)S(1)}, /*index=5*/f...) all-reduce(f32[1024]{0:T(1024)S(1)} %add.452, ...), channel_id=2, replica_groups=mesh['seq'=32] {'seq'}, use_global_device_ids=true, to_apply=%region_36.37.clone | all-reduce | flops 12288 | bytes 98304
  1171.2 40.7 %reduce-scatter.5.cloned.1.call-done = f32[32,3072]{1,0:T(8,128)} async-done(((f32[1024,3072]{1,0:T(8,128)}), f32[32,3072]{1,0:T(8,128)}) %reduce-scatter.5.cloned.1.call-update) | async-done | bytes 393232 | tf_op jit(solution)/shard_map/reduce_scatter | solution.py:391
  1211.9 184.8 %reduce-scatter.9.cloned.1.call-done = f32[32,4096]{1,0:T(8,128)} async-done(((f32[1024,4096]{1,0:T(8,128)}), f32[32,4096]{1,0:T(8,128)}) %reduce-scatter.9.cloned.1.call-update) | async-done | bytes 524304 | tf_op jit(solution)/shard_map/reduce_scatter | solution.py:398
  1396.7 187.5 %reduce-scatter.11.cloned.1.call-done = f32[128,1024]{1,0:T(8,128)} async-done(((f32[4096,1024]{1,0:T(8,128)}), f32[128,1024]{1,0:T(8,128)}) %reduce-scatter.11.cloned.1.call-update) | async-done | bytes 524304 | tf_op jit(solution)/shard_map/reduce_scatter | solution.py:400
  (864 shorter events, 560.3 us)
Async XLA Ops:
  7.2 76.1 %all-gather.6.cloned.1.call-start = ((), (), s32[]{:S(2)}) async-start(), calls=%async_computation.4 | async-start | bytes 6488064 | tf_op jit(solution)/shard_map/all_gather | solution.py:331
  7.9 328.6 %all-gather.8.cloned.1.call-start = ((), (), s32[]{:S(2)}) async-start(), calls=%async_computation.5 | async-start | bytes 2162688 | tf_op jit(solution)/shard_map/all_gather | solution.py:334
  8.7 426.1 %all-gather.10.cloned.1.call-start = ((), (), s32[]{:S(2)}) async-start(), calls=%async_computation.6 | async-start | bytes 8650752 | tf_op jit(solution)/shard_map/all_gather | solution.py:338
  9.4 438.3 %all-gather.12.cloned.1.call-start = ((), (), s32[]{:S(2)}) async-start(), calls=%async_computation.7 | async-start | bytes 8650752 | tf_op jit(solution)/shard_map/all_gather | solution.py:340
  10.0 1161.2 %reduce-scatter.7.cloned.1.call-start = ((), (), s32[]{:S(2)}) async-start(), calls=%async_computation.9 | async-start | bytes 4325376 | tf_op jit(solution)/shard_map/reduce_scatter | solution.py:394
  93.5 75.3 %collective-permute-start.6 = (bf16[256,2048]{1,0:T(8,128)(2,1)}, bf16[256,2048]{1,0:T(8,128)(2,1)}, u32[]{:S(2)}, u32[]{:S(2)}) collective-permute-start(bf16[256,2048]{1,0:T(8,128)(2,1)} %pad_maximum_fusion.5), channel_id=1, source_target_pairs={{0,3},{1,4},{2,5},{3,6},{4,7},{5,8},{6,9},{7,10},{8,11},{9,12},{10... | collective-permute-start | bytes 3145736 | tf_op jit(solution)/shard_map/ppermute | solution.py:17
  149.8 82.6 %collective-permute-start.7 = (bf16[256,2048]{1,0:T(8,128)(2,1)}, bf16[256,2048]{1,0:T(8,128)(2,1)}, u32[]{:S(2)}, u32[]{:S(2)}) collective-permute-start(bf16[256,2048]{1,0:T(8,128)(2,1)} %pad_maximum_fusion.5), channel_id=1, source_target_pairs={{0,2},{1,3},{2,4},{3,5},{4,6},{5,7},{6,8},{7,9},{8,10},{9,11},{10,... | collective-permute-start | bytes 3145736 | tf_op jit(solution)/shard_map/ppermute | solution.py:17
  155.2 83.3 %collective-permute-start.8 = (bf16[256,2048]{1,0:T(8,128)(2,1)}, bf16[256,2048]{1,0:T(8,128)(2,1)}, u32[]{:S(2)}, u32[]{:S(2)}) collective-permute-start(bf16[256,2048]{1,0:T(8,128)(2,1)} %pad_maximum_fusion.5), channel_id=1, source_target_pairs={{0,1},{1,2},{2,3},{3,4},{4,5},{5,6},{6,7},{7,8},{8,9},{9,10},{10,1... | collective-permute-start | bytes 3145736 | tf_op jit(solution)/shard_map/ppermute | solution.py:17
  158.9 105.3 %collective-permute-start.9 = (bf16[256,2048]{1,0:T(8,128)(2,1)}, bf16[256,2048]{1,0:T(8,128)(2,1)}, u32[]{:S(2)}, u32[]{:S(2)}) collective-permute-start(bf16[256,2048]{1,0:T(8,128)(2,1)} %pad_maximum_fusion.5), channel_id=1, source_target_pairs={{1,0},{2,1},{3,2},{4,3},{5,4},{6,5},{7,6},{8,7},{9,8},{10,9},{11,1... | collective-permute-start | bytes 3145736 | tf_op jit(solution)/shard_map/ppermute | solution.py:17
  160.2 108.5 %collective-permute-start.10 = (bf16[256,2048]{1,0:T(8,128)(2,1)}, bf16[256,2048]{1,0:T(8,128)(2,1)}, u32[]{:S(2)}, u32[]{:S(2)}) collective-permute-start(bf16[256,2048]{1,0:T(8,128)(2,1)} %pad_maximum_fusion.5), channel_id=1, source_target_pairs={{2,0},{3,1},{4,2},{5,3},{6,4},{7,5},{8,6},{9,7},{10,8},{11,9},{12,... | collective-permute-start | bytes 3145736 | tf_op jit(solution)/shard_map/ppermute | solution.py:17
  168.8 103.6 %collective-permute-start.11 = (bf16[256,2048]{1,0:T(8,128)(2,1)}, bf16[256,2048]{1,0:T(8,128)(2,1)S(1)}, u32[]{:S(2)}, u32[]{:S(2)}) collective-permute-start(bf16[256,2048]{1,0:T(8,128)(2,1)} %pad_maximum_fusion.5), channel_id=1, source_target_pairs={{3,0},{4,1},{5,2},{6,3},{7,4},{8,5},{9,6},{10,7},{11,8},{12,9},{13... | collective-permute-start | bytes 3145736 | tf_op jit(solution)/shard_map/ppermute | solution.py:17
  232.4 106.7 %collective-permute-start = (bf16[256,2048]{1,0:T(8,128)(2,1)}, bf16[256,2048]{1,0:T(8,128)(2,1)}, u32[]{:S(2)}, u32[]{:S(2)}) collective-permute-start(bf16[256,2048]{1,0:T(8,128)(2,1)} %pad_maximum_fusion.4), channel_id=1, source_target_pairs={{0,3},{1,4},{2,5},{3,6},{4,7},{5,8},{6,9},{7,10},{8,11},{9,12},{10... | collective-permute-start | bytes 3145736 | tf_op jit(solution)/shard_map/ppermute | solution.py:17
  238.5 104.4 %collective-permute-start.1 = (bf16[256,2048]{1,0:T(8,128)(2,1)}, bf16[256,2048]{1,0:T(8,128)(2,1)}, u32[]{:S(2)}, u32[]{:S(2)}) collective-permute-start(bf16[256,2048]{1,0:T(8,128)(2,1)} %pad_maximum_fusion.4), channel_id=1, source_target_pairs={{0,2},{1,3},{2,4},{3,5},{4,6},{5,7},{6,8},{7,9},{8,10},{9,11},{10,... | collective-permute-start | bytes 3145736 | tf_op jit(solution)/shard_map/ppermute | solution.py:17
  264.2 81.1 %collective-permute-start.2 = (bf16[256,2048]{1,0:T(8,128)(2,1)}, bf16[256,2048]{1,0:T(8,128)(2,1)}, u32[]{:S(2)}, u32[]{:S(2)}) collective-permute-start(bf16[256,2048]{1,0:T(8,128)(2,1)} %pad_maximum_fusion.4), channel_id=1, source_target_pairs={{0,1},{1,2},{2,3},{3,4},{4,5},{5,6},{6,7},{7,8},{8,9},{9,10},{10,1... | collective-permute-start | bytes 3145736 | tf_op jit(solution)/shard_map/ppermute | solution.py:17
  268.8 79.9 %collective-permute-start.3 = (bf16[256,2048]{1,0:T(8,128)(2,1)}, bf16[256,2048]{1,0:T(8,128)(2,1)}, u32[]{:S(2)}, u32[]{:S(2)}) collective-permute-start(bf16[256,2048]{1,0:T(8,128)(2,1)} %pad_maximum_fusion.4), channel_id=1, source_target_pairs={{1,0},{2,1},{3,2},{4,3},{5,4},{6,5},{7,6},{8,7},{9,8},{10,9},{11,1... | collective-permute-start | bytes 3145736 | tf_op jit(solution)/shard_map/ppermute | solution.py:17
  272.4 78.6 %collective-permute-start.4 = (bf16[256,2048]{1,0:T(8,128)(2,1)}, bf16[256,2048]{1,0:T(8,128)(2,1)}, u32[]{:S(2)}, u32[]{:S(2)}) collective-permute-start(bf16[256,2048]{1,0:T(8,128)(2,1)} %pad_maximum_fusion.4), channel_id=1, source_target_pairs={{2,0},{3,1},{4,2},{5,3},{6,4},{7,5},{8,6},{9,7},{10,8},{11,9},{12,... | collective-permute-start | bytes 3145736 | tf_op jit(solution)/shard_map/ppermute | solution.py:17
  339.1 17.6 %collective-permute-start.5 = (bf16[256,2048]{1,0:T(8,128)(2,1)}, bf16[256,2048]{1,0:T(8,128)(2,1)S(1)}, u32[]{:S(2)}, u32[]{:S(2)}) collective-permute-start(bf16[256,2048]{1,0:T(8,128)(2,1)} %pad_maximum_fusion.4), channel_id=1, source_target_pairs={{3,0},{4,1},{5,2},{6,3},{7,4},{8,5},{9,6},{10,7},{11,8},{12,9},{13... | collective-permute-start | bytes 3145736 | tf_op jit(solution)/shard_map/ppermute | solution.py:17
  628.8 182.6 %collective-permute-start.23 = (bf16[256,2048]{0,1:T(8,128)(2,1)}, bf16[256,2048]{0,1:T(8,128)(2,1)}, u32[]{:S(2)}, u32[]{:S(2)}) collective-permute-start(bf16[256,2048]{0,1:T(8,128)(2,1)} %get-tuple-element.933), channel_id=1, source_target_pairs={{0,3},{1,4},{2,5},{3,6},{4,7},{5,8},{6,9},{7,10},{8,11},{9,12},{10... | collective-permute-start | bytes 3145736 | tf_op jit(solution)/shard_map/ppermute | solution.py:17
  652.4 559.5 %reduce-scatter.5.cloned.1.call-start = ((), (), s32[]{:S(2)}) async-start(), calls=%async_computation.8 | async-start | bytes 12976128 | tf_op jit(solution)/shard_map/reduce_scatter | solution.py:391
  796.5 39.5 %collective-permute-start.17 = (bf16[256,2048]{0,1:T(8,128)(2,1)}, bf16[256,2048]{0,1:T(8,128)(2,1)S(1)}, u32[]{:S(2)}, u32[]{:S(2)}) collective-permute-start(bf16[256,2048]{0,1:T(8,128)(2,1)} %get-tuple-element.927), channel_id=1, source_target_pairs={{0,3},{1,4},{2,5},{3,6},{4,7},{5,8},{6,9},{7,10},{8,11},{9,12},{10... | collective-permute-start | bytes 3145736 | tf_op jit(solution)/shard_map/ppermute | solution.py:17
  806.0 52.9 %collective-permute-start.16 = (bf16[256,2048]{0,1:T(8,128)(2,1)S(1)}, bf16[256,2048]{0,1:T(8,128)(2,1)S(1)}, u32[]{:S(2)}, u32[]{:S(2)}) collective-permute-start(bf16[256,2048]{0,1:T(8,128)(2,1)S(1)} %get-tuple-element.928), channel_id=1, source_target_pairs={{0,2},{1,3},{2,4},{3,5},{4,6},{5,7},{6,8},{7,9},{8,10},{9,11},{10,... | collective-permute-start | bytes 3145736 | tf_op jit(solution)/shard_map/ppermute | solution.py:17
  808.8 55.5 %collective-permute-start.15 = (bf16[256,2048]{0,1:T(8,128)(2,1)S(1)}, bf16[256,2048]{0,1:T(8,128)(2,1)S(1)}, u32[]{:S(2)}, u32[]{:S(2)}) collective-permute-start(bf16[256,2048]{0,1:T(8,128)(2,1)S(1)} %get-tuple-element.929), channel_id=1, source_target_pairs={{0,1},{1,2},{2,3},{3,4},{4,5},{5,6},{6,7},{7,8},{8,9},{9,10},{10,1... | collective-permute-start | bytes 3145736 | tf_op jit(solution)/shard_map/ppermute | solution.py:17
  810.1 57.7 %collective-permute-start.14 = (bf16[256,2048]{0,1:T(8,128)(2,1)S(1)}, bf16[256,2048]{0,1:T(8,128)(2,1)S(1)}, u32[]{:S(2)}, u32[]{:S(2)}) collective-permute-start(bf16[256,2048]{0,1:T(8,128)(2,1)S(1)} %get-tuple-element.930), channel_id=1, source_target_pairs={{1,0},{2,1},{3,2},{4,3},{5,4},{6,5},{7,6},{8,7},{9,8},{10,9},{11,1... | collective-permute-start | bytes 3145736 | tf_op jit(solution)/shard_map/ppermute | solution.py:17
  811.5 88.1 %collective-permute-start.13 = (bf16[256,2048]{0,1:T(8,128)(2,1)S(1)}, bf16[256,2048]{0,1:T(8,128)(2,1)S(1)}, u32[]{:S(2)}, u32[]{:S(2)}) collective-permute-start(bf16[256,2048]{0,1:T(8,128)(2,1)S(1)} %get-tuple-element.931), channel_id=1, source_target_pairs={{2,0},{3,1},{4,2},{5,3},{6,4},{7,5},{8,6},{9,7},{10,8},{11,9},{12,... | collective-permute-start | bytes 3145736 | tf_op jit(solution)/shard_map/ppermute | solution.py:17
  836.0 77.6 %collective-permute-start.12 = (bf16[256,2048]{0,1:T(8,128)(2,1)S(1)}, bf16[256,2048]{0,1:T(8,128)(2,1)S(1)}, u32[]{:S(2)}, u32[]{:S(2)}) collective-permute-start(bf16[256,2048]{0,1:T(8,128)(2,1)S(1)} %get-tuple-element.926), channel_id=1, source_target_pairs={{3,0},{4,1},{5,2},{6,3},{7,4},{8,5},{9,6},{10,7},{11,8},{12,9},{13... | collective-permute-start | bytes 3145736 | tf_op jit(solution)/shard_map/ppermute | solution.py:17
  858.9 70.1 %collective-permute-start.22 = (bf16[256,2048]{0,1:T(8,128)(2,1)}, bf16[256,2048]{0,1:T(8,128)(2,1)}, u32[]{:S(2)}, u32[]{:S(2)}) collective-permute-start(bf16[256,2048]{0,1:T(8,128)(2,1)} %get-tuple-element.934), channel_id=1, source_target_pairs={{0,2},{1,3},{2,4},{3,5},{4,6},{5,7},{6,8},{7,9},{8,10},{9,11},{10,... | collective-permute-start | bytes 3145736 | tf_op jit(solution)/shard_map/ppermute | solution.py:17
  864.2 64.8 %collective-permute-start.21 = (bf16[256,2048]{0,1:T(8,128)(2,1)}, bf16[256,2048]{0,1:T(8,128)(2,1)}, u32[]{:S(2)}, u32[]{:S(2)}) collective-permute-start(bf16[256,2048]{0,1:T(8,128)(2,1)} %get-tuple-element.935), channel_id=1, source_target_pairs={{0,1},{1,2},{2,3},{3,4},{4,5},{5,6},{6,7},{7,8},{8,9},{9,10},{10,1... | collective-permute-start | bytes 3145736 | tf_op jit(solution)/shard_map/ppermute | solution.py:17
  867.9 61.1 %collective-permute-start.20 = (bf16[256,2048]{0,1:T(8,128)(2,1)}, bf16[256,2048]{0,1:T(8,128)(2,1)}, u32[]{:S(2)}, u32[]{:S(2)}) collective-permute-start(bf16[256,2048]{0,1:T(8,128)(2,1)} %get-tuple-element.936), channel_id=1, source_target_pairs={{1,0},{2,1},{3,2},{4,3},{5,4},{6,5},{7,6},{8,7},{9,8},{10,9},{11,1... | collective-permute-start | bytes 3145736 | tf_op jit(solution)/shard_map/ppermute | solution.py:17
  899.5 70.6 %collective-permute-start.19 = (bf16[256,2048]{0,1:T(8,128)(2,1)}, bf16[256,2048]{0,1:T(8,128)(2,1)}, u32[]{:S(2)}, u32[]{:S(2)}) collective-permute-start(bf16[256,2048]{0,1:T(8,128)(2,1)} %get-tuple-element.937), channel_id=1, source_target_pairs={{2,0},{3,1},{4,2},{5,3},{6,4},{7,5},{8,6},{9,7},{10,8},{11,9},{12,... | collective-permute-start | bytes 3145736 | tf_op jit(solution)/shard_map/ppermute | solution.py:17
  913.6 74.8 %collective-permute-start.18 = (bf16[256,2048]{0,1:T(8,128)(2,1)S(1)}, bf16[256,2048]{0,1:T(8,128)(2,1)}, u32[]{:S(2)}, u32[]{:S(2)}) collective-permute-start(bf16[256,2048]{0,1:T(8,128)(2,1)S(1)} %copy-done.36), channel_id=1, source_target_pairs={{3,0},{4,1},{5,2},{6,3},{7,4},{8,5},{9,6},{10,7},{11,8},{12,9},{13... | collective-permute-start | bytes 3145736 | tf_op jit(solution)/shard_map/ppermute | solution.py:17
  999.8 396.9 %reduce-scatter.9.cloned.1.call-start = ((), (), s32[]{:S(2)}) async-start(), calls=%async_computation.10 | async-start | bytes 17301504 | tf_op jit(solution)/shard_map/reduce_scatter | solution.py:398
  1015.1 569.1 %reduce-scatter.11.cloned.1.call-start = ((), (), s32[]{:S(2)}) async-start(), calls=%async_computation.11 | async-start | bytes 17301504 | tf_op jit(solution)/shard_map/reduce_scatter | solution.py:400
  (133 other events, 3347.6 us)
Sparse Core Ops, SparseCore 0:
  10.8 72.3 all-gather.5
  86.1 58.8 all-gather.7
  147.9 158.3 all-gather.9
  309.1 113.0 all-gather.11
  652.6 191.2 reduce-scatter.6
  999.9 211.9 reduce-scatter.4
  1214.8 181.8 reduce-scatter.8
  1399.6 184.5 reduce-scatter.10
where the time goes:
time: 1610 us; the launch traced here: 1590 us
  waiting for transfers between devices  656 us (41%)
  matrix products  275 us (17%)
  local copies, waits for them, and re-layouts  248 us (15%)
  blocking collectives  198 us (12%)
  starting transfers between devices  100 us (6%)
  other arithmetic  74.4 us (5%)
  loops' own time  23.3 us (1%)
    ppermute x24, waiting for transfers between devices, passed_along(): return lax.ppermute(block, axis, route)  221 us
    reduce_scatter x1, waiting for transfers between devices, body(): lax.psum_scatter(sums[11], 'seq', scatter_dimension=0, tiled=True)  187 us
    reduce_scatter x1, waiting for transfers between devices, body(): lax.psum_scatter(sums[9], 'seq', scatter_dimension=0, tiled=True)  185 us
    unnamed x2, blocking collectives  146 us
    ppermute x24, starting transfers between devices, passed_along(): return lax.ppermute(block, axis, route)  99.7 us
    unnamed x241, local copies, waits for them, and re-layouts  65.2 us
    dot_general x32, matrix products, masked_scores(): jnp.einsum('thd,shd->hts', query_part, key_part, preferred_element_type=j...  63.4 us
    all_gather x1, blocking collectives, body(): lax.all_gather(fc1_bias, 'seq', axis=0, tiled=True)  51.8 us
  transfers between devices with their start and end apart: 32, of which 13 were waited for; matrix products, arithmetic and copies ran while one was open for 26% of the time, Pallas kernels for 0%

commit v1 on v0

v1 whole, which is shorter than its diff:
```python
import functools

import jax
import jax.numpy as jnp
from jax import lax
from jax.experimental import pallas as pl
from jax.experimental.pallas import tpu as pltpu
from jax.sharding import PartitionSpec as P

HEAD_DIM = 64
IMG_TOK = 577
PLANE = 8
PAIR = 2 * HEAD_DIM
HALO = IMG_TOK - 1
LEAD = 640
WINDOW = 640
TILE = 256

epsilon = 1e-05
negative_fill = -1e30
bf16 = jnp.bfloat16
f32 = jnp.float32


def product(left, right):
    return jnp.dot(left, right, preferred_element_type=f32)


def product_tn(left, right):
    return lax.dot_general(left, right, (((0,), (0,)), ((), ())), preferred_element_type=f32)


def product_nt(left, right):
    return lax.dot_general(left, right, (((1,), (1,)), ((), ())), preferred_element_type=f32)


def swap(block, bit):
    n = lax.axis_size("seq")
    return lax.ppermute(block, "seq", [(i, i ^ bit) for i in range(n)])


def shift_plane(block, planes):
    n = lax.axis_size("seq")
    step = planes * PLANE
    return lax.ppermute(block, "seq", [(i, i + step) for i in range(n) if 0 <= i + step < n])


def places(order):
    held = [0]
    for bit in order:
        held = held + [r ^ bit for r in held]
    return held


def gather_bits(block, order):
    current = block[None]
    for bit in order[:-1]:
        current = jnp.concatenate([current, swap(current, bit)], axis=0)
    return current, swap(current, order[-1])


def collect_kernel(parts, info, spots, *refs):
    whole = refs[2 * parts]
    side = jnp.bitwise_and(info[0], 1)
    for k in range(parts):
        whole[0, side, k] = refs[2 * k][0]
        whole[0, 1 - side, k] = refs[2 * k + 1][0]


def spread_kernel(parts, info, spots, *refs):
    whole = refs[0]
    side = jnp.bitwise_and(info[0], 1)
    for k in range(parts):
        refs[1 + 2 * k][0] = whole[0, side, k]
        refs[2 + 2 * k][0] = whole[0, 1 - side, k]


def block_specs(parts, half, part_rows, columns):
    piece = [
        pl.BlockSpec((1, part_rows, columns), lambda s, info, spots, k=k: (spots[k, s], 0, 0))
        for k in range(parts)
        for _ in range(2)
    ]
    whole = pl.BlockSpec(
        (1, 2, parts, part_rows, columns),
        lambda s, info, spots: (jnp.bitwise_xor(info[0] >> 1, s), 0, 0, 0, 0),
    )
    return piece, whole


def spot_table(orders, half):
    table = []
    for order in orders:
        held = places(order)
        table.append([held.index(2 * s) for s in range(half)])
    return jnp.asarray(table, jnp.int32)


def gathered_weight(info, shard, orders):
    rows, columns = shard.shape
    n = lax.axis_size("seq")
    half = n // 2
    parts = len(orders)
    part_rows = rows // parts
    ins = []
    for k, order in enumerate(orders):
        ins += gather_bits(shard[k * part_rows : (k + 1) * part_rows], order)
    piece, whole = block_specs(parts, half, part_rows, columns)
    joined = pl.pallas_call(
        functools.partial(collect_kernel, parts),
        grid_spec=pltpu.PrefetchScalarGridSpec(
            num_scalar_prefetch=2, grid=(half,), in_specs=piece, out_specs=whole
        ),
        out_shape=jax.ShapeDtypeStruct((half, 2, parts, part_rows, columns), shard.dtype),
    )(info, spot_table([order[:-1] for order in orders], half), *ins)
    return joined.reshape(n * rows, columns)


def scattered_sum(info, partial, orders):
    n = lax.axis_size("seq")
    total_rows, columns = partial.shape
    rows = total_rows // n
    parts = len(orders)
    part_rows = rows // parts
    half = n // 2
    piece, whole = block_specs(parts, half, part_rows, columns)
    placed = pl.pallas_call(
        functools.partial(spread_kernel, parts),
        grid_spec=pltpu.PrefetchScalarGridSpec(
            num_scalar_prefetch=2, grid=(half,), in_specs=[whole], out_specs=piece
        ),
        out_shape=[jax.ShapeDtypeStruct((half, part_rows, columns), partial.dtype)] * (2 * parts),
    )(
        info,
        spot_table([order[1:][::-1] for order in orders], half),
        partial.reshape(half, 2, parts, part_rows, columns),
    )
    sums = []
    for k, order in enumerate(orders):
        keep, send = placed[2 * k], placed[2 * k + 1]
        size = half
        for bit in order:
            got = swap(send, bit)
            if size == 1:
                sums.append(keep[0].astype(f32) + got[0].astype(f32))
                break
            size //= 2
            send = (keep[size:].astype(f32) + got[size:].astype(f32)).astype(bf16)
            keep = (keep[:size].astype(f32) + got[:size].astype(f32)).astype(bf16)
    return jnp.concatenate(sums, axis=0) if len(sums) > 1 else sums[0]


def turn_kernel(info, blocks, turned):
    for r in range(blocks.shape[0]):
        turned[r] = blocks[jnp.bitwise_xor(info[0], r)]


def turn_blocks(info, blocks):
    return pl.pallas_call(
        turn_kernel,
        grid_spec=pltpu.PrefetchScalarGridSpec(
            num_scalar_prefetch=1,
            grid=(1,),
            in_specs=[pl.BlockSpec(blocks.shape, lambda g, i: (0, 0, 0))],
            out_specs=pl.BlockSpec(blocks.shape, lambda g, i: (0, 0, 0)),
        ),
        out_shape=jax.ShapeDtypeStruct(blocks.shape, blocks.dtype),
    )(info, blocks)


def load_rows(place_in_plane, qkv, before, after, queries, keys, values, sem):
    micro_count, blocks = qkv.shape[0], qkv.shape[1]
    rows = qkv.shape[2]
    own = blocks * rows
    for buffer in (keys, values):
        for m in range(micro_count):
            buffer[m, 0 : LEAD - HALO, :] = jnp.zeros((LEAD - HALO, PAIR), bf16)
            tail = buffer.shape[1] - (LEAD + own + HALO)
            buffer[m, LEAD + own + HALO :, :] = jnp.zeros((tail, PAIR), bf16)
    started = []
    for m in range(micro_count):
        for r in range(blocks):
            spot = pl.multiple_of(jnp.bitwise_xor(place_in_plane, r) * rows, rows)
            started += [
                pltpu.make_async_copy(
                    qkv.at[m, r, :, pl.ds(0, PAIR)], queries.at[m, pl.ds(spot, rows)], sem
                ),
                pltpu.make_async_copy(
                    qkv.at[m, r, :, pl.ds(PAIR, PAIR)], keys.at[m, pl.ds(LEAD + spot, rows)], sem
                ),
                pltpu.make_async_copy(
                    qkv.at[m, r, :, pl.ds(2 * PAIR, PAIR)], values.at[m, pl.ds(LEAD + spot, rows)], sem
                ),
            ]
        for which, buffer in enumerate((keys, values)):
            columns = pl.ds(which * PAIR, PAIR)
            started += [
                pltpu.make_async_copy(
                    before.at[m, :, columns], buffer.at[m, pl.ds(LEAD - HALO, HALO)], sem
                ),
                pltpu.make_async_copy(
                    after.at[m, :, columns], buffer.at[m, pl.ds(LEAD + own, HALO)], sem
                ),
            ]
    return started


def image_span(bounds, m, image, base):
    begin = bounds[m, image] - base + LEAD
    finish = bounds[m, image + 1] - base + LEAD
    return begin, finish


def key_block(keys, m, begin, finish, key_start, key_aug):
    key_aug[:, :PAIR] = keys[m, pl.ds(key_start, WINDOW), :]
    rows = key_start + lax.broadcasted_iota(jnp.int32, (WINDOW, PAIR), 0)
    inside = (rows >= begin) & (rows < finish)
    key_aug[:, PAIR:] = jnp.where(inside, 0.0, negative_fill).astype(bf16)


def split_heads(rows_f32, lanes):
    first = jnp.where(lanes < HEAD_DIM, rows_f32, 0.0).astype(bf16)
    second = jnp.where(lanes >= HEAD_DIM, rows_f32, 0.0).astype(bf16)
    return first, second


def attend_kernel(
    info, bounds, qkv, before, after, mixed, stats, queries, keys, values, result, result_low, key_aug, value_t, sem
):
    micro_count, blocks, rows, _ = qkv.shape
    own = blocks * rows
    place_in_plane, base = info[1], info[2]
    image_count = bounds.shape[1] - 1
    started = load_rows(place_in_plane, qkv, before, after, queries, keys, values, sem)
    for copy in started:
        copy.start()
    value_t[:, HEAD_DIM:, :] = jnp.ones((2, 16, WINDOW), bf16)
    lanes = lax.broadcasted_iota(jnp.int32, (TILE, PAIR), 1)
    rows_iota = lax.broadcasted_iota(jnp.int32, (TILE, PAIR), 0)
    lane_row = lax.broadcasted_iota(jnp.int32, (1, TILE), 1)
    query_mark = jnp.where(lanes == 0, 1.0, 0.0).astype(bf16)
    for copy in started:
        copy.wait()

    for m in range(micro_count):

        def one_image(image, carry):
            begin, finish = image_span(bounds, m, image, base)

            @pl.when((finish > LEAD) & (begin < LEAD + own))
            def _():
                key_start = pl.multiple_of((begin >> 4) << 4, 16)
                key_block(keys, m, begin, finish, key_start, key_aug)
                turned = values[m, pl.ds(key_start, WINDOW), :].astype(f32).T
                value_t[0, :HEAD_DIM, :] = turned[:HEAD_DIM].astype(bf16)
                value_t[1, :HEAD_DIM, :] = turned[HEAD_DIM:].astype(bf16)
                first_tile = jnp.maximum(begin - LEAD, 0) >> 8
                last_tile = (jnp.minimum(finish - LEAD, own) + TILE - 1) >> 8

                def one_tile(tile, carry):
                    spot = pl.multiple_of(tile * TILE, TILE)
                    scaled = queries[m, pl.ds(spot, TILE), :].astype(f32) * (HEAD_DIM**-0.5)
                    pieces = []
                    inside_lane = (lane_row + (spot + LEAD) >= begin) & (lane_row + (spot + LEAD) < finish)
                    for h, query in enumerate(split_heads(scaled, lanes)):
                        aug = jnp.concatenate([query, query_mark], axis=1)
                        scores = product_nt(key_aug[...], aug)
                        peak = jnp.max(scores, axis=0, keepdims=True)
                        weights = jnp.exp(scores - peak).astype(bf16)
                        out = product(value_t[h], weights)
                        total = out[HEAD_DIM : HEAD_DIM + 1]
                        pieces.append(out[:HEAD_DIM] / total)
                        row = (m * 2 + h) * blocks + tile
                        stats[pl.ds(row, 1), :] = jnp.where(
                            inside_lane, peak + jnp.log(total), stats[pl.ds(row, 1), :]
                        )
                    value = jnp.concatenate(pieces, axis=0).T
                    place_row = rows_iota + (spot + LEAD)
                    inside = (place_row >= begin) & (place_row < finish)
                    result[m, pl.ds(spot, TILE), :] = jnp.where(
                        inside, value, result[m, pl.ds(spot, TILE), :]
                    )
                    return carry

                lax.fori_loop(first_tile, last_tile, one_tile, 0)

            return carry

        lax.fori_loop(0, image_count, one_image, 0)

    result_low[...] = result[...].astype(bf16)
    started = []
    for m in range(micro_count):
        for r in range(blocks):
            spot = pl.multiple_of(jnp.bitwise_xor(place_in_plane, r) * rows, rows)
            started.append(pltpu.make_async_copy(result_low.at[m, pl.ds(spot, rows)], mixed.at[r, m], sem))
    for copy in started:
        copy.start()
    for copy in started:
        copy.wait()


def attend_back_kernel(
    info,
    bounds,
    qkv,
    before,
    after,
    mixed,
    grad_mixed,
    stats,
    grad_query,
    grad_pairs,
    grad_before,
    grad_after,
    queries,
    keys,
    values,
    result,
    grads,
    key_aug,
    key_t,
    acc_query,
    acc_key,
    acc_value,
    edge,
    sem,
):
    micro_count, blocks, rows, _ = qkv.shape
    own = blocks * rows
    place_in_plane, base = info[1], info[2]
    image_count = bounds.shape[1] - 1
    started = load_rows(place_in_plane, qkv, before, after, queries, keys, values, sem)
    for m in range(micro_count):
        for r in range(blocks):
            spot = pl.multiple_of(jnp.bitwise_xor(place_in_plane, r) * rows, rows)
            started += [
                pltpu.make_async_copy(mixed.at[r, m], result.at[m, pl.ds(spot, rows)], sem),
                pltpu.make_async_copy(grad_mixed.at[r, m], grads.at[m, pl.ds(spot, rows)], sem),
            ]
    for copy in started:
        copy.start()
    acc_query[...] = jnp.zeros_like(acc_query)
    acc_key[...] = jnp.zeros_like(acc_key)
    acc_value[...] = jnp.zeros_like(acc_value)
    lanes = lax.broadcasted_iota(jnp.int32, (TILE, PAIR), 1)
    lane_row = lax.broadcasted_iota(jnp.int32, (1, TILE), 1)
    query_mark = jnp.where(lanes == 0, 1.0, 0.0).astype(bf16)
    for copy in started:
        copy.wait()

    for m in range(micro_count):

        def one_image(image, carry):
            begin, finish = image_span(bounds, m, image, base)

            @pl.when((finish > LEAD) & (begin < LEAD + own))
            def _():
                key_start = pl.multiple_of((begin >> 4) << 4, 16)
                key_rows = pl.ds(key_start, WINDOW)
                key_block(keys, m, begin, finish, key_start, key_aug)
                turned = keys[m, key_rows, :].astype(f32).T
                key_t[0] = turned[:HEAD_DIM].astype(bf16)
                key_t[1] = turned[HEAD_DIM:].astype(bf16)
                first_tile = jnp.maximum(begin - LEAD, 0) >> 8
                last_tile = (jnp.minimum(finish - LEAD, own) + TILE - 1) >> 8

                def one_tile(tile, carry):
                    spot = pl.multiple_of(tile * TILE, TILE)
                    here = pl.ds(spot, TILE)
                    scaled = queries[m, here, :].astype(f32) * (HEAD_DIM**-0.5)
                    grad = grads[m, here, :].astype(f32)
                    dots = (grad * result[m, here, :].astype(f32)).T
                    inside_lane = (lane_row + (spot + LEAD) >= begin) & (lane_row + (spot + LEAD) < finish)
                    both = zip(split_heads(scaled, lanes), split_heads(grad, lanes))
                    pieces = []
                    add_key, add_value = None, None
                    for h, (query, grad_h) in enumerate(both):
                        row = (m * 2 + h) * blocks + tile
                        level = jnp.where(inside_lane, stats[pl.ds(row, 1), :], -negative_fill)
                        row_dot = jnp.sum(
                            dots[h * HEAD_DIM : (h + 1) * HEAD_DIM], axis=0, keepdims=True
                        )
                        aug = jnp.concatenate([query, query_mark], axis=1)
                        shares = jnp.exp(product_nt(key_aug[...], aug) - level)
                        grad_share = product_nt(values[m, key_rows, :], grad_h)
                        grad_scores = (shares * (grad_share - row_dot)).astype(bf16)
                        value_part = product(shares.astype(bf16), grad_h)
                        key_part = product(grad_scores, query)
                        add_value = value_part if h == 0 else add_value + value_part
                        add_key = key_part if h == 0 else add_key + key_part
                        pieces.append(product(key_t[h], grad_scores))
                    acc_value[m, key_rows, :] += add_value
                    acc_key[m, key_rows, :] += add_key
                    acc_query[m, here, :] += jnp.concatenate(pieces, axis=0).T * (HEAD_DIM**-0.5)
                    return carry

                lax.fori_loop(first_tile, last_tile, one_tile, 0)

            return carry

        lax.fori_loop(0, image_count, one_image, 0)

    started = []
    for m in range(micro_count):
        started.append(pltpu.make_async_copy(acc_query.at[m], grad_query.at[m], sem))
        for which, acc in enumerate((acc_key, acc_value)):
            columns = pl.ds(which * PAIR, PAIR)
            edge[0, m, :, which * PAIR : (which + 1) * PAIR] = acc[m, LEAD - HALO : LEAD, :].astype(bf16)
            edge[1, m, :, which * PAIR : (which + 1) * PAIR] = acc[
                m, LEAD + own : LEAD + own + HALO, :
            ].astype(bf16)
            started.append(
                pltpu.make_async_copy(acc.at[m, pl.ds(LEAD, own)], grad_pairs.at[m, :, columns], sem)
            )
        started.append(pltpu.make_async_copy(edge.at[0, m], grad_before.at[m], sem))
        started.append(pltpu.make_async_copy(edge.at[1, m], grad_after.at[m], sem))
    for copy in started:
        copy.start()
    for copy in started:
        copy.wait()


def any_specs(count):
    return [pl.BlockSpec(memory_space=pl.ANY)] * count


def attend(info, bounds, qkv, before, after):
    micro_count, blocks, rows, _ = qkv.shape
    own = blocks * rows
    span = LEAD + own + LEAD
    stat_rows = micro_count * 2 * blocks
    return pl.pallas_call(
        attend_kernel,
        grid_spec=pltpu.PrefetchScalarGridSpec(
            num_scalar_prefetch=2,
            grid=(1,),
            in_specs=any_specs(3),
            out_specs=any_specs(1) + [pl.BlockSpec((stat_rows, TILE), lambda g, a, b: (0, 0))],
            scratch_shapes=[
                pltpu.VMEM((micro_count, own, PAIR), bf16),
                pltpu.VMEM((micro_count, span, PAIR), bf16),
                pltpu.VMEM((micro_count, span, PAIR), bf16),
                pltpu.VMEM((micro_count, own, PAIR), f32),
                pltpu.VMEM((micro_count, own, PAIR), bf16),
                pltpu.VMEM((WINDOW, 2 * PAIR), bf16),
                pltpu.VMEM((2, HEAD_DIM + 16, WINDOW), bf16),
                pltpu.SemaphoreType.DMA,
            ],
        ),
        out_shape=[
            jax.ShapeDtypeStruct((blocks, micro_count, rows, PAIR), bf16),
            jax.ShapeDtypeStruct((stat_rows, TILE), f32),
        ],
    )(info, bounds, qkv, before, after)


def attend_back(info, bounds, qkv, before, after, mixed, grad_mixed, stats):
    micro_count, blocks, rows, _ = qkv.shape
    own = blocks * rows
    span = LEAD + own + LEAD
    stat_rows = micro_count * 2 * blocks
    return pl.pallas_call(
        attend_back_kernel,
        grid_spec=pltpu.PrefetchScalarGridSpec(
            num_scalar_prefetch=2,
            grid=(1,),
            in_specs=any_specs(5) + [pl.BlockSpec((stat_rows, TILE), lambda g, a, b: (0, 0))],
            out_specs=any_specs(4),
            scratch_shapes=[
                pltpu.VMEM((micro_count, own, PAIR), bf16),
                pltpu.VMEM((micro_count, span, PAIR), bf16),
                pltpu.VMEM((micro_count, span, PAIR), bf16),
                pltpu.VMEM((micro_count, own, PAIR), bf16),
                pltpu.VMEM((micro_count, own, PAIR), bf16),
                pltpu.VMEM((WINDOW, 2 * PAIR), bf16),
                pltpu.VMEM((2, HEAD_DIM, WINDOW), bf16),
                pltpu.VMEM((micro_count, own, PAIR), f32),
                pltpu.VMEM((micro_count, span, PAIR), f32),
                pltpu.VMEM((micro_count, span, PAIR), f32),
                pltpu.VMEM((2, micro_count, HALO, 2 * PAIR), bf16),
                pltpu.SemaphoreType.DMA,
            ],
        ),
        out_shape=[
            jax.ShapeDtypeStruct((micro_count, own, PAIR), f32),
            jax.ShapeDtypeStruct((micro_count, own, 2 * PAIR), f32),
            jax.ShapeDtypeStruct((micro_count, HALO, 2 * PAIR), bf16),
            jax.ShapeDtypeStruct((micro_count, HALO, 2 * PAIR), bf16),
        ],
    )(info, bounds, qkv, before, after, mixed, grad_mixed, stats)


def join_kernel(first_blocks, last_blocks, blocks, info, query, pairs, head, tail, joined):
    tile = pl.program_id(1)
    total = pairs[0]
    total = total + jnp.where(tile < first_blocks, head[0].astype(f32), 0.0)
    total = total + jnp.where(tile >= blocks - last_blocks, tail[0].astype(f32), 0.0)
    joined[0, 0, :, :PAIR] = query[0].astype(bf16)
    joined[0, 0, :, PAIR:] = total.astype(bf16)


def join_grads(info, grad_query, grad_pairs, head, tail, rows):
    micro_count, own, _ = grad_query.shape
    blocks = own // rows
    edge_blocks = -(-HALO // rows)
    spare = edge_blocks * rows - HALO
    head = jnp.pad(head, ((0, 0), (0, spare), (0, 0)))
    tail = jnp.pad(tail, ((0, 0), (spare, 0), (0, 0)))
    return pl.pallas_call(
        functools.partial(join_kernel, edge_blocks, edge_blocks, blocks),
        grid_spec=pltpu.PrefetchScalarGridSpec(
            num_scalar_prefetch=1,
            grid=(micro_count, blocks),
            in_specs=[
                pl.BlockSpec((1, rows, PAIR), lambda m, t, i: (m, t, 0)),
                pl.BlockSpec((1, rows, 2 * PAIR), lambda m, t, i: (m, t, 0)),
                pl.BlockSpec((1, rows, 2 * PAIR), lambda m, t, i: (m, jnp.minimum(t, edge_blocks - 1), 0)),
                pl.BlockSpec(
                    (1, rows, 2 * PAIR),
                    lambda m, t, i: (m, jnp.maximum(t - (blocks - edge_blocks), 0), 0),
                ),
            ],
            out_specs=pl.BlockSpec(
                (1, 1, rows, 3 * PAIR), lambda m, t, i: (m, jnp.bitwise_xor(t, i[1]), 0, 0)
            ),
        ),
        out_shape=jax.ShapeDtypeStruct((micro_count, blocks, rows, 3 * PAIR), bf16),
    )(info, grad_query, grad_pairs, head, tail)


def layer_norm_parts(values, gain, shift):
    center = values - jnp.mean(values, axis=-1, keepdims=True)
    inverse = lax.rsqrt(jnp.mean(center * center, axis=-1, keepdims=True) + epsilon)
    normal = center * inverse
    return (normal * gain + shift, normal, inverse)


def layer_norm_back(grad_normed, normal, inverse, gain):
    scaled = grad_normed * gain
    centered = scaled - jnp.mean(scaled, axis=-1, keepdims=True)
    return inverse * (centered - normal * jnp.mean(scaled * normal, axis=-1, keepdims=True))


def plane_tokens(block, order):
    near, far = gather_bits(block, order)
    held = places(order)
    half = PLANE // 2
    at = {r: (near[p] if p < half else far[p - half]) for p, r in enumerate(held)}
    return jnp.stack([at[r] for r in range(PLANE)])


def plane_scatter(partial, order):
    pieces = {r: partial[r].astype(bf16) for r in range(PLANE)}
    left = list(range(PLANE))
    total = None
    for step, bit in enumerate(order):
        keep = [r for r in left if not r & bit]
        got = swap(jnp.stack([pieces[r | bit] for r in keep]), bit)
        last = step == len(order) - 1
        for position, r in enumerate(keep):
            added = pieces[r].astype(f32) + got[position].astype(f32)
            pieces[r] = added if last else added.astype(bf16)
        left = keep
    return pieces[0]


def body(
    tokens,
    ln1_gain,
    ln1_bias,
    qkv_weight,
    q_bias,
    v_bias,
    out_weight,
    out_bias,
    ln2_gain,
    ln2_bias,
    fc1_weight,
    fc1_bias,
    fc2_weight,
    fc2_bias,
    image_ids,
    image_starts,
    cotangent,
):
    micro_count, tok_dev, model_width = tokens.shape
    n = lax.axis_size("seq")
    own_tokens = micro_count * tok_dev
    plane_rows = PLANE * tok_dev
    stream_len = tok_dev * n
    me = lax.axis_index("seq")
    mine = jnp.bitwise_and(me, PLANE - 1)
    base = (me - mine) * tok_dev
    info = jnp.stack([me, mine, base]).astype(jnp.int32)
    bounds = jnp.concatenate(
        [image_starts, jnp.full((micro_count, 1), stream_len, jnp.int32)], axis=1
    )
    plane_bits = [1, 2, 4]
    depth_bits = []
    bit = PLANE
    while bit < n:
        depth_bits.append(bit)
        bit *= 2
    order_a = depth_bits + [2, 4, 1]
    order_b = depth_bits + [4, 2, 1]

    small = [ln1_gain, ln1_bias, q_bias, v_bias, out_bias, ln2_gain, ln2_bias, fc2_bias, fc1_bias]
    shard_rows = qkv_weight.shape[0]
    small_len = sum(item.shape[0] for item in small)
    spare_rows = -(-small_len // (8 * 3 * PAIR)) * 8
    small_rows = jnp.pad(jnp.concatenate(small), (0, spare_rows * 3 * PAIR - small_len))
    small_rows = small_rows.reshape(spare_rows, 3 * PAIR)
    by_pair = qkv_weight.reshape(shard_rows, 3, PLANE, PAIR).transpose(2, 0, 1, 3)
    by_pair = by_pair.reshape(PLANE, shard_rows, 3 * PAIR)
    outgoing = jnp.concatenate(
        [by_pair, jnp.broadcast_to(small_rows[None], (PLANE,) + small_rows.shape)], axis=1
    )
    arrived = [lax.dynamic_index_in_dim(outgoing, mine, 0, keepdims=False)]
    for r in range(1, PLANE):
        arrived.append(
            swap(lax.dynamic_index_in_dim(outgoing, jnp.bitwise_xor(mine, r), 0, keepdims=False), r)
        )
    current = jnp.stack(arrived)
    for bit in depth_bits:
        current = jnp.concatenate([current, swap(current, bit)], axis=0)
    pair_blocks = turn_blocks(info, current)
    pair_weight = pair_blocks[:, :shard_rows].reshape(n * shard_rows, 3 * PAIR)
    small_all = pair_blocks[:, shard_rows:].reshape(n, -1).astype(f32)
    small_full = []
    offset = 0
    for item in small:
        width = item.shape[0]
        small_full.append(small_all[:, offset : offset + width].reshape(n * width))
        offset += width
    gain_one, shift_one, q_shift, v_shift, out_shift, gain_two, shift_two, down_shift, up_shift = small_full

    plane_stream = jnp.stack(
        [
            plane_tokens(tokens[m], [2, 4, 1] if m % 2 == 0 else [4, 2, 1])
            for m in range(micro_count)
        ]
    )
    plane_flat = plane_stream.reshape(micro_count * plane_rows, model_width)
    normed, _, _ = layer_norm_parts(plane_flat.astype(f32), gain_one, shift_one)
    normed_low = normed.astype(bf16)
    pair_shift = jnp.concatenate(
        [
            lax.dynamic_slice_in_dim(q_shift, mine * PAIR, PAIR),
            jnp.zeros((PAIR,), f32),
            lax.dynamic_slice_in_dim(v_shift, mine * PAIR, PAIR),
        ]
    )
    qkv = (product(normed_low, pair_weight) + pair_shift).astype(bf16)
    qkv = qkv.reshape(micro_count, PLANE, tok_dev, 3 * PAIR)

    edge_blocks = -(-HALO // tok_dev)

    def plane_block(index):
        return lax.dynamic_index_in_dim(qkv, jnp.bitwise_xor(mine, index), 1, keepdims=False)[:, :, PAIR:]

    last_rows = jnp.concatenate([plane_block(PLANE - edge_blocks + k) for k in range(edge_blocks)], axis=1)
    first_rows = jnp.concatenate([plane_block(k) for k in range(edge_blocks)], axis=1)
    before = shift_plane(last_rows[:, edge_blocks * tok_dev - HALO :], 1)
    after = shift_plane(first_rows[:, :HALO], -1)
    mixed_pair, stats = attend(info, bounds, qkv, before, after)

    def column(r):
        return jnp.bitwise_xor(mine, r) * PAIR

    mixed_low = jnp.zeros((own_tokens, model_width), bf16)
    for r in range(PLANE):
        part = mixed_pair[r] if r == 0 else swap(mixed_pair[r], r)
        mixed_low = lax.dynamic_update_slice(mixed_low, part.reshape(own_tokens, PAIR), (0, column(r)))

    out_full = gathered_weight(info, out_weight, [order_a])
    up_full = gathered_weight(info, fc1_weight, [order_a, order_b])
    down_full = gathered_weight(info, fc2_weight, [order_a, order_b])

    stream = tokens.reshape(own_tokens, model_width).astype(f32)
    cotangent_low = cotangent.reshape(own_tokens, model_width)
    middle = stream + product(mixed_low, out_full) + out_shift
    normed_two, normal_two, inverse_two = layer_norm_parts(middle, gain_two, shift_two)
    normed_two_low = normed_two.astype(bf16)
    hidden = product(normed_two_low, up_full) + up_shift
    gate = jax.nn.sigmoid(1.702 * hidden)
    active_low = (hidden * gate).astype(bf16)
    result = middle + product(active_low, down_full) + down_shift

    grad_active = product_nt(cotangent_low, down_full)
    grad_hidden_low = (grad_active * (gate + 1.702 * hidden * gate * (1.0 - gate))).astype(bf16)
    grad_normed_two = product_nt(grad_hidden_low, up_full)
    grad_middle = cotangent_low.astype(f32) + layer_norm_back(
        grad_normed_two, normal_two, inverse_two, gain_two
    )
    grad_branch_low = grad_middle.astype(bf16)
    grad_mixed_low = product_nt(grad_branch_low, out_full).astype(bf16)

    back_order_a = [1, 2, 4] + depth_bits[::-1]
    back_order_b = [1, 4, 2] + depth_bits[::-1]
    grad_parts = []
    for r in range(PLANE):
        part = lax.dynamic_slice(grad_mixed_low, (0, column(r)), (own_tokens, PAIR))
        part = part.reshape(micro_count, tok_dev, PAIR)
        grad_parts.append(part if r == 0 else swap(part, r))
    grad_mixed_pair = jnp.stack(grad_parts)

    grad_down = product_tn(active_low, cotangent_low).astype(bf16)
    down_sum = scattered_sum(info, grad_down, [back_order_a, back_order_b])
    grad_up = product_tn(normed_two_low, grad_hidden_low).astype(bf16)
    up_sum = scattered_sum(info, grad_up, [back_order_a, back_order_b])
    grad_out_weight = product_tn(mixed_low, grad_branch_low).astype(bf16)
    out_sum = scattered_sum(info, grad_out_weight, [back_order_a])

    grad_query, grad_pairs, grad_before, grad_after = attend_back(
        info, bounds, qkv, before, after, mixed_pair, grad_mixed_pair, stats
    )
    from_next = shift_plane(grad_before, -1)
    from_last = shift_plane(grad_after, 1)
    grad_joined = join_grads(info, grad_query, grad_pairs, from_last, from_next, tok_dev)
    grad_flat = grad_joined.reshape(micro_count * plane_rows, 3 * PAIR)

    grad_plane = product_nt(grad_flat, pair_weight).reshape(micro_count, PLANE, tok_dev, model_width)
    grad_normed = jnp.stack(
        [
            plane_scatter(grad_plane[m], [1, 2, 4] if m % 2 == 0 else [1, 4, 2])
            for m in range(micro_count)
        ]
    ).reshape(own_tokens, model_width)
    _, normal_one, inverse_one = layer_norm_parts(stream, gain_one, shift_one)
    grad_stream = grad_middle + layer_norm_back(grad_normed, normal_one, inverse_one, gain_one)

    grad_pair_weight = product_tn(normed_low, grad_flat)
    column_sum = jnp.sum(grad_flat.astype(f32), axis=0)
    wide = pair_weight.astype(f32)
    grad_shift_one = jnp.sum(wide * column_sum, axis=1)
    grad_gain_one = jnp.sum(wide * grad_pair_weight, axis=1)
    grad_gain_one = (grad_gain_one - shift_one * grad_shift_one) / gain_one

    def at_columns(part):
        return lax.dynamic_update_slice(jnp.zeros((model_width,), f32), part, (mine * PAIR,))

    small_grads = [
        grad_gain_one,
        grad_shift_one,
        at_columns(column_sum[:PAIR]),
        at_columns(column_sum[2 * PAIR :]),
        jnp.sum(grad_branch_low.astype(f32), axis=0),
        jnp.sum(grad_normed_two * normal_two, axis=0),
        jnp.sum(grad_normed_two, axis=0),
        jnp.sum(cotangent_low.astype(f32), axis=0),
        jnp.sum(grad_hidden_low.astype(f32), axis=0),
    ]
    small_out = jnp.concatenate([item.reshape(n, -1) for item in small_grads], axis=1).astype(bf16)
    small_out = jnp.pad(small_out, ((0, 0), (0, spare_rows * 3 * PAIR - small_len)))
    small_out = small_out.reshape(n, spare_rows, 3 * PAIR)
    leaving = jnp.concatenate(
        [grad_pair_weight.astype(bf16).reshape(n, shard_rows, 3 * PAIR), small_out], axis=1
    )
    turned = turn_blocks(info, leaving)
    size = n
    for bit in depth_bits[::-1]:
        size //= 2
        got = swap(turned[size:], bit)
        turned = (turned[:size].astype(f32) + got.astype(f32)).astype(bf16)
    qkv_sum = jnp.zeros((shard_rows, 3, model_width), f32)
    small_sum = jnp.zeros((spare_rows, 3 * PAIR), f32)
    for r in range(PLANE):
        part = turned[r] if r == 0 else swap(turned[r], r)
        columns = part[:shard_rows].reshape(shard_rows, 3, PAIR).astype(f32)
        qkv_sum = lax.dynamic_update_slice(qkv_sum, columns, (0, 0, column(r)))
        small_sum = small_sum + part[shard_rows:].astype(f32)
    qkv_sum = qkv_sum.reshape(shard_rows, 3 * model_width)
    small_sum = small_sum.reshape(-1)
    sums = []
    offset = 0
    for item in small:
        sums.append(small_sum[offset : offset + item.shape[0]])
        offset += item.shape[0]

    return (
        result.astype(bf16).reshape(micro_count, tok_dev, model_width),
        grad_stream.astype(bf16).reshape(micro_count, tok_dev, model_width),
        sums[0],
        sums[1],
        qkv_sum,
        sums[2],
        sums[3],
        out_sum,
        sums[4],
        sums[5],
        sums[6],
        up_sum,
        sums[8],
        down_sum,
        sums[7],
    )


def solution(mesh):
    return jax.shard_map(
        body,
        mesh=mesh,
        in_specs=(
            P(None, "seq", None),
            P("seq"),
            P("seq"),
            P("seq", None),
            P("seq"),
            P("seq"),
            P("seq", None),
            P("seq"),
            P("seq"),
            P("seq"),
            P("seq", None),
            P("seq"),
            P("seq", None),
            P("seq"),
            P(None, "seq"),
            P(),
            P(None, "seq", None),
        ),
        out_specs=(
            P(None, "seq", None),
            P(None, "seq", None),
            P("seq"),
            P("seq"),
            P("seq", None),
            P("seq"),
            P("seq"),
            P("seq", None),
            P("seq"),
            P("seq"),
            P("seq"),
            P("seq", None),
            P("seq"),
            P("seq", None),
            P("seq"),
        ),
        check_vma=False,
    )
```

time: 1610 us -> 821 us (0.51)
  waiting for transfers between devices: 656 us -> 334 us
  blocking collectives: 198 us -> 0 us
  matrix products: 275 us -> 82.1 us
  local copies, waits for them, and re-layouts: 248 us -> 86.4 us
  Pallas kernels: 0 us -> 156 us
  loops' own time: 23.3 us -> 0 us
    reduce_scatter x4 -> x0, waiting for transfers between devices: 413 us -> none  [the longest x1 187 us: body(): lax.psum_scatter(sums[11], 'seq', scatter_dimension=0, tiled=True)]
    dot_general x120 -> x4, matrix products: 189 us -> 25.3 us  [product(): return jnp.dot(left, right, preferred_element_type=f32)]
    pallas_call x0 -> x11, Pallas kernels: none -> 156 us  [the longest x3 35.2 us: scattered_sum(): pl.pallas_call(functools.partial(spread_kernel, parts), grid_spec=pltpu.P...]
    unnamed x2 -> x0, blocking collectives: 146 us -> none
    ppermute x24 -> x98, waiting for transfers between devices: 221 us -> 334 us  [the longest x94 311 us: swap(): return lax.ppermute(block, 'seq', [(i, i ^ bit) for i in range(n)])]
    dynamic_slice x128 -> x3, local copies, waits for them, and re-layouts: 100 us -> 1.86 us  [the longest x1 0.81 us: body(): lax.dynamic_slice_in_dim(v_shift, mine * PAIR, PAIR)]
    all_gather x1 -> x0, blocking collectives: 51.8 us -> none  [body(): lax.all_gather(fc1_bias, 'seq', axis=0, tiled=True)]
    dynamic_update_slice x64 -> x18, local copies, waits for them, and re-layouts: 32.3 us -> 1.76 us  [the longest x8 1.21 us: body(): lax.dynamic_update_slice(mixed_low, part.reshape(own_tokens, PAIR), (0, c...]
  transfers between devices with their start and end apart: 32 -> 98, of which waited for: 13 -> 45; matrix products, arithmetic and copies ran while one was open for 26% -> 22% of each run, Pallas kernels for 0% -> 15%
where the time goes in v1:
time: 821 us; the launch traced here: 810 us
  waiting for transfers between devices  334 us (41%)
  Pallas kernels  156 us (19%)
  local copies, waits for them, and re-layouts  86.4 us (11%)
  starting transfers between devices  86.3 us (11%)
  matrix products  82.1 us (10%)
  other arithmetic  62.5 us (8%)
    ppermute x94, waiting for transfers between devices, swap(): return lax.ppermute(block, 'seq', [(i, i ^ bit) for i in range(n)])  311 us
    ppermute x94, starting transfers between devices, swap(): return lax.ppermute(block, 'seq', [(i, i ^ bit) for i in range(n)])  71.7 us
    unnamed x212, local copies, waits for them, and re-layouts  41.2 us
    pallas_call x3, Pallas kernels, scattered_sum(): pl.pallas_call(functools.partial(spread_kernel, parts), grid_spec=pltpu.P...  35.2 us
    pallas_call x3, Pallas kernels, gathered_weight(): pl.pallas_call(functools.partial(collect_kernel, parts), grid_spec=pltpu....  35 us
    pallas_call x1, Pallas kernels, attend_back(): pl.pallas_call(attend_back_kernel, grid_spec=pltpu.PrefetchScalarGridSpec...  34.6 us
    pallas_call x1, Pallas kernels, attend(): pl.pallas_call(attend_kernel, grid_spec=pltpu.PrefetchScalarGridSpec(num_...  33.7 us
    dot_general x4, matrix products, product_tn(): lax.dot_general(left, right, (((0,), (0,)), ((), ())), preferred_element_...  30.7 us
  transfers between devices with their start and end apart: 98, of which 45 were waited for; matrix products, arithmetic and copies ran while one was open for 22% of the time, Pallas kernels for 15%

profile of v1, /device:TPU:0, one launch (start us, length us, event | category | flops | bytes accessed | tf_op | source)
XLA Modules:
  0.0 810.2 jit_solution(2465886015515618522)
XLA Ops:
  60.0 13.3 %collective-permute-done.30 = bf16[2,16,4096]{2,1,0:T(8,128)(2,1)S(1)} collective-permute-done((bf16[2,16,4096]{2,1,0:T(8,128)(2,1)S(1)}, bf16[2,16,4096]{2,1,0:T(8,128)(2,1)S(1)}, u32[]{:S(2)}, u32[]{:S(2)}) %collective-permute-start.30) | collective-permute-done | bytes 262176 | tf_op jit(solution)/shard_map/ppermute | solution.py:39
  74.9 23.1 %collective-permute-done.35 = bf16[2,16,4096]{2,1,0:T(8,128)(2,1)S(1)} collective-permute-done((bf16[2,16,4096]{2,1,0:T(8,128)(2,1)S(1)}, bf16[2,16,4096]{2,1,0:T(8,128)(2,1)S(1)}, u32[]{:S(2)}, u32[]{:S(2)}) %collective-permute-start.35) | collective-permute-done | bytes 262176 | tf_op jit(solution)/shard_map/ppermute | solution.py:39
  112.5 8.6 %collective-permute-done.14 = bf16[16,40,384]{2,1,0:T(8,128)(2,1)S(1)} collective-permute-done((bf16[16,40,384]{2,1,0:T(8,128)(2,1)S(1)}, bf16[16,40,384]{2,1,0:T(8,128)(2,1)S(1)}, u32[]{:S(2)}, u32[]{:S(2)}) %collective-permute-start.14) | collective-permute-done | bytes 491552 | tf_op jit(solution)/shard_map/ppermute | solution.py:39
  165.2 21.8 %collective-permute-done.42 = bf16[8,64,1024]{2,1,0:T(8,128)(2,1)S(1)} collective-permute-done((bf16[8,64,1024]{2,1,0:T(8,128)(2,1)S(1)}, bf16[8,64,1024]{2,1,0:T(8,128)(2,1)S(1)}, u32[]{:S(2)}, u32[]{:S(2)}) %collective-permute-start.42) | collective-permute-done | bytes 1048608 | tf_op jit(solution)/shard_map/ppermute | solution.py:39
  189.6 19.8 %collective-permute-done.32 = bf16[8,16,4096]{2,1,0:T(8,128)(2,1)S(1)} collective-permute-done((bf16[8,16,4096]{2,1,0:T(8,128)(2,1)S(1)}, bf16[8,16,4096]{2,1,0:T(8,128)(2,1)S(1)}, u32[]{:S(2)}, u32[]{:S(2)}) %collective-permute-start.32) | collective-permute-done | bytes 1048608 | tf_op jit(solution)/shard_map/ppermute | solution.py:39
  231.9 11.7 %collective-permute-done.15.before = bf16[2,576,256]{2,1,0:T(8,128)(2,1)S(1)} collective-permute-done((bf16[2,576,256]{2,1,0:T(8,128)(2,1)S(1)}, bf16[2,576,256]{2,1,0:T(8,128)(2,1)S(1)}, u32[]{:S(2)}, u32[]{:S(2)}) %collective-permute-start.15) | collective-permute-done | bytes 589856 | tf_op jit(solution)/shard_map/ppermute | solution.py:45
  249.4 11.6 %collective-permute-done.16.after = bf16[2,576,256]{2,1,0:T(8,128)(2,1)} collective-permute-done((bf16[2,576,256]{2,1,0:T(8,128)(2,1)S(1)}, bf16[2,576,256]{2,1,0:T(8,128)(2,1)}, u32[]{:S(2)}, u32[]{:S(2)}) %collective-permute-start.16) | collective-permute-done | bytes 589856 | tf_op jit(solution)/shard_map/ppermute | solution.py:45
  264.9 33.7 %shard_map.326 = (bf16[8,2,256,128]{3,2,1,0:T(8,128)(2,1)}, f32[32,256]{1,0:T(8,128)}) custom-call(s32[3]{0:T(128)} %pad_add_fusion.info, s32[2,16]{1,0:T(2,128)} %concatenate.128.bounds, bf16[2,8,256,384]{3,2,1,0:T(8,128)(2,1)} %bitcast.310, bf16[2,576,256]{2,1,0:T(8,128)(2,1)} %copy-done.13, bf16[2,576,256]{2,1,0:T(8,128)(2,1)} %collective-permute-done.16.after), custom_call_target="tpu_custom_call" | custom-call | tf_op jit(solution)/shard_map/pallas_call | solution.py:433
  304.6 9.9 %shard_map.327 = bf16[16,2,1,32,1024]{4,3,2,1,0:T(8,128)(2,1)} custom-call(s32[3]{0:T(128)} %pad_add_fusion.info, s32[1,16]{1,0:T(1,128)} %constant.97.clone.spots, bf16[16,32,1024]{2,1,0:T(8,128)(2,1)} %constant_dynamic-update-slice_fusion.31.refs_0_, bf16[16,32,1024]{2,1,0:T(8,128)(2,1)} %collective-permute-done.28.refs_1_), custom_call_target="tpu_custom_call" | custom-call | tf_op jit(solution)/shard_map/pallas_call | solution.py:109
  314.5 12.5 %shard_map.329 = bf16[16,2,2,64,1024]{4,3,2,1,0:T(8,128)(2,1)} custom-call(s32[3]{0:T(128)} %pad_add_fusion.info, s32[2,16]{1,0:T(2,128)} %constant.98.clone.spots, bf16[16,64,1024]{2,1,0:T(8,128)(2,1)} %constant_dynamic-update-slice_fusion.46.refs_0_, bf16[16,64,1024]{2,1,0:T(8,128)(2,1)} %collective-permute-done.43.refs_1_, ...), custom_call_target="tpu_custom_call" | custom-call | tf_op jit(solution)/shard_map/pallas_call | solution.py:109
  327.0 12.6 %shard_map.328 = bf16[16,2,2,16,4096]{4,3,2,1,0:T(8,128)(2,1)} custom-call(s32[3]{0:T(128)} %pad_add_fusion.info, s32[2,16]{1,0:T(2,128)} %constant.98.clone.spots, bf16[16,16,4096]{2,1,0:T(8,128)(2,1)} %constant_dynamic-update-slice_fusion.36.refs_0_, bf16[16,16,4096]{2,1,0:T(8,128)(2,1)} %collective-permute-done.33.refs_1_, ...), custom_call_target="tpu_custom_call" | custom-call | tf_op jit(solution)/shard_map/pallas_call | solution.py:109
  348.2 7.5 collective-permute-done.21
  367.5 10.6 %fusion.59 = (bf16[4096]{0:T(1024)(128)(2,1)S(1)}, bf16[512,4096]{1,0:T(8,128)(2,1)}) fusion(f32[512,4096]{1,0:T(8,128)} %fusion.54, f32[4096]{0:T(1024)S(1)} %copy-done.65, bf16[4096,1024]{1,0:T(8,128)(2,1)S(1)} %bitcast.316, bf16[512,1024]{1,0:T(8,128)(2,1)S(1)} %bitcast.324), kind=kOutput, calls=%fused_computation.366 | convolution fusion | flops 4320129024 | bytes 22044672 | tf_op jit(solution)/shard_map/dot_general | solution.py:34
  407.6 7.4 collective-permute-done.53
  416.0 34.6 %shard_map.330 = (f32[2,2048,128]{2,1,0:T(8,128)}, f32[2,2048,256]{2,1,0:T(8,128)}, bf16[2,576,256]{2,1,0:T(8,128)(2,1)}, bf16[2,576,256]{2,1,0:T(8,128)(2,1)}) custom-call(s32[3]{0:T(128)} %pad_add_fusion.info, s32[2,16]{1,0:T(2,128)} %concatenate.128.bounds, bf16[2,8,256,384]{3,2,1,0:T(8,128)(2,1)} %bitcast.311, bf16[2,576,256]{2,1,0:T(8,128)(2,1)} %copy-done.13, ...), custom_call_target="tpu_custom_call" | custom-call | tf_op jit(solution)/shard_map/pallas_call | solution.py:463
  450.7 10.1 %collective-permute-start.56 = (bf16[2,576,256]{2,1,0:T(8,128)(2,1)}, bf16[2,576,256]{2,1,0:T(8,128)(2,1)}, u32[]{:S(2)}, u32[]{:S(2)}) collective-permute-start(bf16[2,576,256]{2,1,0:T(8,128)(2,1)} %get-tuple-element.35), channel_id=1, source_target_pairs={{0,8},{1,9},{2,10},{3,11},{4,12},{5,13},{6,14},{7,15},{8,16},{9,17... | collective-permute-start | bytes 1769480 | tf_op jit(solution)/shard_map/ppermute | solution.py:45
  462.6 10.9 %convolution_convert_fusion.1 = bf16[1024,4096]{1,0:T(8,128)(2,1)} fusion(bf16[512,4096]{1,0:T(8,128)(2,1)} %get-tuple-element.203, f32[512,1024]{1,0:T(8,128)} %copy-done.9, f32[1024]{0:T(1024)S(1)} %copy-done.70, f32[1024]{0:T(1024)S(1)} %copy-done.64, f32[512]{0:T(512)S(1)} %add_rsqrt_fusion.2, f32[512]{0:T(512)S(1)} %broadcast_multiply_fusion.4), kind=kOutput, calls=%fused_computation.14 | convolution fusion | flops 4301783040 | bytes 14692352 | tf_op jit(solution)/shard_map/dot_general | solution.py:30
  476.4 10.1 %shard_map.333 = (bf16[16,32,1024]{2,1,0:T(8,128)(2,1)}, bf16[16,32,1024]{2,1,0:T(8,128)(2,1)}) custom-call(s32[3]{0:T(128)} %pad_add_fusion.info, s32[1,16]{1,0:T(1,128)} %constant.100.clone.spots, bf16[16,2,1,32,1024]{4,3,2,1,0:T(8,128)(2,1)} %bitcast.329), custom_call_target="tpu_custom_call" | custom-call | tf_op jit(solution)/shard_map/pallas_call | solution.py:127
  486.4 12.6 %shard_map.334 = (bf16[16,16,4096]{2,1,0:T(8,128)(2,1)}, bf16[16,16,4096]{2,1,0:T(8,128)(2,1)}, bf16[16,16,4096]{2,1,0:T(8,128)(2,1)}, bf16[16,16,4096]{2,1,0:T(8,128)(2,1)}) custom-call(s32[3]{0:T(128)} %pad_add_fusion.info, s32[2,16]{1,0:T(2,128)} %constant.99.clone.spots, bf16[16,2,2,16,4096]{4,3,2,1,0:T(8,128)(2,1)} %bitcast.322), custom_call_target="tpu_custom_call" | custom-call | tf_op jit(solution)/shard_map/pallas_call | solution.py:127
  499.0 12.6 %shard_map.335 = (bf16[16,64,1024]{2,1,0:T(8,128)(2,1)}, bf16[16,64,1024]{2,1,0:T(8,128)(2,1)}, bf16[16,64,1024]{2,1,0:T(8,128)(2,1)}, bf16[16,64,1024]{2,1,0:T(8,128)(2,1)}) custom-call(s32[3]{0:T(128)} %pad_add_fusion.info, s32[2,16]{1,0:T(2,128)} %constant.99.clone.spots, bf16[16,2,2,64,1024]{4,3,2,1,0:T(8,128)(2,1)} %bitcast.321), custom_call_target="tpu_custom_call" | custom-call | tf_op jit(solution)/shard_map/pallas_call | solution.py:127
  515.6 11.6 %shard_map.331 = bf16[2,8,256,384]{3,2,1,0:T(8,128)(2,1)} custom-call(s32[3]{0:T(128)} %pad_add_fusion.info, f32[2,2048,128]{2,1,0:T(8,128)} %get-tuple-element.33.query, f32[2,2048,256]{2,1,0:T(8,128)} %get-tuple-element.34.pairs, bf16[2,768,256]{2,1,0:T(8,128)(2,1)} %pad.18.head, bf16[2,768,256]{2,1,0:T(8,128)(2,1)} %pad.19.tail), custom_call_target="tpu_custom_call" | custom-call | tf_op jit(solution)/shard_map/pallas_call | solution.py:510
  527.2 10.0 %fusion.20 = (f32[1024]{0:T(1024)S(1)}, bf16[1024,384,1,1]{1,0,3,2:T(8,128)(2,1)}) fusion(bf16[32,32,384]{2,1,0:T(8,128)(2,1)} %slice.836, bf16[2,8,256,1024]{3,2,1,0:T(8,128)(2,1)} %copy-done.10, bf16[2,8,256,384]{3,2,1,0:T(8,128)(2,1)} %shard_map.331), kind=kOutput, calls=%fused_computation.61 | convolution fusion | flops 3222797312 | bytes 13111296 | tf_op jit(solution)/shard_map/dot_general | solution.py:30
  540.2 12.0 %add_convert_fusion.9 = bf16[512,1024]{1,0:T(8,128)(2,1)} fusion(f32[512,1024]{1,0:T(8,128)} %copy-done.9, bf16[4096,1024]{1,0:T(8,128)(2,1)} %bitcast.313, f32[1024]{0:T(1024)S(1)} %add.468, f32[512,4096]{1,0:T(8,128)} %fusion.54, f32[4096]{0:T(1024)S(1)} %copy-done.65), kind=kOutput, calls=%fused_computation.52 | convolution fusion | flops 4311220224 | bytes 19943424 | tf_op jit(solution)/shard_map/dot_general | solution.py:26
  573.3 17.9 %collective-permute-done.64 = bf16[16,40,384]{2,1,0:T(8,128)(2,1)S(1)} collective-permute-done((bf16[16,40,384]{2,1,0:T(8,128)(2,1)S(1)}, bf16[16,40,384]{2,1,0:T(8,128)(2,1)S(1)}, u32[]{:S(2)}, u32[]{:S(2)}) %collective-permute-start.64) | collective-permute-done | bytes 491552 | tf_op jit(solution)/shard_map/ppermute | solution.py:39
  609.3 12.5 %collective-permute-done.74 = bf16[8,32,1024]{2,1,0:T(8,128)(2,1)S(1)} collective-permute-done((bf16[8,32,1024]{2,1,0:T(8,128)(2,1)S(1)}, bf16[8,32,1024]{2,1,0:T(8,128)(2,1)S(1)}, u32[]{:S(2)}, u32[]{:S(2)}) %collective-permute-start.74) | collective-permute-done | bytes 524320 | tf_op jit(solution)/shard_map/ppermute | solution.py:39
  623.6 7.2 collective-permute-done.75
  660.4 13.5 %collective-permute-done.84 = bf16[8,16,4096]{2,1,0:T(8,128)(2,1)S(1)} collective-permute-done((bf16[8,16,4096]{2,1,0:T(8,128)(2,1)S(1)}, bf16[8,16,4096]{2,1,0:T(8,128)(2,1)S(1)}, u32[]{:S(2)}, u32[]{:S(2)}) %collective-permute-start.84) | collective-permute-done | bytes 1048608 | tf_op jit(solution)/shard_map/ppermute | solution.py:39
  678.6 16.7 %collective-permute-done.94 = bf16[8,64,1024]{2,1,0:T(8,128)(2,1)S(1)} collective-permute-done((bf16[8,64,1024]{2,1,0:T(8,128)(2,1)S(1)}, bf16[8,64,1024]{2,1,0:T(8,128)(2,1)S(1)}, u32[]{:S(2)}, u32[]{:S(2)}) %collective-permute-start.94) | collective-permute-done | bytes 1048608 | tf_op jit(solution)/shard_map/ppermute | solution.py:39
  701.2 32.0 %collective-permute-done.85 = bf16[4,16,4096]{2,1,0:T(8,128)(2,1)S(1)} collective-permute-done((bf16[4,16,4096]{2,1,0:T(8,128)(2,1)S(1)}, bf16[4,16,4096]{2,1,0:T(8,128)(2,1)S(1)}, u32[]{:S(2)}, u32[]{:S(2)}) %collective-permute-start.85) | collective-permute-done | bytes 524320 | tf_op jit(solution)/shard_map/ppermute | solution.py:39
  735.9 7.4 collective-permute-done.95
  750.5 13.5 %collective-permute-done.86 = bf16[2,16,4096]{2,1,0:T(8,128)(2,1)S(1)} collective-permute-done((bf16[2,16,4096]{2,1,0:T(8,128)(2,1)S(1)}, bf16[2,16,4096]{2,1,0:T(8,128)(2,1)S(1)}, u32[]{:S(2)}, u32[]{:S(2)}) %collective-permute-start.86) | collective-permute-done | bytes 262176 | tf_op jit(solution)/shard_map/ppermute | solution.py:39
  794.9 11.4 %collective-permute-done.63 = bf16[1,256,1024]{2,1,0:T(8,128)(2,1)S(1)} collective-permute-done((bf16[1,256,1024]{2,1,0:T(8,128)(2,1)S(1)}, bf16[1,256,1024]{2,1,0:T(8,128)(2,1)S(1)}, u32[]{:S(2)}, u32[]{:S(2)}) %collective-permute-start.63) | collective-permute-done | bytes 524320 | tf_op jit(solution)/shard_map/ppermute | solution.py:39
  (589 shorter events, 346.8 us)
Async XLA Ops:
  24.0 84.6 %collective-permute-start.3 = (bf16[1,256,1024]{2,1,0:T(8,128)(2,1)S(1)}, bf16[1,256,1024]{2,1,0:T(8,128)(2,1)S(1)}, u32[]{:S(2)}, u32[]{:S(2)}) collective-permute-start(bf16[1,256,1024]{2,1,0:T(8,128)(2,1)S(1)} %get-tuple-element.124), channel_id=1, source_target_pairs={{0,4},{1,5},{2,6},{3,7},{4,0},{5,1},{6,2},{7,3},{8,12},{9,13},{10,... | collective-permute-start | bytes 1572872 | tf_op jit(solution)/shard_map/ppermute | solution.py:39
  27.0 83.2 %collective-permute-start = (bf16[1,256,1024]{2,1,0:T(8,128)(2,1)S(1)}, bf16[1,256,1024]{2,1,0:T(8,128)(2,1)S(1)}, u32[]{:S(2)}, u32[]{:S(2)}) collective-permute-start(bf16[1,256,1024]{2,1,0:T(8,128)(2,1)S(1)} %get-tuple-element.121), channel_id=1, source_target_pairs={{0,2},{1,3},{2,0},{3,1},{4,6},{5,7},{6,4},{7,5},{8,10},{9,11},{10,... | collective-permute-start | bytes 1572872 | tf_op jit(solution)/shard_map/ppermute | solution.py:39
  56.2 43.9 %collective-permute-start.40 = (bf16[2,64,1024]{2,1,0:T(8,128)(2,1)S(1)}, bf16[2,64,1024]{2,1,0:T(8,128)(2,1)S(1)}, u32[]{:S(2)}, u32[]{:S(2)}) collective-permute-start(bf16[2,64,1024]{2,1,0:T(8,128)(2,1)S(1)} %pad_maximum_fusion.29), channel_id=1, source_target_pairs={{0,16},{1,17},{2,18},{3,19},{4,20},{5,21},{6,22},{7,23},{8,24},{9,... | collective-permute-start | bytes 786440 | tf_op jit(solution)/shard_map/ppermute | solution.py:39
  59.2 42.5 %collective-permute-start.45 = (bf16[2,64,1024]{2,1,0:T(8,128)(2,1)S(1)}, bf16[2,64,1024]{2,1,0:T(8,128)(2,1)S(1)}, u32[]{:S(2)}, u32[]{:S(2)}) collective-permute-start(bf16[2,64,1024]{2,1,0:T(8,128)(2,1)S(1)} %pad_maximum_fusion.30), channel_id=1, source_target_pairs={{0,16},{1,17},{2,18},{3,19},{4,20},{5,21},{6,22},{7,23},{8,24},{9,... | collective-permute-start | bytes 786440 | tf_op jit(solution)/shard_map/ppermute | solution.py:39
  110.1 43.4 %collective-permute-start.36 = (bf16[4,16,4096]{2,1,0:T(8,128)(2,1)}, bf16[4,16,4096]{2,1,0:T(8,128)(2,1)}, u32[]{:S(2)}, u32[]{:S(2)}) collective-permute-start(bf16[4,16,4096]{2,1,0:T(8,128)(2,1)} %pad_maximum_fusion.21), channel_id=1, source_target_pairs={{0,4},{1,5},{2,6},{3,7},{4,0},{5,1},{6,2},{7,3},{8,12},{9,13},{10,... | collective-permute-start | bytes 1572872 | tf_op jit(solution)/shard_map/ppermute | solution.py:39
  140.0 46.9 %collective-permute-start.42 = (bf16[8,64,1024]{2,1,0:T(8,128)(2,1)S(1)}, bf16[8,64,1024]{2,1,0:T(8,128)(2,1)S(1)}, u32[]{:S(2)}, u32[]{:S(2)}) collective-permute-start(bf16[8,64,1024]{2,1,0:T(8,128)(2,1)S(1)} %pad_maximum_fusion.10), channel_id=1, source_target_pairs={{0,4},{1,5},{2,6},{3,7},{4,0},{5,1},{6,2},{7,3},{8,12},{9,13},{10,... | collective-permute-start | bytes 3145736 | tf_op jit(solution)/shard_map/ppermute | solution.py:39
  142.8 45.7 %collective-permute-start.47 = (bf16[8,64,1024]{2,1,0:T(8,128)(2,1)S(1)}, bf16[8,64,1024]{2,1,0:T(8,128)(2,1)S(1)}, u32[]{:S(2)}, u32[]{:S(2)}) collective-permute-start(bf16[8,64,1024]{2,1,0:T(8,128)(2,1)S(1)} %pad_maximum_fusion.11), channel_id=1, source_target_pairs={{0,2},{1,3},{2,0},{3,1},{4,6},{5,7},{6,4},{7,5},{8,10},{9,11},{10,... | collective-permute-start | bytes 3145736 | tf_op jit(solution)/shard_map/ppermute | solution.py:39
  151.2 58.2 %collective-permute-start.32 = (bf16[8,16,4096]{2,1,0:T(8,128)(2,1)S(1)}, bf16[8,16,4096]{2,1,0:T(8,128)(2,1)S(1)}, u32[]{:S(2)}, u32[]{:S(2)}) collective-permute-start(bf16[8,16,4096]{2,1,0:T(8,128)(2,1)S(1)} %pad_maximum_fusion.8), channel_id=1, source_target_pairs={{0,4},{1,5},{2,6},{3,7},{4,0},{5,1},{6,2},{7,3},{8,12},{9,13},{10,... | collective-permute-start | bytes 3145736 | tf_op jit(solution)/shard_map/ppermute | solution.py:39
  153.5 57.0 %collective-permute-start.5 = (bf16[4,256,1024]{2,1,0:T(8,128)(2,1)S(1)}, bf16[4,256,1024]{2,1,0:T(8,128)(2,1)S(1)}, u32[]{:S(2)}, u32[]{:S(2)}) collective-permute-start(bf16[4,256,1024]{2,1,0:T(8,128)(2,1)S(1)} %pad_maximum_fusion.2), channel_id=1, source_target_pairs={{0,1},{1,0},{2,3},{3,2},{4,5},{5,4},{6,7},{7,6},{8,9},{9,8},{10,11... | collective-permute-start | bytes 6291464 | tf_op jit(solution)/shard_map/ppermute | solution.py:39
  164.5 67.3 %collective-permute-start.27 = (bf16[8,32,1024]{2,1,0:T(8,128)(2,1)}, bf16[8,32,1024]{2,1,0:T(8,128)(2,1)}, u32[]{:S(2)}, u32[]{:S(2)}) collective-permute-start(bf16[8,32,1024]{2,1,0:T(8,128)(2,1)} %pad_maximum_fusion.19), channel_id=1, source_target_pairs={{0,4},{1,5},{2,6},{3,7},{4,0},{5,1},{6,2},{7,3},{8,12},{9,13},{10,... | collective-permute-start | bytes 1572872 | tf_op jit(solution)/shard_map/ppermute | solution.py:39
  186.9 42.2 %collective-permute-start.37 = (bf16[8,16,4096]{2,1,0:T(8,128)(2,1)}, bf16[8,16,4096]{2,1,0:T(8,128)(2,1)S(1)}, u32[]{:S(2)}, u32[]{:S(2)}) collective-permute-start(bf16[8,16,4096]{2,1,0:T(8,128)(2,1)} %pad_maximum_fusion.9), channel_id=1, source_target_pairs={{0,2},{1,3},{2,0},{3,1},{4,6},{5,7},{6,4},{7,5},{8,10},{9,11},{10,... | collective-permute-start | bytes 3145736 | tf_op jit(solution)/shard_map/ppermute | solution.py:39
  209.4 105.1 %collective-permute-start.43 = (bf16[16,64,1024]{2,1,0:T(8,128)(2,1)}, bf16[16,64,1024]{2,1,0:T(8,128)(2,1)}, u32[]{:S(2)}, u32[]{:S(2)}) collective-permute-start(bf16[16,64,1024]{2,1,0:T(8,128)(2,1)} %constant_dynamic-update-slice_fusion.46.refs_0_), channel_id=1, source_target_pairs={{0,1},{1,0},{2,3},{3,2},{4,5},{5,4},{6,7},{7,6},{8,9},{9,8},{10,11... | collective-permute-start | bytes 6291464 | tf_op jit(solution)/shard_map/ppermute | solution.py:39
  210.4 104.0 %collective-permute-start.48 = (bf16[16,64,1024]{2,1,0:T(8,128)(2,1)}, bf16[16,64,1024]{2,1,0:T(8,128)(2,1)}, u32[]{:S(2)}, u32[]{:S(2)}) collective-permute-start(bf16[16,64,1024]{2,1,0:T(8,128)(2,1)} %constant_dynamic-update-slice_fusion.51.refs_2_), channel_id=1, source_target_pairs={{0,1},{1,0},{2,3},{3,2},{4,5},{5,4},{6,7},{7,6},{8,9},{9,8},{10,11... | collective-permute-start | bytes 6291464 | tf_op jit(solution)/shard_map/ppermute | solution.py:39
  213.5 113.5 %collective-permute-start.33 = (bf16[16,16,4096]{2,1,0:T(8,128)(2,1)}, bf16[16,16,4096]{2,1,0:T(8,128)(2,1)}, u32[]{:S(2)}, u32[]{:S(2)}) collective-permute-start(bf16[16,16,4096]{2,1,0:T(8,128)(2,1)} %constant_dynamic-update-slice_fusion.36.refs_0_), channel_id=1, source_target_pairs={{0,1},{1,0},{2,3},{3,2},{4,5},{5,4},{6,7},{7,6},{8,9},{9,8},{10,11... | collective-permute-start | bytes 6291464 | tf_op jit(solution)/shard_map/ppermute | solution.py:39
  231.7 95.3 %collective-permute-start.38 = (bf16[16,16,4096]{2,1,0:T(8,128)(2,1)}, bf16[16,16,4096]{2,1,0:T(8,128)(2,1)}, u32[]{:S(2)}, u32[]{:S(2)}) collective-permute-start(bf16[16,16,4096]{2,1,0:T(8,128)(2,1)} %constant_dynamic-update-slice_fusion.41.refs_2_), channel_id=1, source_target_pairs={{0,1},{1,0},{2,3},{3,2},{4,5},{5,4},{6,7},{7,6},{8,9},{9,8},{10,11... | collective-permute-start | bytes 6291464 | tf_op jit(solution)/shard_map/ppermute | solution.py:39
  261.0 39.7 %collective-permute-start.28 = (bf16[16,32,1024]{2,1,0:T(8,128)(2,1)}, bf16[16,32,1024]{2,1,0:T(8,128)(2,1)}, u32[]{:S(2)}, u32[]{:S(2)}) collective-permute-start(bf16[16,32,1024]{2,1,0:T(8,128)(2,1)} %constant_dynamic-update-slice_fusion.31.refs_0_), channel_id=1, source_target_pairs={{0,1},{1,0},{2,3},{3,2},{4,5},{5,4},{6,7},{7,6},{8,9},{9,8},{10,11... | collective-permute-start | bytes 3145736 | tf_op jit(solution)/shard_map/ppermute | solution.py:39
  300.7 42.7 %collective-permute-start.17 = (bf16[2,256,128]{2,1,0:T(8,128)(2,1)}, bf16[2,256,128]{2,1,0:T(8,128)(2,1)}, u32[]{:S(2)}, u32[]{:S(2)}) collective-permute-start(bf16[2,256,128]{2,1,0:T(8,128)(2,1)} %get-tuple-element.119), channel_id=1, source_target_pairs={{0,1},{1,0},{2,3},{3,2},{4,5},{5,4},{6,7},{7,6},{8,9},{9,8},{10,11... | collective-permute-start | bytes 393224 | tf_op jit(solution)/shard_map/ppermute | solution.py:39
  450.7 60.9 %collective-permute-start.56 = (bf16[2,576,256]{2,1,0:T(8,128)(2,1)}, bf16[2,576,256]{2,1,0:T(8,128)(2,1)}, u32[]{:S(2)}, u32[]{:S(2)}) collective-permute-start(bf16[2,576,256]{2,1,0:T(8,128)(2,1)} %get-tuple-element.35), channel_id=1, source_target_pairs={{0,8},{1,9},{2,10},{3,11},{4,12},{5,13},{6,14},{7,15},{8,16},{9,17... | collective-permute-start | bytes 1769480 | tf_op jit(solution)/shard_map/ppermute | solution.py:45
  460.8 52.9 %collective-permute-start.57 = (bf16[2,576,256]{2,1,0:T(8,128)(2,1)}, bf16[2,576,256]{2,1,0:T(8,128)(2,1)}, u32[]{:S(2)}, u32[]{:S(2)}) collective-permute-start(bf16[2,576,256]{2,1,0:T(8,128)(2,1)} %get-tuple-element.36), channel_id=1, source_target_pairs={{8,0},{9,1},{10,2},{11,3},{12,4},{13,5},{14,6},{15,7},{16,8},{17,9... | collective-permute-start | bytes 1769480 | tf_op jit(solution)/shard_map/ppermute | solution.py:45
  486.4 105.0 %collective-permute-start.73 = (bf16[16,32,1024]{2,1,0:T(8,128)(2,1)}, bf16[16,32,1024]{2,1,0:T(8,128)(2,1)}, u32[]{:S(2)}, u32[]{:S(2)}) collective-permute-start(bf16[16,32,1024]{2,1,0:T(8,128)(2,1)} %get-tuple-element.38), channel_id=1, source_target_pairs={{0,1},{1,0},{2,3},{3,2},{4,5},{5,4},{6,7},{7,6},{8,9},{9,8},{10,11... | collective-permute-start | bytes 3145736 | tf_op jit(solution)/shard_map/ppermute | solution.py:39
  605.6 39.1 %collective-permute-start.83 = (bf16[16,16,4096]{2,1,0:T(8,128)(2,1)}, bf16[16,16,4096]{2,1,0:T(8,128)(2,1)}, u32[]{:S(2)}, u32[]{:S(2)}) collective-permute-start(bf16[16,16,4096]{2,1,0:T(8,128)(2,1)} %get-tuple-element.42), channel_id=1, source_target_pairs={{0,1},{1,0},{2,3},{3,2},{4,5},{5,4},{6,7},{7,6},{8,9},{9,8},{10,11... | collective-permute-start | bytes 6291464 | tf_op jit(solution)/shard_map/ppermute | solution.py:39
  605.8 41.9 %collective-permute-start.78 = (bf16[16,16,4096]{2,1,0:T(8,128)(2,1)}, bf16[16,16,4096]{2,1,0:T(8,128)(2,1)}, u32[]{:S(2)}, u32[]{:S(2)}) collective-permute-start(bf16[16,16,4096]{2,1,0:T(8,128)(2,1)} %get-tuple-element.40), channel_id=1, source_target_pairs={{0,1},{1,0},{2,3},{3,2},{4,5},{5,4},{6,7},{7,6},{8,9},{9,8},{10,11... | collective-permute-start | bytes 6291464 | tf_op jit(solution)/shard_map/ppermute | solution.py:39
  606.8 44.2 %collective-permute-start.93 = (bf16[16,64,1024]{2,1,0:T(8,128)(2,1)}, bf16[16,64,1024]{2,1,0:T(8,128)(2,1)}, u32[]{:S(2)}, u32[]{:S(2)}) collective-permute-start(bf16[16,64,1024]{2,1,0:T(8,128)(2,1)} %get-tuple-element.46), channel_id=1, source_target_pairs={{0,1},{1,0},{2,3},{3,2},{4,5},{5,4},{6,7},{7,6},{8,9},{9,8},{10,11... | collective-permute-start | bytes 6291464 | tf_op jit(solution)/shard_map/ppermute | solution.py:39
  607.5 47.5 %collective-permute-start.88 = (bf16[16,64,1024]{2,1,0:T(8,128)(2,1)}, bf16[16,64,1024]{2,1,0:T(8,128)(2,1)}, u32[]{:S(2)}, u32[]{:S(2)}) collective-permute-start(bf16[16,64,1024]{2,1,0:T(8,128)(2,1)} %get-tuple-element.44), channel_id=1, source_target_pairs={{0,1},{1,0},{2,3},{3,2},{4,5},{5,4},{6,7},{7,6},{8,9},{9,8},{10,11... | collective-permute-start | bytes 6291464 | tf_op jit(solution)/shard_map/ppermute | solution.py:39
  644.0 102.7 %collective-permute-start.61 = (bf16[4,256,1024]{2,1,0:T(8,128)(2,1)}, bf16[4,256,1024]{2,1,0:T(8,128)(2,1)S(1)}, u32[]{:S(2)}, u32[]{:S(2)}) collective-permute-start(bf16[4,256,1024]{2,1,0:T(8,128)(2,1)} %pad_maximum_fusion.4), channel_id=1, source_target_pairs={{0,1},{1,0},{2,3},{3,2},{4,5},{5,4},{6,7},{7,6},{8,9},{9,8},{10,11... | collective-permute-start | bytes 6291464 | tf_op jit(solution)/shard_map/ppermute | solution.py:39
  655.0 40.3 %collective-permute-start.94 = (bf16[8,64,1024]{2,1,0:T(8,128)(2,1)S(1)}, bf16[8,64,1024]{2,1,0:T(8,128)(2,1)S(1)}, u32[]{:S(2)}, u32[]{:S(2)}) collective-permute-start(bf16[8,64,1024]{2,1,0:T(8,128)(2,1)S(1)} %get-tuple-element.73), channel_id=1, source_target_pairs={{0,4},{1,5},{2,6},{3,7},{4,0},{5,1},{6,2},{7,3},{8,12},{9,13},{10,... | collective-permute-start | bytes 3145736 | tf_op jit(solution)/shard_map/ppermute | solution.py:39
  657.8 41.8 %collective-permute-start.89 = (bf16[8,64,1024]{2,1,0:T(8,128)(2,1)S(1)}, bf16[8,64,1024]{2,1,0:T(8,128)(2,1)S(1)}, u32[]{:S(2)}, u32[]{:S(2)}) collective-permute-start(bf16[8,64,1024]{2,1,0:T(8,128)(2,1)S(1)} %get-tuple-element.71), channel_id=1, source_target_pairs={{0,2},{1,3},{2,0},{3,1},{4,6},{5,7},{6,4},{7,5},{8,10},{9,11},{10,... | collective-permute-start | bytes 3145736 | tf_op jit(solution)/shard_map/ppermute | solution.py:39
  673.8 74.1 %collective-permute-start.59 = (bf16[2,256,1024]{2,1,0:T(8,128)(2,1)S(1)}, bf16[2,256,1024]{2,1,0:T(8,128)(2,1)S(1)}, u32[]{:S(2)}, u32[]{:S(2)}) collective-permute-start(bf16[2,256,1024]{2,1,0:T(8,128)(2,1)S(1)} %pad_maximum_fusion.12), channel_id=1, source_target_pairs={{0,2},{1,3},{2,0},{3,1},{4,6},{5,7},{6,4},{7,5},{8,10},{9,11},{10,... | collective-permute-start | bytes 3145736 | tf_op jit(solution)/shard_map/ppermute | solution.py:39
  677.1 56.2 %collective-permute-start.85 = (bf16[4,16,4096]{2,1,0:T(8,128)(2,1)S(1)}, bf16[4,16,4096]{2,1,0:T(8,128)(2,1)S(1)}, u32[]{:S(2)}, u32[]{:S(2)}) collective-permute-start(bf16[4,16,4096]{2,1,0:T(8,128)(2,1)S(1)} %get-tuple-element.91), channel_id=1, source_target_pairs={{0,2},{1,3},{2,0},{3,1},{4,6},{5,7},{6,4},{7,5},{8,10},{9,11},{10,... | collective-permute-start | bytes 1572872 | tf_op jit(solution)/shard_map/ppermute | solution.py:39
  695.3 39.4 %collective-permute-start.80 = (bf16[4,16,4096]{2,1,0:T(8,128)(2,1)S(1)}, bf16[4,16,4096]{2,1,0:T(8,128)(2,1)S(1)}, u32[]{:S(2)}, u32[]{:S(2)}) collective-permute-start(bf16[4,16,4096]{2,1,0:T(8,128)(2,1)S(1)} %get-tuple-element.89), channel_id=1, source_target_pairs={{0,4},{1,5},{2,6},{3,7},{4,0},{5,1},{6,2},{7,3},{8,12},{9,13},{10,... | collective-permute-start | bytes 1572872 | tf_op jit(solution)/shard_map/ppermute | solution.py:39
  699.6 43.7 %collective-permute-start.95 = (bf16[4,64,1024]{2,1,0:T(8,128)(2,1)S(1)}, bf16[4,64,1024]{2,1,0:T(8,128)(2,1)S(1)}, u32[]{:S(2)}, u32[]{:S(2)}) collective-permute-start(bf16[4,64,1024]{2,1,0:T(8,128)(2,1)S(1)} %get-tuple-element.87), channel_id=1, source_target_pairs={{0,2},{1,3},{2,0},{3,1},{4,6},{5,7},{6,4},{7,5},{8,10},{9,11},{10,... | collective-permute-start | bytes 1572872 | tf_op jit(solution)/shard_map/ppermute | solution.py:39
  749.0 42.7 %collective-permute-start.60 = (bf16[1,256,1024]{2,1,0:T(8,128)(2,1)S(1)}, bf16[1,256,1024]{2,1,0:T(8,128)(2,1)S(1)}, u32[]{:S(2)}, u32[]{:S(2)}) collective-permute-start(bf16[1,256,1024]{2,1,0:T(8,128)(2,1)S(1)} %get-tuple-element.61), channel_id=1, source_target_pairs={{0,4},{1,5},{2,6},{3,7},{4,0},{5,1},{6,2},{7,3},{8,12},{9,13},{10,... | collective-permute-start | bytes 1572872 | tf_op jit(solution)/shard_map/ppermute | solution.py:39
  (146 other events, 2190.5 us)

commit v2 on v1

--- a/solution.py
+++ b/solution.py
@@ -59,95 +59,54 @@
     return current, swap(current, order[-1])
 
 
-def collect_kernel(parts, info, spots, *refs):
-    whole = refs[2 * parts]
-    side = jnp.bitwise_and(info[0], 1)
-    for k in range(parts):
-        whole[0, side, k] = refs[2 * k][0]
-        whole[0, 1 - side, k] = refs[2 * k + 1][0]
-
-
-def spread_kernel(parts, info, spots, *refs):
-    whole = refs[0]
-    side = jnp.bitwise_and(info[0], 1)
-    for k in range(parts):
-        refs[1 + 2 * k][0] = whole[0, side, k]
-        refs[2 + 2 * k][0] = whole[0, 1 - side, k]
-
-
-def block_specs(parts, half, part_rows, columns):
-    piece = [
-        pl.BlockSpec((1, part_rows, columns), lambda s, info, spots, k=k: (spots[k, s], 0, 0))
-        for k in range(parts)
-        for _ in range(2)
-    ]
-    whole = pl.BlockSpec(
-        (1, 2, parts, part_rows, columns),
-        lambda s, info, spots: (jnp.bitwise_xor(info[0] >> 1, s), 0, 0, 0, 0),
-    )
-    return piece, whole
-
-
-def spot_table(orders, half):
-    table = []
-    for order in orders:
-        held = places(order)
-        table.append([held.index(2 * s) for s in range(half)])
-    return jnp.asarray(table, jnp.int32)
-
-
-def gathered_weight(info, shard, orders):
-    rows, columns = shard.shape
-    n = lax.axis_size("seq")
-    half = n // 2
-    parts = len(orders)
-    part_rows = rows // parts
-    ins = []
-    for k, order in enumerate(orders):
-        ins += gather_bits(shard[k * part_rows : (k + 1) * part_rows], order)
-    piece, whole = block_specs(parts, half, part_rows, columns)
-    joined = pl.pallas_call(
-        functools.partial(collect_kernel, parts),
-        grid_spec=pltpu.PrefetchScalarGridSpec(
-            num_scalar_prefetch=2, grid=(half,), in_specs=piece, out_specs=whole
-        ),
-        out_shape=jax.ShapeDtypeStruct((half, 2, parts, part_rows, columns), shard.dtype),
-    )(info, spot_table([order[:-1] for order in orders], half), *ins)
-    return joined.reshape(n * rows, columns)
-
-
-def scattered_sum(info, partial, orders):
-    n = lax.axis_size("seq")
-    total_rows, columns = partial.shape
-    rows = total_rows // n
-    parts = len(orders)
-    part_rows = rows // parts
-    half = n // 2
-    piece, whole = block_specs(parts, half, part_rows, columns)
-    placed = pl.pallas_call(
-        functools.partial(spread_kernel, parts),
-        grid_spec=pltpu.PrefetchScalarGridSpec(
-            num_scalar_prefetch=2, grid=(half,), in_specs=[whole], out_specs=piece
-        ),
-        out_shape=[jax.ShapeDtypeStruct((half, part_rows, columns), partial.dtype)] * (2 * parts),
-    )(
-        info,
-        spot_table([order[1:][::-1] for order in orders], half),
-        partial.reshape(half, 2, parts, part_rows, columns),
-    )
-    sums = []
-    for k, order in enumerate(orders):
-        keep, send = placed[2 * k], placed[2 * k + 1]
-        size = half
-        for bit in order:
-            got = swap(send, bit)
-            if size == 1:
-                sums.append(keep[0].astype(f32) + got[0].astype(f32))
-                break
-            size //= 2
-            send = (keep[size:].astype(f32) + got[size:].astype(f32)).astype(bf16)
-            keep = (keep[:size].astype(f32) + got[:size].astype(f32)).astype(bf16)
-    return jnp.concatenate(sums, axis=0) if len(sums) > 1 else sums[0]
+def tie(value, *earlier):
+    return lax.optimization_barrier((value,) + earlier)[0]
+
+
+def own_bit(me, bit):
+    return jnp.where(jnp.bitwise_and(me, bit) != 0, 1, 0)
+
+
+def pick(block, axis, index):
+    return lax.dynamic_index_in_dim(block, index, axis, keepdims=False)
+
+
+class Scatter:
+    def __init__(self, me, partial, order):
+        count = partial.shape[0]
+        depth = count.bit_length() - 1
+        self.me = me
+        self.block = partial.reshape((2,) * depth + partial.shape[1:])
+        self.bits = [1 << (depth - 1 - axis) for axis in range(depth)]
+        self.order = list(order)
+        self.got = None
+        self.send = None
+        self.split()
+
+    def half(self, index, axis):
+        part = pick(self.block, axis, index)
+        if self.got is None:
+            return part
+        return (part.astype(f32) + pick(self.got, axis, index).astype(f32)).astype(bf16)
+
+    def split(self):
+        bit = self.order.pop(0)
+        axis = self.bits.index(bit)
+        self.bits.pop(axis)
+        mine = own_bit(self.me, bit)
+        self.send, keep = self.half(1 - mine, axis), self.half(mine, axis)
+        self.block, self.got, self.bit = keep, None, bit
+
+    def swap(self, *earlier):
+        send = tie(self.send, *earlier) if earlier else self.send
+        self.got = swap(send, self.bit)
+
+    def advance(self, *earlier):
+        self.split()
+        self.swap(*earlier)
+
+    def total(self):
+        return self.block.astype(f32) + self.got.astype(f32)
 
 
 def turn_kernel(info, blocks, turned):
@@ -168,38 +127,37 @@
     )(info, blocks)
 
 
-def load_rows(place_in_plane, qkv, before, after, queries, keys, values, sem):
-    micro_count, blocks = qkv.shape[0], qkv.shape[1]
-    rows = qkv.shape[2]
+def load_rows(micros, place_in_plane, qkv, before, after, queries, keys, values, sem):
+    blocks, rows = qkv.shape[1], qkv.shape[2]
     own = blocks * rows
     for buffer in (keys, values):
-        for m in range(micro_count):
-            buffer[m, 0 : LEAD - HALO, :] = jnp.zeros((LEAD - HALO, PAIR), bf16)
+        for slot in range(len(micros)):
+            buffer[slot, 0 : LEAD - HALO, :] = jnp.zeros((LEAD - HALO, PAIR), bf16)
             tail = buffer.shape[1] - (LEAD + own + HALO)
-            buffer[m, LEAD + own + HALO :, :] = jnp.zeros((tail, PAIR), bf16)
+            buffer[slot, LEAD + own + HALO :, :] = jnp.zeros((tail, PAIR), bf16)
     started = []
-    for m in range(micro_count):
+    for slot, m in enumerate(micros):
         for r in range(blocks):
             spot = pl.multiple_of(jnp.bitwise_xor(place_in_plane, r) * rows, rows)
             started += [
                 pltpu.make_async_copy(
-                    qkv.at[m, r, :, pl.ds(0, PAIR)], queries.at[m, pl.ds(spot, rows)], sem
+                    qkv.at[m, r, :, pl.ds(0, PAIR)], queries.at[slot, pl.ds(spot, rows)], sem
                 ),
                 pltpu.make_async_copy(
-                    qkv.at[m, r, :, pl.ds(PAIR, PAIR)], keys.at[m, pl.ds(LEAD + spot, rows)], sem
+                    qkv.at[m, r, :, pl.ds(PAIR, PAIR)], keys.at[slot, pl.ds(LEAD + spot, rows)], sem
                 ),
                 pltpu.make_async_copy(
-                    qkv.at[m, r, :, pl.ds(2 * PAIR, PAIR)], values.at[m, pl.ds(LEAD + spot, rows)], sem
+                    qkv.at[m, r, :, pl.ds(2 * PAIR, PAIR)], values.at[slot, pl.ds(LEAD + spot, rows)], sem
                 ),
             ]
         for which, buffer in enumerate((keys, values)):
             columns = pl.ds(which * PAIR, PAIR)
             started += [
                 pltpu.make_async_copy(
-                    before.at[m, :, columns], buffer.at[m, pl.ds(LEAD - HALO, HALO)], sem
+                    before.at[m, :, columns], buffer.at[slot, pl.ds(LEAD - HALO, HALO)], sem
                 ),
                 pltpu.make_async_copy(
-                    after.at[m, :, columns], buffer.at[m, pl.ds(LEAD + own, HALO)], sem
+                    after.at[m, :, columns], buffer.at[slot, pl.ds(LEAD + own, HALO)], sem
                 ),
             ]
     return started
@@ -231,7 +189,7 @@
     own = blocks * rows
     place_in_plane, base = info[1], info[2]
     image_count = bounds.shape[1] - 1
-    started = load_rows(place_in_plane, qkv, before, after, queries, keys, values, sem)
+    started = load_rows(range(micro_count), place_in_plane, qkv, before, after, queries, keys, values, sem)
     for copy in started:
         copy.start()
     value_t[:, HEAD_DIM:, :] = jnp.ones((2, 16, WINDOW), bf16)
@@ -300,44 +258,21 @@
         copy.wait()
 
 
-def attend_back_kernel(
-    info,
-    bounds,
-    qkv,
-    before,
-    after,
-    mixed,
-    grad_mixed,
-    stats,
-    grad_query,
-    grad_pairs,
-    grad_before,
-    grad_after,
-    queries,
-    keys,
-    values,
-    result,
-    grads,
-    key_aug,
-    key_t,
-    acc_query,
-    acc_key,
-    acc_value,
-    edge,
-    sem,
-):
-    micro_count, blocks, rows, _ = qkv.shape
+def attend_back_kernel(m, info, bounds, qkv, before, after, mixed, *refs):
+    blocks, rows = qkv.shape[1], qkv.shape[2]
     own = blocks * rows
+    grad_mixed, refs = refs[:blocks], refs[blocks:]
+    stats, grad_query, grad_pairs, grad_before, grad_after, refs = *refs[:5], refs[5:]
+    queries, keys, values, result, grads, key_aug, key_t, acc_query, acc_key, acc_value, edge, sem = refs
     place_in_plane, base = info[1], info[2]
     image_count = bounds.shape[1] - 1
-    started = load_rows(place_in_plane, qkv, before, after, queries, keys, values, sem)
-    for m in range(micro_count):
-        for r in range(blocks):
-            spot = pl.multiple_of(jnp.bitwise_xor(place_in_plane, r) * rows, rows)
-            started += [
-                pltpu.make_async_copy(mixed.at[r, m], result.at[m, pl.ds(spot, rows)], sem),
-                pltpu.make_async_copy(grad_mixed.at[r, m], grads.at[m, pl.ds(spot, rows)], sem),
-            ]
+    started = load_rows([m], place_in_plane, qkv, before, after, queries, keys, values, sem)
+    for r in range(blocks):
+        spot = pl.multiple_of(jnp.bitwise_xor(place_in_plane, r) * rows, rows)
+        started += [
+            pltpu.make_async_copy(mixed.at[r, m], result.at[pl.ds(spot, rows)], sem),
+            pltpu.make_async_copy(grad_mixed[r].at[m], grads.at[pl.ds(spot, rows)], sem),
+        ]
     for copy in started:
         copy.start()
     acc_query[...] = jnp.zeros_like(acc_query)
@@ -349,72 +284,68 @@
     for copy in started:
         copy.wait()
 
-    for m in range(micro_count):
-
-        def one_image(image, carry):
-            begin, finish = image_span(bounds, m, image, base)
-
-            @pl.when((finish > LEAD) & (begin < LEAD + own))
-            def _():
-                key_start = pl.multiple_of((begin >> 4) << 4, 16)
-                key_rows = pl.ds(key_start, WINDOW)
-                key_block(keys, m, begin, finish, key_start, key_aug)
-                turned = keys[m, key_rows, :].astype(f32).T
-                key_t[0] = turned[:HEAD_DIM].astype(bf16)
-                key_t[1] = turned[HEAD_DIM:].astype(bf16)
-                first_tile = jnp.maximum(begin - LEAD, 0) >> 8
-                last_tile = (jnp.minimum(finish - LEAD, own) + TILE - 1) >> 8
-
-                def one_tile(tile, carry):
-                    spot = pl.multiple_of(tile * TILE, TILE)
-                    here = pl.ds(spot, TILE)
-                    scaled = queries[m, here, :].astype(f32) * (HEAD_DIM**-0.5)
-                    grad = grads[m, here, :].astype(f32)
-                    dots = (grad * result[m, here, :].astype(f32)).T
-                    inside_lane = (lane_row + (spot + LEAD) >= begin) & (lane_row + (spot + LEAD) < finish)
-                    both = zip(split_heads(scaled, lanes), split_heads(grad, lanes))
-                    pieces = []
-                    add_key, add_value = None, None
-                    for h, (query, grad_h) in enumerate(both):
-                        row = (m * 2 + h) * blocks + tile
-                        level = jnp.where(inside_lane, stats[pl.ds(row, 1), :], -negative_fill)
-                        row_dot = jnp.sum(
-                            dots[h * HEAD_DIM : (h + 1) * HEAD_DIM], axis=0, keepdims=True
-                        )
-                        aug = jnp.concatenate([query, query_mark], axis=1)
-                        shares = jnp.exp(product_nt(key_aug[...], aug) - level)
-                        grad_share = product_nt(values[m, key_rows, :], grad_h)
-                        grad_scores = (shares * (grad_share - row_dot)).astype(bf16)
-                        value_part = product(shares.astype(bf16), grad_h)
-                        key_part = product(grad_scores, query)
-                        add_value = value_part if h == 0 else add_value + value_part
-                        add_key = key_part if h == 0 else add_key + key_part
-                        pieces.append(product(key_t[h], grad_scores))
-                    acc_value[m, key_rows, :] += add_value
-                    acc_key[m, key_rows, :] += add_key
-                    acc_query[m, here, :] += jnp.concatenate(pieces, axis=0).T * (HEAD_DIM**-0.5)
-                    return carry
-
-                lax.fori_loop(first_tile, last_tile, one_tile, 0)
-
-            return carry
-
-        lax.fori_loop(0, image_count, one_image, 0)
-
-    started = []
-    for m in range(micro_count):
-        started.append(pltpu.make_async_copy(acc_query.at[m], grad_query.at[m], sem))
-        for which, acc in enumerate((acc_key, acc_value)):
-            columns = pl.ds(which * PAIR, PAIR)
-            edge[0, m, :, which * PAIR : (which + 1) * PAIR] = acc[m, LEAD - HALO : LEAD, :].astype(bf16)
-            edge[1, m, :, which * PAIR : (which + 1) * PAIR] = acc[
-                m, LEAD + own : LEAD + own + HALO, :
-            ].astype(bf16)
-            started.append(
-                pltpu.make_async_copy(acc.at[m, pl.ds(LEAD, own)], grad_pairs.at[m, :, columns], sem)
-            )
-        started.append(pltpu.make_async_copy(edge.at[0, m], grad_before.at[m], sem))
-        started.append(pltpu.make_async_copy(edge.at[1, m], grad_after.at[m], sem))
+
+    def one_image(image, carry):
+        begin, finish = image_span(bounds, m, image, base)
+
+        @pl.when((finish > LEAD) & (begin < LEAD + own))
+        def _():
+            key_start = pl.multiple_of((begin >> 4) << 4, 16)
+            key_rows = pl.ds(key_start, WINDOW)
+            key_block(keys, 0, begin, finish, key_start, key_aug)
+            turned = keys[0, key_rows, :].astype(f32).T
+            key_t[0] = turned[:HEAD_DIM].astype(bf16)
+            key_t[1] = turned[HEAD_DIM:].astype(bf16)
+            first_tile = jnp.maximum(begin - LEAD, 0) >> 8
+            last_tile = (jnp.minimum(finish - LEAD, own) + TILE - 1) >> 8
+
+            def one_tile(tile, carry):
+                spot = pl.multiple_of(tile * TILE, TILE)
+                here = pl.ds(spot, TILE)
+                scaled = queries[0, here, :].astype(f32) * (HEAD_DIM**-0.5)
+                grad = grads[ here, :].astype(f32)
+                dots = (grad * result[ here, :].astype(f32)).T
+                inside_lane = (lane_row + (spot + LEAD) >= begin) & (lane_row + (spot + LEAD) < finish)
+                both = zip(split_heads(scaled, lanes), split_heads(grad, lanes))
+                pieces = []
+                add_key, add_value = None, None
+                for h, (query, grad_h) in enumerate(both):
+                    row = (m * 2 + h) * blocks + tile
+                    level = jnp.where(inside_lane, stats[pl.ds(row, 1), :], -negative_fill)
+                    row_dot = jnp.sum(
+                        dots[h * HEAD_DIM : (h + 1) * HEAD_DIM], axis=0, keepdims=True
+                    )
+                    aug = jnp.concatenate([query, query_mark], axis=1)
+                    shares = jnp.exp(product_nt(key_aug[...], aug) - level)
+                    grad_share = product_nt(values[0, key_rows, :], grad_h)
+                    grad_scores = (shares * (grad_share - row_dot)).astype(bf16)
+                    value_part = product(shares.astype(bf16), grad_h)
+                    key_part = product(grad_scores, query)
+                    add_value = value_part if h == 0 else add_value + value_part
+                    add_key = key_part if h == 0 else add_key + key_part
+                    pieces.append(product(key_t[h], grad_scores))
+                acc_value[ key_rows, :] += add_value
+                acc_key[ key_rows, :] += add_key
+                acc_query[ here, :] += jnp.concatenate(pieces, axis=0).T * (HEAD_DIM**-0.5)
+                return carry
+
+            lax.fori_loop(first_tile, last_tile, one_tile, 0)
+
+        return carry
+
+    lax.fori_loop(0, image_count, one_image, 0)
+
+    edge_rows = grad_before.shape[0]
+    edge[0, : edge_rows - HALO, :] = jnp.zeros((edge_rows - HALO, 2 * PAIR), bf16)
+    edge[1, HALO:, :] = jnp.zeros((edge_rows - HALO, 2 * PAIR), bf16)
+    started = [pltpu.make_async_copy(acc_query, grad_query, sem)]
+    for which, acc in enumerate((acc_key, acc_value)):
+        columns = pl.ds(which * PAIR, PAIR)
+        edge[0, edge_rows - HALO :, which * PAIR : (which + 1) * PAIR] = acc[LEAD - HALO : LEAD, :].astype(bf16)
+        edge[1, :HALO, which * PAIR : (which + 1) * PAIR] = acc[LEAD + own : LEAD + own + HALO, :].astype(bf16)
+        started.append(pltpu.make_async_copy(acc.at[pl.ds(LEAD, own)], grad_pairs.at[:, columns], sem))
+    started.append(pltpu.make_async_copy(edge.at[0], grad_before, sem))
+    started.append(pltpu.make_async_copy(edge.at[1], grad_after, sem))
     for copy in started:
         copy.start()
     for copy in started:
@@ -455,78 +386,71 @@
     )(info, bounds, qkv, before, after)
 
 
-def attend_back(info, bounds, qkv, before, after, mixed, grad_mixed, stats):
-    micro_count, blocks, rows, _ = qkv.shape
+def attend_back(m, info, bounds, qkv, before, after, mixed, grad_mixed, stats):
+    _, blocks, rows, _ = qkv.shape
     own = blocks * rows
     span = LEAD + own + LEAD
-    stat_rows = micro_count * 2 * blocks
+    edge_rows = -(-HALO // rows) * rows
     return pl.pallas_call(
-        attend_back_kernel,
+        functools.partial(attend_back_kernel, m),
         grid_spec=pltpu.PrefetchScalarGridSpec(
             num_scalar_prefetch=2,
             grid=(1,),
-            in_specs=any_specs(5) + [pl.BlockSpec((stat_rows, TILE), lambda g, a, b: (0, 0))],
+            in_specs=any_specs(4 + blocks) + [pl.BlockSpec(stats.shape, lambda g, a, b: (0, 0))],
             out_specs=any_specs(4),
             scratch_shapes=[
-                pltpu.VMEM((micro_count, own, PAIR), bf16),
-                pltpu.VMEM((micro_count, span, PAIR), bf16),
-                pltpu.VMEM((micro_count, span, PAIR), bf16),
-                pltpu.VMEM((micro_count, own, PAIR), bf16),
-                pltpu.VMEM((micro_count, own, PAIR), bf16),
+                pltpu.VMEM((1, own, PAIR), bf16),
+                pltpu.VMEM((1, span, PAIR), bf16),
+                pltpu.VMEM((1, span, PAIR), bf16),
+                pltpu.VMEM((own, PAIR), bf16),
+                pltpu.VMEM((own, PAIR), bf16),
                 pltpu.VMEM((WINDOW, 2 * PAIR), bf16),
                 pltpu.VMEM((2, HEAD_DIM, WINDOW), bf16),
-                pltpu.VMEM((micro_count, own, PAIR), f32),
-                pltpu.VMEM((micro_count, span, PAIR), f32),
-                pltpu.VMEM((micro_count, span, PAIR), f32),
-                pltpu.VMEM((2, micro_count, HALO, 2 * PAIR), bf16),
+                pltpu.VMEM((own, PAIR), f32),
+                pltpu.VMEM((span, PAIR), f32),
+                pltpu.VMEM((span, PAIR), f32),
+                pltpu.VMEM((2, edge_rows, 2 * PAIR), bf16),
                 pltpu.SemaphoreType.DMA,
             ],
         ),
         out_shape=[
-            jax.ShapeDtypeStruct((micro_count, own, PAIR), f32),
-            jax.ShapeDtypeStruct((micro_count, own, 2 * PAIR), f32),
-            jax.ShapeDtypeStruct((micro_count, HALO, 2 * PAIR), bf16),
-            jax.ShapeDtypeStruct((micro_count, HALO, 2 * PAIR), bf16),
+            jax.ShapeDtypeStruct((own, PAIR), f32),
+            jax.ShapeDtypeStruct((own, 2 * PAIR), f32),
+            jax.ShapeDtypeStruct((edge_rows, 2 * PAIR), bf16),
+            jax.ShapeDtypeStruct((edge_rows, 2 * PAIR), bf16),
         ],
-    )(info, bounds, qkv, before, after, mixed, grad_mixed, stats)
-
-
-def join_kernel(first_blocks, last_blocks, blocks, info, query, pairs, head, tail, joined):
-    tile = pl.program_id(1)
-    total = pairs[0]
-    total = total + jnp.where(tile < first_blocks, head[0].astype(f32), 0.0)
-    total = total + jnp.where(tile >= blocks - last_blocks, tail[0].astype(f32), 0.0)
-    joined[0, 0, :, :PAIR] = query[0].astype(bf16)
-    joined[0, 0, :, PAIR:] = total.astype(bf16)
+    )(info, bounds, qkv, before, after, mixed, *grad_mixed, stats)
+
+
+def join_kernel(info, query, pairs, head, tail, joined):
+    blocks, rows, _ = joined.shape
+    edge_blocks = head.shape[0] // rows
+    for tile in range(blocks):
+        here = pl.ds(tile * rows, rows)
+        total = pairs[here, :]
+        if tile < edge_blocks:
+            total = total + head[here, :].astype(f32)
+        if tile >= blocks - edge_blocks:
+            total = total + tail[pl.ds((tile - (blocks - edge_blocks)) * rows, rows), :].astype(f32)
+        target = jnp.bitwise_xor(info[1], tile)
+        joined[target, :, :PAIR] = query[here, :].astype(bf16)
+        joined[target, :, PAIR:] = total.astype(bf16)
 
 
 def join_grads(info, grad_query, grad_pairs, head, tail, rows):
-    micro_count, own, _ = grad_query.shape
+    own = grad_query.shape[0]
     blocks = own // rows
-    edge_blocks = -(-HALO // rows)
-    spare = edge_blocks * rows - HALO
-    head = jnp.pad(head, ((0, 0), (0, spare), (0, 0)))
-    tail = jnp.pad(tail, ((0, 0), (spare, 0), (0, 0)))
+    ins = (grad_query, grad_pairs, head, tail)
     return pl.pallas_call(
-        functools.partial(join_kernel, edge_blocks, edge_blocks, blocks),
+        join_kernel,
         grid_spec=pltpu.PrefetchScalarGridSpec(
             num_scalar_prefetch=1,
-            grid=(micro_count, blocks),
-            in_specs=[
-                pl.BlockSpec((1, rows, PAIR), lambda m, t, i: (m, t, 0)),
-                pl.BlockSpec((1, rows, 2 * PAIR), lambda m, t, i: (m, t, 0)),
-                pl.BlockSpec((1, rows, 2 * PAIR), lambda m, t, i: (m, jnp.minimum(t, edge_blocks - 1), 0)),
-                pl.BlockSpec(
-                    (1, rows, 2 * PAIR),
-                    lambda m, t, i: (m, jnp.maximum(t - (blocks - edge_blocks), 0), 0),
-                ),
-            ],
-            out_specs=pl.BlockSpec(
-                (1, 1, rows, 3 * PAIR), lambda m, t, i: (m, jnp.bitwise_xor(t, i[1]), 0, 0)
-            ),
+            grid=(1,),
+            in_specs=[pl.BlockSpec(item.shape, lambda g, i: (0, 0)) for item in ins],
+            out_specs=pl.BlockSpec((blocks, rows, 3 * PAIR), lambda g, i: (0, 0, 0)),
         ),
-        out_shape=jax.ShapeDtypeStruct((micro_count, blocks, rows, 3 * PAIR), bf16),
-    )(info, grad_query, grad_pairs, head, tail)
+        out_shape=jax.ShapeDtypeStruct((blocks, rows, 3 * PAIR), bf16),
+    )(info, *ins)
 
 
 def layer_norm_parts(values, gain, shift):
@@ -602,8 +526,16 @@
     while bit < n:
         depth_bits.append(bit)
         bit *= 2
-    order_a = depth_bits + [2, 4, 1]
-    order_b = depth_bits + [4, 2, 1]
+
+    wide_parts = fc1_weight.shape[1] // model_width
+    shards = [out_weight]
+    shards += [fc1_weight[:, k * model_width : (k + 1) * model_width] for k in range(wide_parts)]
+    every = lax.all_gather(jnp.concatenate(shards + [fc2_weight], axis=0), "seq")
+    step = out_weight.shape[0]
+    out_full = every[:, :step].reshape(model_width, model_width)
+    up_full = every[:, step : (1 + wide_parts) * step].reshape(n, wide_parts, step, model_width)
+    up_full = up_full.transpose(0, 2, 1, 3).reshape(model_width, wide_parts * model_width)
+    down_full = every[:, (1 + wide_parts) * step :].reshape(wide_parts * model_width, model_width)
 
     small = [ln1_gain, ln1_bias, q_bias, v_bias, out_bias, ln2_gain, ln2_bias, fc2_bias, fc1_bias]
     shard_rows = qkv_weight.shape[0]
@@ -673,10 +605,6 @@
         part = mixed_pair[r] if r == 0 else swap(mixed_pair[r], r)
         mixed_low = lax.dynamic_update_slice(mixed_low, part.reshape(own_tokens, PAIR), (0, column(r)))
 
-    out_full = gathered_weight(info, out_weight, [order_a])
-    up_full = gathered_weight(info, fc1_weight, [order_a, order_b])
-    down_full = gathered_weight(info, fc2_weight, [order_a, order_b])
-
     stream = tokens.reshape(own_tokens, model_width).astype(f32)
     cotangent_low = cotangent.reshape(own_tokens, model_width)
     middle = stream + product(mixed_low, out_full) + out_shift
@@ -685,50 +613,81 @@
     hidden = product(normed_two_low, up_full) + up_shift
     gate = jax.nn.sigmoid(1.702 * hidden)
     active_low = (hidden * gate).astype(bf16)
-    result = middle + product(active_low, down_full) + down_shift
-
     grad_active = product_nt(cotangent_low, down_full)
     grad_hidden_low = (grad_active * (gate + 1.702 * hidden * gate * (1.0 - gate))).astype(bf16)
+
+    order_a = [1, 2, 4] + depth_bits[::-1]
+    order_b = [1, 4, 2] + depth_bits[::-1]
+    grad_down = product_tn(active_low, cotangent_low).astype(bf16).reshape(n, -1, model_width)
+    half = grad_down.shape[1] // 2
+    down = [Scatter(me, grad_down[:, :half], order_a), Scatter(me, grad_down[:, half:], order_b)]
+    for part in down:
+        part.swap()
+    grad_hidden_low = tie(grad_hidden_low, *[part.send for part in down])
+
     grad_normed_two = product_nt(grad_hidden_low, up_full)
     grad_middle = cotangent_low.astype(f32) + layer_norm_back(
         grad_normed_two, normal_two, inverse_two, gain_two
     )
     grad_branch_low = grad_middle.astype(bf16)
     grad_mixed_low = product_nt(grad_branch_low, out_full).astype(bf16)
-
-    back_order_a = [1, 2, 4] + depth_bits[::-1]
-    back_order_b = [1, 4, 2] + depth_bits[::-1]
     grad_parts = []
     for r in range(PLANE):
         part = lax.dynamic_slice(grad_mixed_low, (0, column(r)), (own_tokens, PAIR))
         part = part.reshape(micro_count, tok_dev, PAIR)
         grad_parts.append(part if r == 0 else swap(part, r))
-    grad_mixed_pair = jnp.stack(grad_parts)
-
-    grad_down = product_tn(active_low, cotangent_low).astype(bf16)
-    down_sum = scattered_sum(info, grad_down, [back_order_a, back_order_b])
-    grad_up = product_tn(normed_two_low, grad_hidden_low).astype(bf16)
-    up_sum = scattered_sum(info, grad_up, [back_order_a, back_order_b])
-    grad_out_weight = product_tn(mixed_low, grad_branch_low).astype(bf16)
-    out_sum = scattered_sum(info, grad_out_weight, [back_order_a])
-
-    grad_query, grad_pairs, grad_before, grad_after = attend_back(
-        info, bounds, qkv, before, after, mixed_pair, grad_mixed_pair, stats
-    )
-    from_next = shift_plane(grad_before, -1)
-    from_last = shift_plane(grad_after, 1)
-    grad_joined = join_grads(info, grad_query, grad_pairs, from_last, from_next, tok_dev)
-    grad_flat = grad_joined.reshape(micro_count * plane_rows, 3 * PAIR)
-
-    grad_plane = product_nt(grad_flat, pair_weight).reshape(micro_count, PLANE, tok_dev, model_width)
-    grad_normed = jnp.stack(
-        [
-            plane_scatter(grad_plane[m], [1, 2, 4] if m % 2 == 0 else [1, 4, 2])
-            for m in range(micro_count)
-        ]
-    ).reshape(own_tokens, model_width)
+
+    for part in down:
+        part.advance(grad_branch_low)
+
+    later = tie(normed_two_low, grad_mixed_low)
+    grad_up = product_tn(later, grad_hidden_low).astype(bf16).reshape(n, step, -1)
+    up = [Scatter(me, grad_up[:, : step // 2], order_a), Scatter(me, grad_up[:, step // 2 :], order_b)]
+    for part in up:
+        part.swap()
+    grad_out_weight = product_tn(mixed_low, grad_branch_low).astype(bf16).reshape(n, step, model_width)
+    out_part = Scatter(me, grad_out_weight, order_b)
+    out_part.swap()
+    result = middle + product(tie(active_low, grad_mixed_low), down_full) + down_shift
+    result_low = result.astype(bf16)
+    moving = up + [out_part]
+    for part in moving:
+        part.advance()
+
+    grad_flat = []
+    before_back = [part.send for part in moving] + [result_low]
+    for m in range(micro_count):
+        own_grad = tie(grad_parts[0], *before_back)
+        grad_query, grad_pairs, grad_before, grad_after = attend_back(
+            m, info, bounds, qkv, before, after, mixed_pair, [own_grad] + grad_parts[1:], stats
+        )
+        from_next = shift_plane(grad_before, -1)
+        from_last = shift_plane(grad_after, 1)
+        if m == 0:
+            for part in down:
+                part.advance(grad_before)
+            before_back = [part.send for part in down]
+        joined = join_grads(info, grad_query, grad_pairs, from_last, from_next, tok_dev)
+        grad_flat.append(joined.reshape(plane_rows, 3 * PAIR))
+        last_grad = grad_before
+
+    for part in moving + down:
+        part.advance(last_grad)
+
+    grad_normed = []
+    for m in range(micro_count):
+        grad_plane = product_nt(grad_flat[m], pair_weight).reshape(PLANE, tok_dev, model_width)
+        grad_normed.append(plane_scatter(grad_plane, [1, 2, 4] if m % 2 == 0 else [1, 4, 2]))
+    grad_normed = jnp.concatenate(grad_normed, axis=0)
+    for part in moving + down:
+        while part.order:
+            part.advance()
+    down_sum = jnp.concatenate([part.total() for part in down], axis=0)
+    up_sum = jnp.concatenate([part.total() for part in up], axis=0)
+    out_sum = out_part.total()
     _, normal_one, inverse_one = layer_norm_parts(stream, gain_one, shift_one)
     grad_stream = grad_middle + layer_norm_back(grad_normed, normal_one, inverse_one, gain_one)
+    grad_flat = jnp.concatenate(grad_flat, axis=0)
 
     grad_pair_weight = product_tn(normed_low, grad_flat)
     column_sum = jnp.sum(grad_flat.astype(f32), axis=0)
@@ -779,7 +738,7 @@
         offset += item.shape[0]
 
     return (
-        result.astype(bf16).reshape(micro_count, tok_dev, model_width),
+        result_low.reshape(micro_count, tok_dev, model_width),
         grad_stream.astype(bf16).reshape(micro_count, tok_dev, model_width),
         sums[0],
         sums[1],

time: 821 us -> 749 us (0.912)
  Pallas kernels: 156 us -> 85.3 us
  waiting for transfers between devices: 334 us -> 276 us
  other arithmetic: 62.5 us -> 100 us
  local copies, waits for them, and re-layouts: 86.4 us -> 105 us
  between operations: 2.71 us -> 16 us
  matrix products: 82.1 us -> 71.9 us
    pallas_call x8 -> x4, Pallas kernels: 117 us -> 46 us  [the longest x2 37.8 us: attend_back(): pl.pallas_call(functools.partial(attend_back_kernel, m), grid_spec=pltpu....]
    ppermute x94 -> x69, waiting for transfers between devices: 311 us -> 258 us  [swap(): return lax.ppermute(block, 'seq', [(i, i ^ bit) for i in range(n)])]
    convert_element_type x20 -> x25, other arithmetic: 15.5 us -> 40 us  [the longest x24 39.6 us: half(): (part.astype(f32) + pick(self.got, axis, index).astype(f32)).astype(bf16)]
    slice x0 -> x4, local copies, waits for them, and re-layouts: none -> 14.2 us  [the longest x1 10.3 us: body(): every[:, (1 + wide_parts) * step:]]
    unnamed x212 -> x214, local copies, waits for them, and re-layouts: 41.2 us -> 51.2 us
    dot_general x4, matrix products: 30.7 us -> 20.7 us  [product_tn(): lax.dot_general(left, right, (((0,), (0,)), ((), ())), preferred_element_...]
    concatenate x19 -> x4, other arithmetic: 15.6 us -> 5.62 us  [gather_bits(): current = jnp.concatenate([current, swap(current, bit)], axis=0)]
    convert_element_type x1 -> x2, other arithmetic: 3.39 us -> 12.9 us  [body(): normed_low = normed.astype(bf16)]
  transfers between devices with their start and end apart: 98 -> 76, of which waited for: 45 -> 31; matrix products, arithmetic and copies ran while one was open for 22% -> 27% of each run, Pallas kernels for 15% -> 12%
where the time goes in v2:
time: 749 us; the launch traced here: 739 us
  waiting for transfers between devices  276 us (37%)
  local copies, waits for them, and re-layouts  105 us (14%)
  other arithmetic  100 us (13%)
  Pallas kernels  85.3 us (11%)
  starting transfers between devices  84.9 us (11%)
  matrix products  71.9 us (10%)
  between operations  16 us (2%)
    ppermute x69, waiting for transfers between devices, swap(): return lax.ppermute(block, 'seq', [(i, i ^ bit) for i in range(n)])  258 us
    ppermute x69, starting transfers between devices, swap(): return lax.ppermute(block, 'seq', [(i, i ^ bit) for i in range(n)])  64.2 us
    unnamed x214, local copies, waits for them, and re-layouts  51.2 us
    convert_element_type x24, other arithmetic, half(): (part.astype(f32) + pick(self.got, axis, index).astype(f32)).astype(bf16)  39.6 us
    pallas_call x2, Pallas kernels, attend_back(): pl.pallas_call(functools.partial(attend_back_kernel, m), grid_spec=pltpu....  37.8 us
    pallas_call x1, Pallas kernels, attend(): pl.pallas_call(attend_kernel, grid_spec=pltpu.PrefetchScalarGridSpec(num_...  33.3 us
    dot_general x5, matrix products, product_nt(): lax.dot_general(left, right, (((1,), (1,)), ((), ())), preferred_element_...  28.1 us
    dot_general x4, matrix products, product(): return jnp.dot(left, right, preferred_element_type=f32)  23 us
  transfers between devices with their start and end apart: 76, of which 31 were waited for; matrix products, arithmetic and copies ran while one was open for 27% of the time, Pallas kernels for 12%

profile of v2, /device:TPU:0, one launch (start us, length us, event | category | flops | bytes accessed | tf_op | source)
XLA Modules:
  0.0 738.8 jit_solution(6566468321773389418)
XLA Ops:
  21.1 12.4 %collective-permute-done.3 = bf16[1,256,1024]{2,1,0:T(8,128)(2,1)S(1)} collective-permute-done((bf16[1,256,1024]{2,1,0:T(8,128)(2,1)S(1)}, bf16[1,256,1024]{2,1,0:T(8,128)(2,1)S(1)}, u32[]{:S(2)}, u32[]{:S(2)}) %collective-permute-start.3) | collective-permute-done | bytes 524320 | tf_op jit(solution)/shard_map/ppermute | solution.py:39
  41.5 42.1 %collective-permute-done = bf16[1,256,1024]{2,1,0:T(8,128)(2,1)S(1)} collective-permute-done((bf16[1,256,1024]{2,1,0:T(8,128)(2,1)S(1)}, bf16[1,256,1024]{2,1,0:T(8,128)(2,1)S(1)}, u32[]{:S(2)}, u32[]{:S(2)}) %collective-permute-start) | collective-permute-done | bytes 524320 | tf_op jit(solution)/shard_map/ppermute | solution.py:39
  94.1 28.6 %collective-permute-done.1 = bf16[2,256,1024]{2,1,0:T(8,128)(2,1)} collective-permute-done((bf16[2,256,1024]{2,1,0:T(8,128)(2,1)}, bf16[2,256,1024]{2,1,0:T(8,128)(2,1)}, u32[]{:S(2)}, u32[]{:S(2)}) %collective-permute-start.1) | collective-permute-done | bytes 1048608 | tf_op jit(solution)/shard_map/ppermute | solution.py:39
  131.4 43.1 %collective-permute-done.14 = bf16[16,40,384]{2,1,0:T(8,128)(2,1)S(1)} collective-permute-done((bf16[16,40,384]{2,1,0:T(8,128)(2,1)S(1)}, bf16[16,40,384]{2,1,0:T(8,128)(2,1)S(1)}, u32[]{:S(2)}, u32[]{:S(2)}) %collective-permute-start.14) | collective-permute-done | bytes 491552 | tf_op jit(solution)/shard_map/ppermute | solution.py:39
  207.4 4.8 add_convert_fusion.1
  224.0 6.6 collective-permute-done.15.before
  230.6 5.0 collective-permute-done.16.after
  236.4 33.3 %shard_map.272 = (bf16[8,2,256,128]{3,2,1,0:T(8,128)(2,1)}, f32[32,256]{1,0:T(8,128)}) custom-call(s32[3]{0:T(128)} %pad_add_fusion.info, s32[2,16]{1,0:T(2,128)} %concatenate.64.bounds, bf16[2,8,256,384]{3,2,1,0:T(8,128)(2,1)} %bitcast.518, bf16[2,576,256]{2,1,0:T(8,128)(2,1)} %copy-done.12, bf16[2,576,256]{2,1,0:T(8,128)(2,1)} %copy-done.13), custom_call_target="tpu_custom_call" | custom-call | tf_op jit(solution)/shard_map/pallas_call | solution.py:364
  271.2 9.5 %fusion.3 = bf16[4096,1024]{1,0:T(8,128)(2,1)} fusion(f32[1024]{0:T(1024)S(1)} %add.644, f32[1024]{0:T(1024)S(1)} %mul.222, f32[4096]{0:T(1024)S(1)} %bitcast.592, f32[4096]{0:T(1024)S(1)} %bitcast.593, bf16[1,8,256,1024]{3,2,1,0:T(8,128)(2,1)} %bitcast.513, bf16[1,8,256,1024]{3,2,1,0:T(8,128)(2,1)} %bitcast.512), kind=kLoop, calls=%fused_computation.4 | loop fusion | flops 29360128 | bytes 16818176 | tf_op jit(solution)/shard_map/convert_element_type | solution.py:578
  289.0 7.6 %collective-permute-done.21 = bf16[2,256,128]{2,1,0:T(8,128)(2,1)S(1)} collective-permute-done((bf16[2,256,128]{2,1,0:T(8,128)(2,1)S(1)}, bf16[2,256,128]{2,1,0:T(8,128)(2,1)S(1)}, u32[]{:S(2)}, u32[]{:S(2)}) %collective-permute-start.21) | collective-permute-done | bytes 131104 | tf_op jit(solution)/shard_map/ppermute | solution.py:39
  299.0 10.3 %fusion.107 = (bf16[32,128,1024]{2,1,0:T(8,128)(2,1)}, bf16[32,128,1024]{2,1,0:T(8,128)(2,1)S(1)}) fusion(bf16[32,288,1024]{2,1,0:T(8,128)(2,1)} %bitcast.524), kind=kLoop, calls=%fused_computation.399 | loop fusion | bytes 33554432 | tf_op jit(solution)/shard_map/slice | solution.py:538
  311.0 7.9 %copy.59 = bf16[32,32,4,1024]{3,2,1,0:T(4,128)(2,1)} copy(bf16[32,32,4,1024]{3,1,2,0:T(8,128)(2,1)S(1)} %bitcast.522) | data formatting | bytes 16777216 | tf_op jit(solution)/shard_map/transpose | solution.py:537
  318.9 12.3 %copy.94 = bf16[128,8,4,1024]{3,1,2,0:T(8,128)(2,1)} copy(bf16[128,8,4,1024]{3,2,1,0:T(4,128)(2,1)} %bitcast.521) | data formatting | bytes 16777216
  331.6 11.3 %multiply_convert_fusion = (bf16[512,4096]{1,0:T(8,128)(2,1)S(1)}, f32[512,4096]{1,0:T(8,128)}) fusion(f32[4096]{0:T(1024)S(1)} %slice_bitcast_fusion.32, bf16[512,1024]{1,0:T(8,128)(2,1)S(1)} %add_convert_fusion.3, bf16[1024,4096]{1,0:T(8,128)(2,1)} %bitcast.535), kind=kOutput, calls=%fused_computation.11 | convolution fusion | flops 4309647360 | bytes 22036480 | tf_op jit(solution)/shard_map/dot_general | solution.py:26
  342.9 4.8 convolution_convert_fusion.1
  354.6 11.6 %fusion.4 = bf16[512,4096]{1,0:T(8,128)(2,1)S(1)} fusion(f32[512,4096]{1,0:T(8,128)} %get-tuple-element.215, bf16[4096,1024]{1,0:T(8,128)(2,1)} %bitcast.543, bf16[512,1024]{1,0:T(8,128)(2,1)S(1)} %bitcast.554, f32[4096]{0:T(1024)S(1)} %slice_bitcast_fusion.32), kind=kOutput, calls=%fused_computation.10 | convolution fusion | flops 4318035968 | bytes 22036480 | tf_op jit(solution)/shard_map/dot_general | solution.py:34
  366.3 6.3 multiply_reduce_fusion.1
  380.1 4.8 convolution_convert_fusion
  392.2 5.5 add_convert_fusion.2
  442.0 18.8 %shard_map.273 = (f32[2048,128]{1,0:T(8,128)}, f32[2048,256]{1,0:T(8,128)}, bf16[768,256]{1,0:T(8,128)(2,1)}, bf16[768,256]{1,0:T(8,128)(2,1)}) custom-call(s32[3]{0:T(128)} %pad_add_fusion.info, s32[2,16]{1,0:T(2,128)} %concatenate.64.bounds, bf16[2,8,256,384]{3,2,1,0:T(8,128)(2,1)} %bitcast.519, bf16[2,576,256]{2,1,0:T(8,128)(2,1)} %copy-done.12, ...), custom_call_target="tpu_custom_call" | custom-call | tf_op jit(solution)/shard_map/pallas_call | solution.py:394
  460.8 9.1 %collective-permute-start.34 = (bf16[768,256]{1,0:T(8,128)(2,1)}, bf16[768,256]{1,0:T(8,128)(2,1)}, u32[]{:S(2)}, u32[]{:S(2)}) collective-permute-start(bf16[768,256]{1,0:T(8,128)(2,1)} %get-tuple-element.47), channel_id=1, source_target_pairs={{0,8},{1,9},{2,10},{3,11},{4,12},{5,13},{6,14},{7,15},{8,16},{9,17... | collective-permute-start | bytes 1179656 | tf_op jit(solution)/shard_map/ppermute | solution.py:45
  499.5 19.0 %shard_map.275 = (f32[2048,128]{1,0:T(8,128)}, f32[2048,256]{1,0:T(8,128)}, bf16[768,256]{1,0:T(8,128)(2,1)}, bf16[768,256]{1,0:T(8,128)(2,1)}) custom-call(s32[3]{0:T(128)} %pad_add_fusion.info, s32[2,16]{1,0:T(2,128)} %concatenate.64.bounds, bf16[2,8,256,384]{3,2,1,0:T(8,128)(2,1)} %bitcast.520, bf16[2,576,256]{2,1,0:T(8,128)(2,1)} %copy-done.12, ...), custom_call_target="tpu_custom_call" | custom-call | tf_op jit(solution)/shard_map/pallas_call | solution.py:394
  518.5 4.3 collective-permute-start.43
  540.6 4.2 shard_map.276
  552.0 8.5 %fusion.110 = (bf16[1024,384]{1,0:T(8,128)(2,1)}, f32[1024]{0:T(1024)S(1)}) fusion(bf16[32,32,384]{2,1,0:T(8,128)(2,1)S(1)} %copy-done.41, bf16[4096,1024]{1,0:T(8,128)(2,1)} %fusion.3, bf16[2048,384]{1,0:T(8,128)(2,1)S(1)} %bitcast.552, bf16[2048,384]{1,0:T(8,128)(2,1)S(1)} %bitcast.549), kind=kOutput, calls=%fused_computation.402 | convolution fusion | flops 3229088768 | bytes 13111296 | tf_op jit(solution)/shard_map/dot_general | solution.py:30
  579.4 4.7 collective-permute-done.69
  586.2 19.5 %collective-permute-done.67 = bf16[2,16,4096]{2,1,0:T(8,128)(2,1)S(1)} collective-permute-done((bf16[2,16,4096]{2,1,0:T(8,128)(2,1)S(1)}, bf16[2,16,4096]{2,1,0:T(8,128)(2,1)S(1)}, u32[]{:S(2)}, u32[]{:S(2)}) %collective-permute-start.67) | collective-permute-done | bytes 262176 | tf_op jit(solution)/shard_map/ppermute | solution.py:39
  605.8 21.7 %collective-permute-done.63 = bf16[2,16,4096]{2,1,0:T(8,128)(2,1)S(1)} collective-permute-done((bf16[2,16,4096]{2,1,0:T(8,128)(2,1)S(1)}, bf16[2,16,4096]{2,1,0:T(8,128)(2,1)S(1)}, u32[]{:S(2)}, u32[]{:S(2)}) %collective-permute-start.63) | collective-permute-done | bytes 262176 | tf_op jit(solution)/shard_map/ppermute | solution.py:39
  627.6 11.2 %collective-permute-done.73 = bf16[2,64,1024]{2,1,0:T(8,128)(2,1)S(1)} collective-permute-done((bf16[2,64,1024]{2,1,0:T(8,128)(2,1)S(1)}, bf16[2,64,1024]{2,1,0:T(8,128)(2,1)S(1)}, u32[]{:S(2)}, u32[]{:S(2)}) %collective-permute-start.73) | collective-permute-done | bytes 262176 | tf_op jit(solution)/shard_map/ppermute | solution.py:39
  638.8 5.2 collective-permute-done.70
  688.4 19.0 %collective-permute-done.37 = bf16[2,256,1024]{2,1,0:T(8,128)(2,1)S(1)} collective-permute-done((bf16[2,256,1024]{2,1,0:T(8,128)(2,1)S(1)}, bf16[2,256,1024]{2,1,0:T(8,128)(2,1)S(1)}, u32[]{:S(2)}, u32[]{:S(2)}) %collective-permute-start.37) | collective-permute-done | bytes 1048608 | tf_op jit(solution)/shard_map/ppermute | solution.py:39
  715.0 8.4 %collective-permute-done.38 = bf16[1,256,1024]{2,1,0:T(8,128)(2,1)S(1)} collective-permute-done((bf16[1,256,1024]{2,1,0:T(8,128)(2,1)}, bf16[1,256,1024]{2,1,0:T(8,128)(2,1)S(1)}, u32[]{:S(2)}, u32[]{:S(2)}) %collective-permute-start.38) | collective-permute-done | bytes 524320 | tf_op jit(solution)/shard_map/ppermute | solution.py:39
  (545 shorter events, 301.4 us)
Async XLA Ops:
  7.2 289.6 %all-gather.3.cloned.1.call-start = ((), (), s32[]{:S(2)}) async-start(), calls=%async_computation | async-start | bytes 19464192 | tf_op jit(solution)/shard_map/all_gather | solution.py:533
  20.9 63.9 %collective-permute-start.9 = (bf16[40,384]{1,0:T(8,128)(2,1)S(1)}, bf16[40,384]{1,0:T(8,128)(2,1)S(1)}, u32[]{:S(2)}, u32[]{:S(2)}) collective-permute-start(bf16[40,384]{1,0:T(8,128)(2,1)S(1)} %get-tuple-element.167), channel_id=1, source_target_pairs={{0,4},{1,5},{2,6},{3,7},{4,0},{5,1},{6,2},{7,3},{8,12},{9,13},{10,... | collective-permute-start | bytes 92168 | tf_op jit(solution)/shard_map/ppermute | solution.py:39
  33.6 54.3 %collective-permute-start.4 = (bf16[2,256,1024]{2,1,0:T(8,128)(2,1)S(1)}, bf16[2,256,1024]{2,1,0:T(8,128)(2,1)S(1)}, u32[]{:S(2)}, u32[]{:S(2)}) collective-permute-start(bf16[2,256,1024]{2,1,0:T(8,128)(2,1)S(1)} %pad_maximum_fusion.9), channel_id=1, source_target_pairs={{0,2},{1,3},{2,0},{3,1},{4,6},{5,7},{6,4},{7,5},{8,10},{9,11},{10,... | collective-permute-start | bytes 3145736 | tf_op jit(solution)/shard_map/ppermute | solution.py:39
  35.7 48.0 %collective-permute-start = (bf16[1,256,1024]{2,1,0:T(8,128)(2,1)S(1)}, bf16[1,256,1024]{2,1,0:T(8,128)(2,1)S(1)}, u32[]{:S(2)}, u32[]{:S(2)}) collective-permute-start(bf16[1,256,1024]{2,1,0:T(8,128)(2,1)S(1)} %get-tuple-element.138), channel_id=1, source_target_pairs={{0,2},{1,3},{2,0},{3,1},{4,6},{5,7},{6,4},{7,5},{8,10},{9,11},{10,... | collective-permute-start | bytes 1572872 | tf_op jit(solution)/shard_map/ppermute | solution.py:39
  37.0 53.5 %collective-permute-start.10 = (bf16[40,384]{1,0:T(8,128)(2,1)S(1)}, bf16[40,384]{1,0:T(8,128)(2,1)S(1)}, u32[]{:S(2)}, u32[]{:S(2)}) collective-permute-start(bf16[40,384]{1,0:T(8,128)(2,1)S(1)} %get-tuple-element.168), channel_id=1, source_target_pairs={{0,5},{1,4},{2,7},{3,6},{4,1},{5,0},{6,3},{7,2},{8,13},{9,12},{10,... | collective-permute-start | bytes 92168 | tf_op jit(solution)/shard_map/ppermute | solution.py:39
  37.6 53.5 %collective-permute-start.11 = (bf16[40,384]{1,0:T(8,128)(2,1)S(1)}, bf16[40,384]{1,0:T(8,128)(2,1)S(1)}, u32[]{:S(2)}, u32[]{:S(2)}) collective-permute-start(bf16[40,384]{1,0:T(8,128)(2,1)S(1)} %get-tuple-element.170), channel_id=1, source_target_pairs={{0,6},{1,7},{2,4},{3,5},{4,2},{5,3},{6,0},{7,1},{8,14},{9,15},{10,... | collective-permute-start | bytes 92168 | tf_op jit(solution)/shard_map/ppermute | solution.py:39
  84.7 37.9 %collective-permute-start.1 = (bf16[2,256,1024]{2,1,0:T(8,128)(2,1)}, bf16[2,256,1024]{2,1,0:T(8,128)(2,1)}, u32[]{:S(2)}, u32[]{:S(2)}) collective-permute-start(bf16[2,256,1024]{2,1,0:T(8,128)(2,1)} %pad_maximum_fusion.8), channel_id=1, source_target_pairs={{0,4},{1,5},{2,6},{3,7},{4,0},{5,1},{6,2},{7,3},{8,12},{9,13},{10,... | collective-permute-start | bytes 3145736 | tf_op jit(solution)/shard_map/ppermute | solution.py:39
  89.7 93.2 %collective-permute-start.5 = (bf16[4,256,1024]{2,1,0:T(8,128)(2,1)}, bf16[4,256,1024]{2,1,0:T(8,128)(2,1)}, u32[]{:S(2)}, u32[]{:S(2)}) collective-permute-start(bf16[4,256,1024]{2,1,0:T(8,128)(2,1)} %pad_maximum_fusion.3), channel_id=1, source_target_pairs={{0,1},{1,0},{2,3},{3,2},{4,5},{5,4},{6,7},{7,6},{8,9},{9,8},{10,11... | collective-permute-start | bytes 6291464 | tf_op jit(solution)/shard_map/ppermute | solution.py:39
  92.4 33.9 %collective-permute-start.13 = (bf16[8,40,384]{2,1,0:T(8,128)(2,1)}, bf16[8,40,384]{2,1,0:T(8,128)(2,1)S(1)}, u32[]{:S(2)}, u32[]{:S(2)}) collective-permute-start(bf16[8,40,384]{2,1,0:T(8,128)(2,1)} %get-tuple-element.175), channel_id=1, source_target_pairs={{0,8},{1,9},{2,10},{3,11},{4,12},{5,13},{6,14},{7,15},{8,0},{9,1},... | collective-permute-start | bytes 737288 | tf_op jit(solution)/shard_map/ppermute | solution.py:39
  125.4 63.1 %collective-permute-start.2 = (bf16[4,256,1024]{2,1,0:T(8,128)(2,1)}, bf16[4,256,1024]{2,1,0:T(8,128)(2,1)}, u32[]{:S(2)}, u32[]{:S(2)}) collective-permute-start(bf16[4,256,1024]{2,1,0:T(8,128)(2,1)} %pad_maximum_fusion.2), channel_id=1, source_target_pairs={{0,1},{1,0},{2,3},{3,2},{4,5},{5,4},{6,7},{7,6},{8,9},{9,8},{10,11... | collective-permute-start | bytes 6291464 | tf_op jit(solution)/shard_map/ppermute | solution.py:39
  127.1 47.4 %collective-permute-start.14 = (bf16[16,40,384]{2,1,0:T(8,128)(2,1)S(1)}, bf16[16,40,384]{2,1,0:T(8,128)(2,1)S(1)}, u32[]{:S(2)}, u32[]{:S(2)}) collective-permute-start(bf16[16,40,384]{2,1,0:T(8,128)(2,1)S(1)} %get-tuple-element.161), channel_id=1, source_target_pairs={{0,16},{1,17},{2,18},{3,19},{4,20},{5,21},{6,22},{7,23},{8,24},{9,... | collective-permute-start | bytes 1474568 | tf_op jit(solution)/shard_map/ppermute | solution.py:39
  354.1 77.4 %collective-permute-start.39 = (bf16[2,2,2,2,64,1024]{5,4,1,0,2,3:T(8,128)(2,1)}, bf16[2,2,2,2,64,1024]{5,4,1,0,2,3:T(8,128)(2,1)}, u32[]{:S(2)}, u32[]{:S(2)}) collective-permute-start(bf16[2,2,2,2,64,1024]{5,4,1,0,2,3:T(8,128)(2,1)} %copy_bitcast_fusion.3), channel_id=1, source_target_pairs={{0,1},{1,0},{2,3},{3,2},{4,5},{5,4},{6,7},{7,6},{8,9},{9,8},{10,11... | collective-permute-start | bytes 6291464 | tf_op jit(solution)/shard_map/ppermute | solution.py:39
  354.3 69.8 %collective-permute-start.41 = (bf16[2,2,2,2,64,1024]{5,4,1,3,0,2:T(8,128)(2,1)}, bf16[2,2,2,2,64,1024]{5,4,1,3,0,2:T(8,128)(2,1)}, u32[]{:S(2)}, u32[]{:S(2)}) collective-permute-start(bf16[2,2,2,2,64,1024]{5,4,1,3,0,2:T(8,128)(2,1)} %copy_bitcast_fusion.2), channel_id=1, source_target_pairs={{0,1},{1,0},{2,3},{3,2},{4,5},{5,4},{6,7},{7,6},{8,9},{9,8},{10,11... | collective-permute-start | bytes 6291464 | tf_op jit(solution)/shard_map/ppermute | solution.py:39
  388.4 27.3 %collective-permute-start.24 = (bf16[2,2,2,2,16,4096]{5,4,1,2,0,3:T(8,128)(2,1)}, bf16[2,2,2,2,16,4096]{5,4,1,2,0,3:T(8,128)(2,1)}, u32[]{:S(2)}, u32[]{:S(2)}) collective-permute-start(bf16[2,2,2,2,16,4096]{5,4,1,2,0,3:T(8,128)(2,1)} %copy_bitcast_fusion.1), channel_id=1, source_target_pairs={{0,1},{1,0},{2,3},{3,2},{4,5},{5,4},{6,7},{7,6},{8,9},{9,8},{10,11... | collective-permute-start | bytes 6291464 | tf_op jit(solution)/shard_map/ppermute | solution.py:39
  390.2 28.9 %collective-permute-start.25 = (bf16[2,2,2,2,16,4096]{5,4,1,3,0,2:T(8,128)(2,1)}, bf16[2,2,2,2,16,4096]{5,4,1,3,0,2:T(8,128)(2,1)}, u32[]{:S(2)}, u32[]{:S(2)}) collective-permute-start(bf16[2,2,2,2,16,4096]{5,4,1,3,0,2:T(8,128)(2,1)} %copy_bitcast_fusion), channel_id=1, source_target_pairs={{0,1},{1,0},{2,3},{3,2},{4,5},{5,4},{6,7},{7,6},{8,9},{9,8},{10,11... | collective-permute-start | bytes 6291464 | tf_op jit(solution)/shard_map/ppermute | solution.py:39
  435.4 88.9 %collective-permute-start.65 = (bf16[2,2,2,16,4096]{4,3,1,2,0:T(8,128)(2,1)}, bf16[2,2,2,16,4096]{4,3,1,2,0:T(8,128)(2,1)}, u32[]{:S(2)}, u32[]{:S(2)}) collective-permute-start(bf16[2,2,2,16,4096]{4,3,1,2,0:T(8,128)(2,1)} %get-tuple-element.103), channel_id=1, source_target_pairs={{0,4},{1,5},{2,6},{3,7},{4,0},{5,1},{6,2},{7,3},{8,12},{9,13},{10,... | collective-permute-start | bytes 3145736 | tf_op jit(solution)/shard_map/ppermute | solution.py:39
  436.9 58.0 %collective-permute-start.40 = (bf16[2,2,2,64,1024]{4,3,2,1,0:T(8,128)(2,1)}, bf16[2,2,2,64,1024]{4,3,2,1,0:T(8,128)(2,1)}, u32[]{:S(2)}, u32[]{:S(2)}) collective-permute-start(bf16[2,2,2,64,1024]{4,3,2,1,0:T(8,128)(2,1)} %fusion.9), channel_id=1, source_target_pairs={{0,2},{1,3},{2,0},{3,1},{4,6},{5,7},{6,4},{7,5},{8,10},{9,11},{10,... | collective-permute-start | bytes 3145736 | tf_op jit(solution)/shard_map/ppermute | solution.py:39
  440.7 56.2 %collective-permute-start.42 = (bf16[2,2,2,64,1024]{4,3,1,2,0:T(8,128)(2,1)}, bf16[2,2,2,64,1024]{4,3,1,2,0:T(8,128)(2,1)}, u32[]{:S(2)}, u32[]{:S(2)}) collective-permute-start(bf16[2,2,2,64,1024]{4,3,1,2,0:T(8,128)(2,1)} %get-tuple-element.50), channel_id=1, source_target_pairs={{0,4},{1,5},{2,6},{3,7},{4,0},{5,1},{6,2},{7,3},{8,12},{9,13},{10,... | collective-permute-start | bytes 3145736 | tf_op jit(solution)/shard_map/ppermute | solution.py:39
  478.3 49.5 %collective-permute-start.61 = (bf16[2,2,2,16,4096]{4,3,1,2,0:T(8,128)(2,1)}, bf16[2,2,2,16,4096]{4,3,1,2,0:T(8,128)(2,1)}, u32[]{:S(2)}, u32[]{:S(2)}) collective-permute-start(bf16[2,2,2,16,4096]{4,3,1,2,0:T(8,128)(2,1)} %fusion.12), channel_id=1, source_target_pairs={{0,2},{1,3},{2,0},{3,1},{4,6},{5,7},{6,4},{7,5},{8,10},{9,11},{10,... | collective-permute-start | bytes 3145736 | tf_op jit(solution)/shard_map/ppermute | solution.py:39
  494.9 185.2 %collective-permute-start.36 = (bf16[4,256,1024]{2,1,0:T(8,128)(2,1)}, bf16[4,256,1024]{2,1,0:T(8,128)(2,1)}, u32[]{:S(2)}, u32[]{:S(2)}) collective-permute-start(bf16[4,256,1024]{2,1,0:T(8,128)(2,1)} %pad_maximum_fusion.4), channel_id=1, source_target_pairs={{0,1},{1,0},{2,3},{3,2},{4,5},{5,4},{6,7},{7,6},{8,9},{9,8},{10,11... | collective-permute-start | bytes 6291464 | tf_op jit(solution)/shard_map/ppermute | solution.py:39
  527.8 44.8 %collective-permute-start.66 = (bf16[2,2,16,4096]{3,2,1,0:T(8,128)(2,1)}, bf16[2,2,16,4096]{3,2,1,0:T(8,128)(2,1)}, u32[]{:S(2)}, u32[]{:S(2)}) collective-permute-start(bf16[2,2,16,4096]{3,2,1,0:T(8,128)(2,1)} %get-tuple-element.58), channel_id=1, source_target_pairs={{0,2},{1,3},{2,0},{3,1},{4,6},{5,7},{6,4},{7,5},{8,10},{9,11},{10,... | collective-permute-start | bytes 1572872 | tf_op jit(solution)/shard_map/ppermute | solution.py:39
  535.1 38.7 %collective-permute-start.62 = (bf16[2,2,16,4096]{3,2,1,0:T(8,128)(2,1)}, bf16[2,2,16,4096]{3,2,1,0:T(8,128)(2,1)}, u32[]{:S(2)}, u32[]{:S(2)}) collective-permute-start(bf16[2,2,16,4096]{3,2,1,0:T(8,128)(2,1)} %fusion.43), channel_id=1, source_target_pairs={{0,4},{1,5},{2,6},{3,7},{4,0},{5,1},{6,2},{7,3},{8,12},{9,13},{10,... | collective-permute-start | bytes 1572872 | tf_op jit(solution)/shard_map/ppermute | solution.py:39
  537.3 39.9 %collective-permute-start.72 = (bf16[2,2,64,1024]{3,2,1,0:T(8,128)(2,1)}, bf16[2,2,64,1024]{3,2,1,0:T(8,128)(2,1)}, u32[]{:S(2)}, u32[]{:S(2)}) collective-permute-start(bf16[2,2,64,1024]{3,2,1,0:T(8,128)(2,1)} %get-tuple-element.61), channel_id=1, source_target_pairs={{0,2},{1,3},{2,0},{3,1},{4,6},{5,7},{6,4},{7,5},{8,10},{9,11},{10,... | collective-permute-start | bytes 1572872 | tf_op jit(solution)/shard_map/ppermute | solution.py:39
  538.2 23.9 %collective-permute-start.59 = (bf16[2,32,1024]{2,1,0:T(8,128)(2,1)}, bf16[2,32,1024]{2,1,0:T(8,128)(2,1)S(1)}, u32[]{:S(2)}, u32[]{:S(2)}) collective-permute-start(bf16[2,32,1024]{2,1,0:T(8,128)(2,1)} %get-tuple-element.145), channel_id=1, source_target_pairs={{0,16},{1,17},{2,18},{3,19},{4,20},{5,21},{6,22},{7,23},{8,24},{9,... | collective-permute-start | bytes 393224 | tf_op jit(solution)/shard_map/ppermute | solution.py:39
  572.6 110.7 %collective-permute-start.45 = (bf16[4,256,1024]{2,1,0:T(8,128)(2,1)}, bf16[4,256,1024]{2,1,0:T(8,128)(2,1)}, u32[]{:S(2)}, u32[]{:S(2)}) collective-permute-start(bf16[4,256,1024]{2,1,0:T(8,128)(2,1)} %pad_maximum_fusion.5), channel_id=1, source_target_pairs={{0,1},{1,0},{2,3},{3,2},{4,5},{5,4},{6,7},{7,6},{8,9},{9,8},{10,11... | collective-permute-start | bytes 6291464 | tf_op jit(solution)/shard_map/ppermute | solution.py:39
  573.9 31.9 %collective-permute-start.67 = (bf16[2,16,4096]{2,1,0:T(8,128)(2,1)S(1)}, bf16[2,16,4096]{2,1,0:T(8,128)(2,1)S(1)}, u32[]{:S(2)}, u32[]{:S(2)}) collective-permute-start(bf16[2,16,4096]{2,1,0:T(8,128)(2,1)S(1)} %get-tuple-element.117), channel_id=1, source_target_pairs={{0,16},{1,17},{2,18},{3,19},{4,20},{5,21},{6,22},{7,23},{8,24},{9,... | collective-permute-start | bytes 786440 | tf_op jit(solution)/shard_map/ppermute | solution.py:39
  577.3 66.8 %collective-permute-start.48 = (bf16[16,40,384]{2,1,0:T(8,128)(2,1)S(1)}, bf16[16,40,384]{2,1,0:T(8,128)(2,1)S(1)}, u32[]{:S(2)}, u32[]{:S(2)}) collective-permute-start(bf16[16,40,384]{2,1,0:T(8,128)(2,1)S(1)} %slice.574), channel_id=1, source_target_pairs={{0,16},{1,17},{2,18},{3,19},{4,20},{5,21},{6,22},{7,23},{8,24},{9,... | collective-permute-start | bytes 1474568 | tf_op jit(solution)/shard_map/ppermute | solution.py:39
  584.1 43.4 %collective-permute-start.63 = (bf16[2,16,4096]{2,1,0:T(8,128)(2,1)S(1)}, bf16[2,16,4096]{2,1,0:T(8,128)(2,1)S(1)}, u32[]{:S(2)}, u32[]{:S(2)}) collective-permute-start(bf16[2,16,4096]{2,1,0:T(8,128)(2,1)S(1)} %get-tuple-element.115), channel_id=1, source_target_pairs={{0,16},{1,17},{2,18},{3,19},{4,20},{5,21},{6,22},{7,23},{8,24},{9,... | collective-permute-start | bytes 786440 | tf_op jit(solution)/shard_map/ppermute | solution.py:39
  605.8 33.0 %collective-permute-start.73 = (bf16[2,64,1024]{2,1,0:T(8,128)(2,1)S(1)}, bf16[2,64,1024]{2,1,0:T(8,128)(2,1)S(1)}, u32[]{:S(2)}, u32[]{:S(2)}) collective-permute-start(bf16[2,64,1024]{2,1,0:T(8,128)(2,1)S(1)} %get-tuple-element.62), channel_id=1, source_target_pairs={{0,16},{1,17},{2,18},{3,19},{4,20},{5,21},{6,22},{7,23},{8,24},{9,... | collective-permute-start | bytes 786440 | tf_op jit(solution)/shard_map/ppermute | solution.py:39
  660.5 19.4 %collective-permute-start.56 = (bf16[40,384]{1,0:T(8,128)(2,1)S(1)}, bf16[40,384]{1,0:T(8,128)(2,1)S(1)}, u32[]{:S(2)}, u32[]{:S(2)}) collective-permute-start(bf16[40,384]{1,0:T(8,128)(2,1)S(1)} %get-tuple-element.155), channel_id=1, source_target_pairs={{0,7},{1,6},{2,5},{3,4},{4,3},{5,2},{6,1},{7,0},{8,15},{9,14},{10,... | collective-permute-start | bytes 92168 | tf_op jit(solution)/shard_map/ppermute | solution.py:39
  682.1 25.2 %collective-permute-start.37 = (bf16[2,256,1024]{2,1,0:T(8,128)(2,1)S(1)}, bf16[2,256,1024]{2,1,0:T(8,128)(2,1)S(1)}, u32[]{:S(2)}, u32[]{:S(2)}) collective-permute-start(bf16[2,256,1024]{2,1,0:T(8,128)(2,1)S(1)} %pad_maximum_fusion.10), channel_id=1, source_target_pairs={{0,2},{1,3},{2,0},{3,1},{4,6},{5,7},{6,4},{7,5},{8,10},{9,11},{10,... | collective-permute-start | bytes 3145736 | tf_op jit(solution)/shard_map/ppermute | solution.py:39
  686.3 25.3 %collective-permute-start.46 = (bf16[2,256,1024]{2,1,0:T(8,128)(2,1)}, bf16[2,256,1024]{2,1,0:T(8,128)(2,1)}, u32[]{:S(2)}, u32[]{:S(2)}) collective-permute-start(bf16[2,256,1024]{2,1,0:T(8,128)(2,1)} %pad_maximum_fusion.11), channel_id=1, source_target_pairs={{0,4},{1,5},{2,6},{3,7},{4,0},{5,1},{6,2},{7,3},{8,12},{9,13},{10,... | collective-permute-start | bytes 3145736 | tf_op jit(solution)/shard_map/ppermute | solution.py:39
  (134 other events, 1243.0 us)
Sparse Core Ops, SparseCore 0:
  13.6 166.3 all-gather.2

commit v3 on v2

--- a/solution.py
+++ b/solution.py
@@ -71,42 +71,52 @@
     return lax.dynamic_index_in_dim(block, index, axis, keepdims=False)
 
 
+def exchange(blocks):
+    bits = PLANE.bit_length() - 1
+    cube = blocks.reshape((2,) * bits + blocks.shape[1:])
+    for axis in reversed(range(bits)):
+        got = swap(lax.index_in_dim(cube, 1, axis, keepdims=False), 1 << (bits - 1 - axis))
+        cube = jnp.stack([lax.index_in_dim(cube, 0, axis, keepdims=False), got], axis=axis)
+    return cube.reshape(blocks.shape)
+
+
 class Scatter:
-    def __init__(self, me, partial, order):
-        count = partial.shape[0]
+    def __init__(self, me, partials, order):
+        count = partials[0].shape[0]
         depth = count.bit_length() - 1
         self.me = me
-        self.block = partial.reshape((2,) * depth + partial.shape[1:])
+        self.blocks = [item.reshape((2,) * depth + item.shape[1:]) for item in partials]
         self.bits = [1 << (depth - 1 - axis) for axis in range(depth)]
         self.order = list(order)
         self.got = None
-        self.send = None
         self.split()
 
-    def half(self, index, axis):
-        part = pick(self.block, axis, index)
+    def half(self, axis, index):
         if self.got is None:
-            return part
-        return (part.astype(f32) + pick(self.got, axis, index).astype(f32)).astype(bf16)
+            picked = [pick(block, axis, index) for block in self.blocks]
+            return picked[0] if len(picked) == 1 else jnp.concatenate(picked, axis=-2)
+        kept = pick(self.blocks[0], axis, index).astype(f32)
+        return (kept + pick(self.got, axis, index).astype(f32)).astype(bf16)
 
     def split(self):
-        bit = self.order.pop(0)
-        axis = self.bits.index(bit)
+        self.bit = self.order.pop(0)
+        axis = self.bits.index(self.bit)
         self.bits.pop(axis)
-        mine = own_bit(self.me, bit)
-        self.send, keep = self.half(1 - mine, axis), self.half(mine, axis)
-        self.block, self.got, self.bit = keep, None, bit
-
-    def swap(self, *earlier):
-        send = tie(self.send, *earlier) if earlier else self.send
-        self.got = swap(send, self.bit)
+        mine = own_bit(self.me, self.bit)
+        self.send, keep = self.half(axis, 1 - mine), self.half(axis, mine)
+        self.blocks, self.got = [keep], None
+
+    def swap(self):
+        self.got = swap(self.send, self.bit)
 
     def advance(self, *earlier):
+        if earlier:
+            self.got = tie(self.got, *earlier)
         self.split()
-        self.swap(*earlier)
+        self.swap()
 
     def total(self):
-        return self.block.astype(f32) + self.got.astype(f32)
+        return self.blocks[0].astype(f32) + self.got.astype(f32)
 
 
 def turn_kernel(info, blocks, turned):
@@ -352,6 +362,13 @@
         copy.wait()
 
 
+def cover(rows, passes):
+    scores = 2 * rows * WINDOW
+    return pl.CostEstimate(
+        flops=4 * scores * PAIR, transcendentals=scores, bytes_accessed=passes * scores
+    )
+
+
 def any_specs(count):
     return [pl.BlockSpec(memory_space=pl.ANY)] * count
 
@@ -383,6 +400,7 @@
             jax.ShapeDtypeStruct((blocks, micro_count, rows, PAIR), bf16),
             jax.ShapeDtypeStruct((stat_rows, TILE), f32),
         ],
+        cost_estimate=cover(micro_count * own, 30),
     )(info, bounds, qkv, before, after)
 
 
@@ -419,6 +437,7 @@
             jax.ShapeDtypeStruct((edge_rows, 2 * PAIR), bf16),
             jax.ShapeDtypeStruct((edge_rows, 2 * PAIR), bf16),
         ],
+        cost_estimate=cover(own, 35),
     )(info, bounds, qkv, before, after, mixed, *grad_mixed, stats)
 
 
@@ -466,27 +485,32 @@
     return inverse * (centered - normal * jnp.mean(scaled * normal, axis=-1, keepdims=True))
 
 
-def plane_tokens(block, order):
-    near, far = gather_bits(block, order)
+def plane_tokens(near, far, order):
     held = places(order)
     half = PLANE // 2
     at = {r: (near[p] if p < half else far[p - half]) for p, r in enumerate(held)}
     return jnp.stack([at[r] for r in range(PLANE)])
 
 
-def plane_scatter(partial, order):
-    pieces = {r: partial[r].astype(bf16) for r in range(PLANE)}
-    left = list(range(PLANE))
-    total = None
-    for step, bit in enumerate(order):
-        keep = [r for r in left if not r & bit]
-        got = swap(jnp.stack([pieces[r | bit] for r in keep]), bit)
-        last = step == len(order) - 1
-        for position, r in enumerate(keep):
-            added = pieces[r].astype(f32) + got[position].astype(f32)
-            pieces[r] = added if last else added.astype(bf16)
-        left = keep
-    return pieces[0]
+class PlaneScatter:
+    def __init__(self, partial, order):
+        self.pieces = [partial[r].astype(bf16) for r in range(PLANE)]
+        self.left = list(range(PLANE))
+        self.order = list(order)
+
+    def start(self, *earlier):
+        self.bit = self.order.pop(0)
+        self.keep = [r for r in self.left if not r & self.bit]
+        self.send = jnp.stack([self.pieces[r | self.bit] for r in self.keep])
+        if earlier:
+            self.send = tie(self.send, *earlier)
+        self.got = swap(self.send, self.bit)
+
+    def finish(self):
+        for position, r in enumerate(self.keep):
+            added = self.pieces[r].astype(f32) + self.got[position].astype(f32)
+            self.pieces[r] = added.astype(bf16) if self.order else added
+        self.left = self.keep
 
 
 def body(
@@ -527,16 +551,6 @@
         depth_bits.append(bit)
         bit *= 2
 
-    wide_parts = fc1_weight.shape[1] // model_width
-    shards = [out_weight]
-    shards += [fc1_weight[:, k * model_width : (k + 1) * model_width] for k in range(wide_parts)]
-    every = lax.all_gather(jnp.concatenate(shards + [fc2_weight], axis=0), "seq")
-    step = out_weight.shape[0]
-    out_full = every[:, :step].reshape(model_width, model_width)
-    up_full = every[:, step : (1 + wide_parts) * step].reshape(n, wide_parts, step, model_width)
-    up_full = up_full.transpose(0, 2, 1, 3).reshape(model_width, wide_parts * model_width)
-    down_full = every[:, (1 + wide_parts) * step :].reshape(wide_parts * model_width, model_width)
-
     small = [ln1_gain, ln1_bias, q_bias, v_bias, out_bias, ln2_gain, ln2_bias, fc2_bias, fc1_bias]
     shard_rows = qkv_weight.shape[0]
     small_len = sum(item.shape[0] for item in small)
@@ -548,14 +562,36 @@
     outgoing = jnp.concatenate(
         [by_pair, jnp.broadcast_to(small_rows[None], (PLANE,) + small_rows.shape)], axis=1
     )
-    arrived = [lax.dynamic_index_in_dim(outgoing, mine, 0, keepdims=False)]
-    for r in range(1, PLANE):
-        arrived.append(
-            swap(lax.dynamic_index_in_dim(outgoing, jnp.bitwise_xor(mine, r), 0, keepdims=False), r)
-        )
-    current = jnp.stack(arrived)
-    for bit in depth_bits:
-        current = jnp.concatenate([current, swap(current, bit)], axis=0)
+    arrived = exchange(outgoing[jnp.bitwise_xor(mine, jnp.arange(PLANE))])
+
+    token_orders = [[2, 4, 1] if m % 2 == 0 else [4, 2, 1] for m in range(micro_count)]
+    gathered = [tokens[m][None] for m in range(micro_count)]
+    current = arrived
+    for k in range(3):
+        if k == 1:
+            gathered = [tie(item, arrived) for item in gathered]
+        got = [swap(item, token_orders[m][k]) for m, item in enumerate(gathered)]
+        if k == 1:
+            for bit in depth_bits:
+                current = jnp.concatenate([current, swap(current, bit)], axis=0)
+            got[0] = tie(got[0], current)
+        halves = list(zip(gathered, got))
+        gathered = [jnp.concatenate(pair, axis=0) for pair in halves]
+
+    step = out_weight.shape[0]
+    wide_parts = fc1_weight.shape[1] // model_width
+    up_shard = fc1_weight.reshape(step, n, wide_parts, step).transpose(2, 0, 1, 3)
+    shards = [out_weight, up_shard.reshape(wide_parts * step, model_width), fc2_weight]
+    packed = tie(jnp.concatenate(shards, axis=0), current, *[near for near, _ in halves])
+    every = lax.all_gather(packed, "seq")
+
+    def whole_part(k):
+        return every[:, k * step : (k + 1) * step].reshape(model_width, model_width)
+
+    out_full = whole_part(0)
+    ups = [whole_part(1 + k) for k in range(wide_parts)]
+    downs = [whole_part(1 + wide_parts + k) for k in range(wide_parts)]
+
     pair_blocks = turn_blocks(info, current)
     pair_weight = pair_blocks[:, :shard_rows].reshape(n * shard_rows, 3 * PAIR)
     small_all = pair_blocks[:, shard_rows:].reshape(n, -1).astype(f32)
@@ -567,12 +603,7 @@
         offset += width
     gain_one, shift_one, q_shift, v_shift, out_shift, gain_two, shift_two, down_shift, up_shift = small_full
 
-    plane_stream = jnp.stack(
-        [
-            plane_tokens(tokens[m], [2, 4, 1] if m % 2 == 0 else [4, 2, 1])
-            for m in range(micro_count)
-        ]
-    )
+    plane_stream = jnp.stack([plane_tokens(near, far, order) for (near, far), order in zip(halves, token_orders)])
     plane_flat = plane_stream.reshape(micro_count * plane_rows, model_width)
     normed, _, _ = layer_norm_parts(plane_flat.astype(f32), gain_one, shift_one)
     normed_low = normed.astype(bf16)
@@ -610,22 +641,33 @@
     middle = stream + product(mixed_low, out_full) + out_shift
     normed_two, normal_two, inverse_two = layer_norm_parts(middle, gain_two, shift_two)
     normed_two_low = normed_two.astype(bf16)
-    hidden = product(normed_two_low, up_full) + up_shift
-    gate = jax.nn.sigmoid(1.702 * hidden)
-    active_low = (hidden * gate).astype(bf16)
-    grad_active = product_nt(cotangent_low, down_full)
-    grad_hidden_low = (grad_active * (gate + 1.702 * hidden * gate * (1.0 - gate))).astype(bf16)
+    up_shifts = up_shift.reshape(n, wide_parts, step).transpose(1, 0, 2).reshape(wide_parts, model_width)
+    actives, grad_hiddens = [], []
+    for k in range(wide_parts):
+        hidden = product(normed_two_low, ups[k]) + up_shifts[k]
+        gate = jax.nn.sigmoid(1.702 * hidden)
+        actives.append((hidden * gate).astype(bf16))
+        grad_active = product_nt(cotangent_low, downs[k])
+        grad_hiddens.append((grad_active * (gate + 1.702 * hidden * gate * (1.0 - gate))).astype(bf16))
+
+    def by_device(partial):
+        return partial.astype(bf16).reshape(n, -1, model_width)
 
     order_a = [1, 2, 4] + depth_bits[::-1]
     order_b = [1, 4, 2] + depth_bits[::-1]
-    grad_down = product_tn(active_low, cotangent_low).astype(bf16).reshape(n, -1, model_width)
-    half = grad_down.shape[1] // 2
-    down = [Scatter(me, grad_down[:, :half], order_a), Scatter(me, grad_down[:, half:], order_b)]
+    grad_downs = [by_device(product_tn(active, cotangent_low)) for active in actives]
+    mid = wide_parts // 2
+    down = [Scatter(me, grad_downs[:mid], order_a), Scatter(me, grad_downs[mid:], order_b)]
     for part in down:
         part.swap()
-    grad_hidden_low = tie(grad_hidden_low, *[part.send for part in down])
-
-    grad_normed_two = product_nt(grad_hidden_low, up_full)
+    grad_hiddens[0] = tie(grad_hiddens[0], *[part.send for part in down])
+
+    grad_normed_two = product_nt(grad_hiddens[0], ups[0])
+    for k in range(1, wide_parts):
+        grad_normed_two = grad_normed_two + product_nt(grad_hiddens[k], ups[k])
+    for part in down:
+        part.advance(grad_normed_two)
+    grad_normed_two = tie(grad_normed_two, *[part.send for part in down])
     grad_middle = cotangent_low.astype(f32) + layer_norm_back(
         grad_normed_two, normal_two, inverse_two, gain_two
     )
@@ -637,25 +679,26 @@
         part = part.reshape(micro_count, tok_dev, PAIR)
         grad_parts.append(part if r == 0 else swap(part, r))
 
-    for part in down:
-        part.advance(grad_branch_low)
-
     later = tie(normed_two_low, grad_mixed_low)
-    grad_up = product_tn(later, grad_hidden_low).astype(bf16).reshape(n, step, -1)
-    up = [Scatter(me, grad_up[:, : step // 2], order_a), Scatter(me, grad_up[:, step // 2 :], order_b)]
+    grad_ups = [by_device(product_tn(later, grad_hidden)) for grad_hidden in grad_hiddens]
+    grad_out_weight = by_device(product_tn(mixed_low, grad_branch_low))
+    up = [
+        Scatter(me, grad_ups[:mid] + [grad_out_weight[:, : step // 2]], order_a),
+        Scatter(me, grad_ups[mid:] + [grad_out_weight[:, step // 2 :]], order_b),
+    ]
     for part in up:
         part.swap()
-    grad_out_weight = product_tn(mixed_low, grad_branch_low).astype(bf16).reshape(n, step, model_width)
-    out_part = Scatter(me, grad_out_weight, order_b)
-    out_part.swap()
-    result = middle + product(tie(active_low, grad_mixed_low), down_full) + down_shift
+    result = middle + down_shift
+    after_up = tie(actives[0], *[part.send for part in up])
+    for k in range(wide_parts):
+        result = result + product(after_up if k == 0 else actives[k], downs[k])
     result_low = result.astype(bf16)
-    moving = up + [out_part]
-    for part in moving:
-        part.advance()
+    for part in up:
+        part.advance(result_low, *grad_parts)
 
     grad_flat = []
-    before_back = [part.send for part in moving] + [result_low]
+    before_back = [part.send for part in up]
+    joined_parts = []
     for m in range(micro_count):
         own_grad = tie(grad_parts[0], *before_back)
         grad_query, grad_pairs, grad_before, grad_after = attend_back(
@@ -663,31 +706,30 @@
         )
         from_next = shift_plane(grad_before, -1)
         from_last = shift_plane(grad_after, 1)
-        if m == 0:
-            for part in down:
-                part.advance(grad_before)
-            before_back = [part.send for part in down]
+        moving = down if m % 2 == 0 else up
+        for part in moving:
+            part.advance(grad_before)
+        before_back = [part.send for part in moving]
+        joined_parts.append((grad_query, grad_pairs, from_last, from_next))
+    grad_planes = []
+    for m in range(micro_count):
+        grad_query, grad_pairs, from_last, from_next = joined_parts[m]
+        grad_query = tie(grad_query, *before_back)
         joined = join_grads(info, grad_query, grad_pairs, from_last, from_next, tok_dev)
         grad_flat.append(joined.reshape(plane_rows, 3 * PAIR))
-        last_grad = grad_before
-
-    for part in moving + down:
-        part.advance(last_grad)
-
-    grad_normed = []
-    for m in range(micro_count):
         grad_plane = product_nt(grad_flat[m], pair_weight).reshape(PLANE, tok_dev, model_width)
-        grad_normed.append(plane_scatter(grad_plane, [1, 2, 4] if m % 2 == 0 else [1, 4, 2]))
-    grad_normed = jnp.concatenate(grad_normed, axis=0)
-    for part in moving + down:
-        while part.order:
-            part.advance()
-    down_sum = jnp.concatenate([part.total() for part in down], axis=0)
-    up_sum = jnp.concatenate([part.total() for part in up], axis=0)
-    out_sum = out_part.total()
-    _, normal_one, inverse_one = layer_norm_parts(stream, gain_one, shift_one)
-    grad_stream = grad_middle + layer_norm_back(grad_normed, normal_one, inverse_one, gain_one)
-    grad_flat = jnp.concatenate(grad_flat, axis=0)
+        order = [1, 2, 4] if m % 2 == 0 else [1, 4, 2]
+        grad_planes.append(PlaneScatter(grad_plane, order))
+        grad_planes[m].start()
+        moving = down if m % 2 == 0 else up
+        for part in moving:
+            part.advance(joined)
+        before_back = [part.send for part in moving]
+    for plane in grad_planes:
+        plane.finish()
+        plane.start(*before_back)
+    plane_sends = [plane.send for plane in grad_planes]
+    grad_flat = tie(jnp.concatenate(grad_flat, axis=0), *plane_sends)
 
     grad_pair_weight = product_tn(normed_low, grad_flat)
     column_sum = jnp.sum(grad_flat.astype(f32), axis=0)
@@ -708,7 +750,7 @@
         jnp.sum(grad_normed_two * normal_two, axis=0),
         jnp.sum(grad_normed_two, axis=0),
         jnp.sum(cotangent_low.astype(f32), axis=0),
-        jnp.sum(grad_hidden_low.astype(f32), axis=0),
+        jnp.stack([jnp.sum(item.astype(f32), axis=0).reshape(n, step) for item in grad_hiddens], axis=1),
     ]
     small_out = jnp.concatenate([item.reshape(n, -1) for item in small_grads], axis=1).astype(bf16)
     small_out = jnp.pad(small_out, ((0, 0), (0, spare_rows * 3 * PAIR - small_len)))
@@ -717,18 +759,43 @@
         [grad_pair_weight.astype(bf16).reshape(n, shard_rows, 3 * PAIR), small_out], axis=1
     )
     turned = turn_blocks(info, leaving)
+
+    for part in down:
+        part.advance(turned)
     size = n
-    for bit in depth_bits[::-1]:
+    for index, bit in enumerate(depth_bits[::-1]):
         size //= 2
         got = swap(turned[size:], bit)
+        if index == 0:
+            for plane in grad_planes:
+                plane.got = tie(plane.got, turned)
+                plane.finish()
+                plane.start()
+            got = tie(got, *[plane.send for plane in grad_planes])
         turned = (turned[:size].astype(f32) + got.astype(f32)).astype(bf16)
+    for part in up:
+        part.advance(turned)
+    for plane in grad_planes:
+        plane.got = tie(plane.got, *[part.send for part in up])
+        plane.finish()
+    grad_normed = jnp.concatenate([plane.pieces[0] for plane in grad_planes], axis=0)
+    _, normal_one, inverse_one = layer_norm_parts(stream, gain_one, shift_one)
+    grad_stream = grad_middle + layer_norm_back(grad_normed, normal_one, inverse_one, gain_one)
+    stream_low = grad_stream.astype(bf16)
+    for part in up + down:
+        while part.order:
+            part.advance(stream_low)
+    down_sum = jnp.concatenate([part.total() for part in down], axis=0)
+    up_totals = [part.total() for part in up]
+    out_sum = jnp.concatenate([total[mid * step :] for total in up_totals], axis=0)
+    up_sum = jnp.concatenate([total[: mid * step] for total in up_totals], axis=0)
+    up_sum = up_sum.reshape(wide_parts, step, n, step).transpose(1, 2, 0, 3).reshape(step, -1)
+    back = exchange(turned).astype(f32)
     qkv_sum = jnp.zeros((shard_rows, 3, model_width), f32)
-    small_sum = jnp.zeros((spare_rows, 3 * PAIR), f32)
     for r in range(PLANE):
-        part = turned[r] if r == 0 else swap(turned[r], r)
-        columns = part[:shard_rows].reshape(shard_rows, 3, PAIR).astype(f32)
+        columns = back[r, :shard_rows].reshape(shard_rows, 3, PAIR)
         qkv_sum = lax.dynamic_update_slice(qkv_sum, columns, (0, 0, column(r)))
-        small_sum = small_sum + part[shard_rows:].astype(f32)
+    small_sum = jnp.sum(back[:, shard_rows:], axis=0)
     qkv_sum = qkv_sum.reshape(shard_rows, 3 * model_width)
     small_sum = small_sum.reshape(-1)
     sums = []
@@ -739,7 +806,7 @@
 
     return (
         result_low.reshape(micro_count, tok_dev, model_width),
-        grad_stream.astype(bf16).reshape(micro_count, tok_dev, model_width),
+        stream_low.reshape(micro_count, tok_dev, model_width),
         sums[0],
         sums[1],
         qkv_sum,

time: 749 us -> 599 us (0.80)
  waiting for transfers between devices: 276 us -> 120 us
  starting transfers between devices: 84.9 us -> 70.6 us
  local copies, waits for them, and re-layouts: 105 us -> 114 us
    ppermute x69 -> x56, waiting for transfers between devices: 258 us -> 95.5 us  [swap(): return lax.ppermute(block, 'seq', [(i, i ^ bit) for i in range(n)])]
    reshape x0 -> x6, local copies, waits for them, and re-layouts: none -> 20.2 us  [the longest x3 12.3 us: body(): up_sum.reshape(wide_parts, step, n, step).transpose(1, 2, 0, 3)]
    unnamed x214 -> x213, local copies, waits for them, and re-layouts: 51.2 us -> 36.7 us
    ppermute x69 -> x56, starting transfers between devices: 64.2 us -> 53.8 us  [swap(): return lax.ppermute(block, 'seq', [(i, i ^ bit) for i in range(n)])]
    transpose x1 -> x0, local copies, waits for them, and re-layouts: 7.91 us -> none  [body(): up_full.transpose(0, 2, 1, 3).reshape(model_width, wide_parts * model_width)]
    dot_general x4 -> x10, matrix products: 20.7 us -> 28.1 us  [product_tn(): lax.dot_general(left, right, (((0,), (0,)), ((), ())), preferred_element_...]
    convert_element_type x37 -> x22, other arithmetic: 49.4 us -> 42.4 us  [the longest x16 31.9 us: half(): return (kept + pick(self.got, axis, index).astype(f32)).astype(bf16)]
    slice x5 -> x11, local copies, waits for them, and re-layouts: 15.5 us -> 10.7 us  [the longest x1 10.2 us: whole_part(): return every[:, k * step:(k + 1) * step].reshape(model_width, model_width)]
  transfers between devices with their start and end apart: 76 -> 63, of which waited for: 31 -> 15; matrix products, arithmetic and copies ran while one was open for 27% -> 34% of each run, Pallas kernels for 12% -> 16%
where the time goes in v3:
time: 599 us; the launch traced here: 588 us
  waiting for transfers between devices  120 us (20%)
  local copies, waits for them, and re-layouts  114 us (19%)
  other arithmetic  99.5 us (17%)
  Pallas kernels  91.2 us (15%)
  matrix products  76.6 us (13%)
  starting transfers between devices  70.6 us (12%)
  between operations  16.6 us (3%)
    ppermute x56, waiting for transfers between devices, swap(): return lax.ppermute(block, 'seq', [(i, i ^ bit) for i in range(n)])  95.5 us
    ppermute x56, starting transfers between devices, swap(): return lax.ppermute(block, 'seq', [(i, i ^ bit) for i in range(n)])  53.8 us
    pallas_call x2, Pallas kernels, attend_back(): pl.pallas_call(functools.partial(attend_back_kernel, m), grid_spec=pltpu....  40.7 us
    unnamed x213, local copies, waits for them, and re-layouts  36.7 us
    pallas_call x1, Pallas kernels, attend(): pl.pallas_call(attend_kernel, grid_spec=pltpu.PrefetchScalarGridSpec(num_...  36.4 us
    convert_element_type x16, other arithmetic, half(): return (kept + pick(self.got, axis, index).astype(f32)).astype(bf16)  31.9 us
    dot_general x10, matrix products, product_tn(): lax.dot_general(left, right, (((0,), (0,)), ((), ())), preferred_element_...  28.1 us
    dot_general x11, matrix products, product_nt(): lax.dot_general(left, right, (((1,), (1,)), ((), ())), preferred_element_...  26.7 us
  transfers between devices with their start and end apart: 63, of which 15 were waited for; matrix products, arithmetic and copies ran while one was open for 34% of the time, Pallas kernels for 16%

profile of v3, /device:TPU:0, one launch (start us, length us, event | category | flops | bytes accessed | tf_op | source)
XLA Modules:
  0.0 588.1 jit_solution(10128115372229382932)
XLA Ops:
  7.2 6.2 %concatenate.90 = bf16[384]{0:T(512)(128)(2,1)S(1)} concatenate(bf16[32]{0:T(256)(128)(2,1)} %param.18, bf16[32]{0:T(256)(128)(2,1)} %param.19, bf16[32]{0:T(256)(128)(2,1)} %param.21, bf16[32]{0:T(256)(128)(2,1)} %param.22, bf16[32]{0:T(256)(128)(2,1)} %param.24, bf16[32]{0:T(256)(128)(2,1)} %param.25, bf16[32]{0:T(256)(128)(2,1)} %param.26, bf16[32]{0:T(256)(128)(2,1)} %param.30, ...), dimensions={0} | concatenate | bytes 1536 | tf_op jit(solution)/shard_map/concatenate | solution.py:558
  21.4 12.4 %collective-permute-done.2 = bf16[2,2,40,384]{3,2,0,1:T(8,128)(2,1)S(1)} collective-permute-done((bf16[2,2,40,384]{3,2,0,1:T(8,128)(2,1)S(1)}, bf16[2,2,40,384]{3,2,0,1:T(8,128)(2,1)S(1)}, u32[]{:S(2)}, u32[]{:S(2)}) %collective-permute-start.2) | collective-permute-done | bytes 122912 | tf_op jit(solution)/shard_map/ppermute | solution.py:39
  35.7 3.4 collective-permute-done.3
  60.6 10.0 %collective-permute-done.6 = bf16[16,40,384]{2,1,0:T(8,128)(2,1)} collective-permute-done((bf16[16,40,384]{2,1,0:T(8,128)(2,1)}, bf16[16,40,384]{2,1,0:T(8,128)(2,1)}, u32[]{:S(2)}, u32[]{:S(2)}) %collective-permute-start.6) | collective-permute-done | bytes 491552 | tf_op jit(solution)/shard_map/ppermute | solution.py:39
  113.1 3.4 add_convert_fusion
  116.5 4.8 add_convert_fusion.1
  127.9 18.9 %collective-permute-done.11.before = bf16[2,576,256]{2,1,0:T(8,128)(2,1)S(1)} collective-permute-done((bf16[2,576,256]{2,1,0:T(8,128)(2,1)S(1)}, bf16[2,576,256]{2,1,0:T(8,128)(2,1)S(1)}, u32[]{:S(2)}, u32[]{:S(2)}) %collective-permute-start.11) | collective-permute-done | bytes 589856 | tf_op jit(solution)/shard_map/ppermute | solution.py:45
  146.8 3.8 collective-permute-done.12.after
  151.5 36.4 %shard_map.272 = (bf16[8,2,256,128]{3,2,1,0:T(8,128)(2,1)}, f32[32,256]{1,0:T(8,128)}) custom-call(s32[3]{0:T(128)} %pad_add_fusion.info, s32[2,16]{1,0:T(2,128)} %concatenate.88.bounds, bf16[2,8,256,384]{3,2,1,0:T(8,128)(2,1)} %bitcast.525, bf16[2,576,256]{2,1,0:T(8,128)(2,1)} %copy-done.19, bf16[2,576,256]{2,1,0:T(8,128)(2,1)} %copy-done.20), custom_call_target="tpu_custom_call" | custom-call | flops 2684354560 | bytes 157286400 | tf_op jit(solution)/shard_map/pallas_call | solution.py:381
  201.0 5.1 collective-permute-done.17
  209.4 10.2 %fusion.99 = (bf16[32,32,1024]{2,1,0:T(8,128)(2,1)S(1)}, bf16[32,32,1024]{2,1,0:T(8,128)(2,1)S(1)}, bf16[32,32,1024]{2,1,0:T(8,128)(2,1)S(1)}, bf16[32,32,1024]{...) fusion(bf16[32,288,1024]{2,1,0:T(8,128)(2,1)} %bitcast.528), kind=kLoop, calls=%fused_computation.393 | loop fusion | bytes 37748736 | tf_op jit(solution)/shard_map/slice | solution.py:589
  219.6 3.3 fusion.107
  239.7 10.1 %convolution_convert_fusion.7 = bf16[1024,1024]{1,0:T(8,128)(2,1)S(1)} fusion(bf16[512,1024]{1,0:T(8,128)(2,1)S(1)} %bitcast.555, f32[512,1024]{1,0:T(8,128)S(1)} %fusion.113, f32[1024]{0:T(1024)S(1)} %add.617), kind=kOutput, calls=%fused_computation.87 | convolution fusion | flops 1078460416 | bytes 5246976 | tf_op jit(solution)/shard_map/dot_general | solution.py:30
  250.4 3.4 fusion.110
  289.1 3.1 fusion.98
  307.7 7.7 %collective-permute-done.27.refs_5_ = bf16[2,256,128]{2,1,0:T(8,128)(2,1)S(1)} collective-permute-done((bf16[2,256,128]{2,1,0:T(8,128)(2,1)S(1)}, bf16[2,256,128]{2,1,0:T(8,128)(2,1)S(1)}, u32[]{:S(2)}, u32[]{:S(2)}) %collective-permute-start.27) | collective-permute-done | bytes 131104 | tf_op jit(solution)/shard_map/ppermute | solution.py:39
  327.9 20.3 %shard_map.273 = (f32[2048,128]{1,0:T(8,128)}, f32[2048,256]{1,0:T(8,128)}, bf16[768,256]{1,0:T(8,128)(2,1)}, bf16[768,256]{1,0:T(8,128)(2,1)}) custom-call(s32[3]{0:T(128)} %pad_add_fusion.info, s32[2,16]{1,0:T(2,128)} %concatenate.88.bounds, bf16[2,8,256,384]{3,2,1,0:T(8,128)(2,1)} %bitcast.526, bf16[2,576,256]{2,1,0:T(8,128)(2,1)} %copy-done.19, ...), custom_call_target="tpu_custom_call" | custom-call | flops 1342177280 | bytes 91750400 | tf_op jit(solution)/shard_map/pallas_call | solution.py:412
  353.4 5.3 collective-permute-start.35
  361.3 7.8 %collective-permute-done.31 = bf16[2,2,2,80,1024]{4,3,1,2,0:T(8,128)(2,1)} collective-permute-done((bf16[2,2,2,80,1024]{4,3,1,2,0:T(8,128)(2,1)}, bf16[2,2,2,80,1024]{4,3,1,2,0:T(8,128)(2,1)}, u32[]{:S(2)}, u32[]{:S(2)}) %collective-permute-start.31) | collective-permute-done | bytes 1310752 | tf_op jit(solution)/shard_map/ppermute | solution.py:39
  375.9 20.4 %shard_map.274 = (f32[2048,128]{1,0:T(8,128)}, f32[2048,256]{1,0:T(8,128)}, bf16[768,256]{1,0:T(8,128)(2,1)}, bf16[768,256]{1,0:T(8,128)(2,1)}) custom-call(s32[3]{0:T(128)} %pad_add_fusion.info, s32[2,16]{1,0:T(2,128)} %concatenate.88.bounds, bf16[2,8,256,384]{3,2,1,0:T(8,128)(2,1)} %bitcast.527, bf16[2,576,256]{2,1,0:T(8,128)(2,1)} %copy-done.19, ...), custom_call_target="tpu_custom_call" | custom-call | flops 1342177280 | bytes 91750400 | tf_op jit(solution)/shard_map/pallas_call | solution.py:412
  397.7 5.3 collective-permute-start.41
  403.1 3.3 fusion.23
  410.7 4.1 shard_map.275
  420.1 4.1 shard_map.276
  424.2 4.0 convolution_convert_fusion
  440.9 6.9 %fusion.3 = bf16[4096,1024]{1,0:T(8,128)(2,1)} fusion(f32[1024]{0:T(1024)S(1)} %copy-done.63, f32[1024]{0:T(1024)S(1)} %copy-done.53, f32[4096]{0:T(1024)S(1)} %bitcast.640, f32[4096]{0:T(1024)S(1)} %bitcast.641, bf16[1,8,256,1024]{3,2,1,0:T(8,128)(2,1)S(1)} %bitcast.523, bf16[1,8,256,1024]{3,2,1,0:T(8,128)(2,1)S(1)} %bitcast.519), kind=kLoop, calls=%fused_computation.5 | loop fusion | flops 29360128 | bytes 16818176 | tf_op jit(solution)/shard_map/convert_element_type | solution.py:609
  468.5 6.0 %fusion.101 = (bf16[1024,384]{1,0:T(8,128)(2,1)}, f32[1024]{0:T(1024)}) fusion(bf16[32,32,384]{2,1,0:T(8,128)(2,1)S(1)} %copy-done.41, bf16[4096,1024]{1,0:T(8,128)(2,1)S(1)} %bitcast.534, bf16[4096,384]{1,0:T(8,128)(2,1)S(1)} %pad_maximum_fusion.1), kind=kOutput, calls=%fused_computation.395 | convolution fusion | flops 3222797312 | bytes 13111296 | tf_op jit(solution)/shard_map/dot_general | solution.py:30
  500.9 37.0 %collective-permute-done.48 = bf16[16,40,384]{2,1,0:T(8,128)(2,1)S(1)} collective-permute-done((bf16[16,40,384]{2,1,0:T(8,128)(2,1)S(1)}, bf16[16,40,384]{2,1,0:T(8,128)(2,1)S(1)}, u32[]{:S(2)}, u32[]{:S(2)}) %collective-permute-start.48) | collective-permute-done | bytes 491552 | tf_op jit(solution)/shard_map/ppermute | solution.py:39
  549.1 3.2 collective-permute-done.57
  556.3 3.1 reshape.820
  559.4 4.7 copy.187
  564.1 4.4 reshape.821
  (578 shorter events, 289.3 us)
Async XLA Ops:
  7.2 202.2 %all-gather.3.cloned.1.call-start = ((), (), s32[]{:S(2)}) async-start(), calls=%async_computation | async-start | bytes 19464192 | tf_op jit(solution)/shard_map/all_gather | solution.py:586
  16.0 24.7 %collective-permute-start = (bf16[1,256,1024]{2,1,0:T(8,128)(2,1)S(1)}, bf16[1,256,1024]{2,1,0:T(8,128)(2,1)S(1)}, u32[]{:S(2)}, u32[]{:S(2)}) collective-permute-start(bf16[1,256,1024]{2,1,0:T(8,128)(2,1)S(1)} %get-tuple-element.211), channel_id=1, source_target_pairs={{0,2},{1,3},{2,0},{3,1},{4,6},{5,7},{6,4},{7,5},{8,10},{9,11},{10,... | collective-permute-start | bytes 1572872 | tf_op jit(solution)/shard_map/ppermute | solution.py:39
  40.8 31.8 %collective-permute-start.4 = (bf16[2,256,1024]{2,1,0:T(8,128)(2,1)S(1)}, bf16[2,256,1024]{2,1,0:T(8,128)(2,1)}, u32[]{:S(2)}, u32[]{:S(2)}) collective-permute-start(bf16[2,256,1024]{2,1,0:T(8,128)(2,1)S(1)} %pad_maximum_fusion.11), channel_id=1, source_target_pairs={{0,4},{1,5},{2,6},{3,7},{4,0},{5,1},{6,2},{7,3},{8,12},{9,13},{10,... | collective-permute-start | bytes 3145736 | tf_op jit(solution)/shard_map/ppermute | solution.py:39
  42.5 31.4 %collective-permute-start.9 = (bf16[2,256,1024]{2,1,0:T(8,128)(2,1)S(1)}, bf16[2,256,1024]{2,1,0:T(8,128)(2,1)}, u32[]{:S(2)}, u32[]{:S(2)}) collective-permute-start(bf16[2,256,1024]{2,1,0:T(8,128)(2,1)S(1)} %pad_maximum_fusion.12), channel_id=1, source_target_pairs={{0,2},{1,3},{2,0},{3,1},{4,6},{5,7},{6,4},{7,5},{8,10},{9,11},{10,... | collective-permute-start | bytes 3145736 | tf_op jit(solution)/shard_map/ppermute | solution.py:39
  47.6 22.9 %collective-permute-start.6 = (bf16[16,40,384]{2,1,0:T(8,128)(2,1)}, bf16[16,40,384]{2,1,0:T(8,128)(2,1)}, u32[]{:S(2)}, u32[]{:S(2)}) collective-permute-start(bf16[16,40,384]{2,1,0:T(8,128)(2,1)} %pad_maximum_fusion.24), channel_id=1, source_target_pairs={{0,16},{1,17},{2,18},{3,19},{4,20},{5,21},{6,22},{7,23},{8,24},{9,... | collective-permute-start | bytes 1474568 | tf_op jit(solution)/shard_map/ppermute | solution.py:39
  123.1 23.7 %collective-permute-start.11 = (bf16[2,576,256]{2,1,0:T(8,128)(2,1)S(1)}, bf16[2,576,256]{2,1,0:T(8,128)(2,1)S(1)}, u32[]{:S(2)}, u32[]{:S(2)}) collective-permute-start(bf16[2,576,256]{2,1,0:T(8,128)(2,1)S(1)} %pad_maximum_fusion.19), channel_id=1, source_target_pairs={{0,8},{1,9},{2,10},{3,11},{4,12},{5,13},{6,14},{7,15},{8,16},{9,17... | collective-permute-start | bytes 1769480 | tf_op jit(solution)/shard_map/ppermute | solution.py:45
  125.7 25.0 %collective-permute-start.12 = (bf16[2,576,256]{2,1,0:T(8,128)(2,1)}, bf16[2,576,256]{2,1,0:T(8,128)(2,1)S(1)}, u32[]{:S(2)}, u32[]{:S(2)}) collective-permute-start(bf16[2,576,256]{2,1,0:T(8,128)(2,1)} %pad_maximum_fusion.17), channel_id=1, source_target_pairs={{8,0},{9,1},{10,2},{11,3},{12,4},{13,5},{14,6},{15,7},{16,8},{17,9... | collective-permute-start | bytes 1769480 | tf_op jit(solution)/shard_map/ppermute | solution.py:45
  288.1 29.1 %collective-permute-start.22 = (bf16[2,2,2,2,80,1024]{5,4,1,0,3,2:T(8,128)(2,1)S(1)}, bf16[2,2,2,2,80,1024]{5,4,1,0,3,2:T(8,128)(2,1)S(1)}, u32[]{:S(2)}, u32[]{:S(2)}) collective-permute-start(bf16[2,2,2,2,80,1024]{5,4,1,0,3,2:T(8,128)(2,1)S(1)} %pad_maximum_fusion.2), channel_id=1, source_target_pairs={{0,1},{1,0},{2,3},{3,2},{4,5},{5,4},{6,7},{7,6},{8,9},{9,8},{10,11... | collective-permute-start | bytes 7864328 | tf_op jit(solution)/shard_map/ppermute | solution.py:39
  288.8 33.2 %collective-permute-start.30 = (bf16[2,2,2,2,80,1024]{5,4,1,0,3,2:T(8,128)(2,1)S(1)}, bf16[2,2,2,2,80,1024]{5,4,1,0,3,2:T(8,128)(2,1)S(1)}, u32[]{:S(2)}, u32[]{:S(2)}) collective-permute-start(bf16[2,2,2,2,80,1024]{5,4,1,0,3,2:T(8,128)(2,1)S(1)} %pad_maximum_fusion.3), channel_id=1, source_target_pairs={{0,1},{1,0},{2,3},{3,2},{4,5},{5,4},{6,7},{7,6},{8,9},{9,8},{10,11... | collective-permute-start | bytes 7864328 | tf_op jit(solution)/shard_map/ppermute | solution.py:39
  315.4 34.4 %collective-permute-start.32 = (bf16[2,2,2,64,1024]{4,3,1,2,0:T(8,128)(2,1)}, bf16[2,2,2,64,1024]{4,3,1,2,0:T(8,128)(2,1)}, u32[]{:S(2)}, u32[]{:S(2)}) collective-permute-start(bf16[2,2,2,64,1024]{4,3,1,2,0:T(8,128)(2,1)} %copy.132), channel_id=1, source_target_pairs={{0,2},{1,3},{2,0},{3,1},{4,6},{5,7},{6,4},{7,5},{8,10},{9,11},{10,... | collective-permute-start | bytes 3145736 | tf_op jit(solution)/shard_map/ppermute | solution.py:39
  315.9 33.9 %collective-permute-start.33 = (bf16[2,2,2,64,1024]{4,3,1,2,0:T(8,128)(2,1)}, bf16[2,2,2,64,1024]{4,3,1,2,0:T(8,128)(2,1)}, u32[]{:S(2)}, u32[]{:S(2)}) collective-permute-start(bf16[2,2,2,64,1024]{4,3,1,2,0:T(8,128)(2,1)} %copy.133), channel_id=1, source_target_pairs={{0,4},{1,5},{2,6},{3,7},{4,0},{5,1},{6,2},{7,3},{8,12},{9,13},{10,... | collective-permute-start | bytes 3145736 | tf_op jit(solution)/shard_map/ppermute | solution.py:39
  321.0 48.1 %collective-permute-start.31 = (bf16[2,2,2,80,1024]{4,3,1,2,0:T(8,128)(2,1)}, bf16[2,2,2,80,1024]{4,3,1,2,0:T(8,128)(2,1)}, u32[]{:S(2)}, u32[]{:S(2)}) collective-permute-start(bf16[2,2,2,80,1024]{4,3,1,2,0:T(8,128)(2,1)} %copy.131), channel_id=1, source_target_pairs={{0,2},{1,3},{2,0},{3,1},{4,6},{5,7},{6,4},{7,5},{8,10},{9,11},{10,... | collective-permute-start | bytes 3932168 | tf_op jit(solution)/shard_map/ppermute | solution.py:39
  325.6 72.1 %collective-permute-start.34 = (bf16[2,2,2,80,1024]{4,3,1,2,0:T(8,128)(2,1)}, bf16[2,2,2,80,1024]{4,3,1,2,0:T(8,128)(2,1)}, u32[]{:S(2)}, u32[]{:S(2)}) collective-permute-start(bf16[2,2,2,80,1024]{4,3,1,2,0:T(8,128)(2,1)} %copy.134), channel_id=1, source_target_pairs={{0,4},{1,5},{2,6},{3,7},{4,0},{5,1},{6,2},{7,3},{8,12},{9,13},{10,... | collective-permute-start | bytes 3932168 | tf_op jit(solution)/shard_map/ppermute | solution.py:39
  348.2 61.1 %collective-permute-start.36 = (bf16[768,256]{1,0:T(8,128)(2,1)}, bf16[768,256]{1,0:T(8,128)(2,1)S(1)}, u32[]{:S(2)}, u32[]{:S(2)}) collective-permute-start(bf16[768,256]{1,0:T(8,128)(2,1)} %get-tuple-element.77), channel_id=1, source_target_pairs={{8,0},{9,1},{10,2},{11,3},{12,4},{13,5},{14,6},{15,7},{16,8},{17,9... | collective-permute-start | bytes 1179656 | tf_op jit(solution)/shard_map/ppermute | solution.py:45
  352.9 62.0 %collective-permute-start.39 = (bf16[2,2,64,1024]{3,2,1,0:T(8,128)(2,1)}, bf16[2,2,64,1024]{3,2,1,0:T(8,128)(2,1)}, u32[]{:S(2)}, u32[]{:S(2)}) collective-permute-start(bf16[2,2,64,1024]{3,2,1,0:T(8,128)(2,1)} %get-tuple-element.161), channel_id=1, source_target_pairs={{0,4},{1,5},{2,6},{3,7},{4,0},{5,1},{6,2},{7,3},{8,12},{9,13},{10,... | collective-permute-start | bytes 1572872 | tf_op jit(solution)/shard_map/ppermute | solution.py:39
  353.4 42.9 %collective-permute-start.35 = (bf16[768,256]{1,0:T(8,128)(2,1)}, bf16[768,256]{1,0:T(8,128)(2,1)}, u32[]{:S(2)}, u32[]{:S(2)}) collective-permute-start(bf16[768,256]{1,0:T(8,128)(2,1)} %get-tuple-element.86), channel_id=1, source_target_pairs={{0,8},{1,9},{2,10},{3,11},{4,12},{5,13},{6,14},{7,15},{8,16},{9,17... | collective-permute-start | bytes 1179656 | tf_op jit(solution)/shard_map/ppermute | solution.py:45
  369.1 46.6 %collective-permute-start.40 = (bf16[2,2,64,1024]{3,2,1,0:T(8,128)(2,1)}, bf16[2,2,64,1024]{3,2,1,0:T(8,128)(2,1)}, u32[]{:S(2)}, u32[]{:S(2)}) collective-permute-start(bf16[2,2,64,1024]{3,2,1,0:T(8,128)(2,1)} %get-tuple-element.159), channel_id=1, source_target_pairs={{0,2},{1,3},{2,0},{3,1},{4,6},{5,7},{6,4},{7,5},{8,10},{9,11},{10,... | collective-permute-start | bytes 1572872 | tf_op jit(solution)/shard_map/ppermute | solution.py:39
  396.3 23.8 %collective-permute-start.42 = (bf16[768,256]{1,0:T(8,128)(2,1)}, bf16[768,256]{1,0:T(8,128)(2,1)}, u32[]{:S(2)}, u32[]{:S(2)}) collective-permute-start(bf16[768,256]{1,0:T(8,128)(2,1)} %get-tuple-element.81), channel_id=1, source_target_pairs={{8,0},{9,1},{10,2},{11,3},{12,4},{13,5},{14,6},{15,7},{16,8},{17,9... | collective-permute-start | bytes 1179656 | tf_op jit(solution)/shard_map/ppermute | solution.py:45
  409.3 44.0 %collective-permute-start.38 = (bf16[2,2,80,1024]{3,2,1,0:T(8,128)(2,1)}, bf16[2,2,80,1024]{3,2,1,0:T(8,128)(2,1)}, u32[]{:S(2)}, u32[]{:S(2)}) collective-permute-start(bf16[2,2,80,1024]{3,2,1,0:T(8,128)(2,1)} %get-tuple-element.155), channel_id=1, source_target_pairs={{0,4},{1,5},{2,6},{3,7},{4,0},{5,1},{6,2},{7,3},{8,12},{9,13},{10,... | collective-permute-start | bytes 1966088 | tf_op jit(solution)/shard_map/ppermute | solution.py:39
  414.8 40.2 %collective-permute-start.43 = (bf16[2,2,80,1024]{3,2,1,0:T(8,128)(2,1)}, bf16[2,2,80,1024]{3,2,1,0:T(8,128)(2,1)}, u32[]{:S(2)}, u32[]{:S(2)}) collective-permute-start(bf16[2,2,80,1024]{3,2,1,0:T(8,128)(2,1)} %get-tuple-element.153), channel_id=1, source_target_pairs={{0,2},{1,3},{2,0},{3,1},{4,6},{5,7},{6,4},{7,5},{8,10},{9,11},{10,... | collective-permute-start | bytes 1966088 | tf_op jit(solution)/shard_map/ppermute | solution.py:39
  431.7 27.7 %collective-permute-start.45 = (bf16[4,256,1024]{2,1,0:T(8,128)(2,1)}, bf16[4,256,1024]{2,1,0:T(8,128)(2,1)}, u32[]{:S(2)}, u32[]{:S(2)}) collective-permute-start(bf16[4,256,1024]{2,1,0:T(8,128)(2,1)} %pad_maximum_fusion.9), channel_id=1, source_target_pairs={{0,1},{1,0},{2,3},{3,2},{4,5},{5,4},{6,7},{7,6},{8,9},{9,8},{10,11... | collective-permute-start | bytes 6291464 | tf_op jit(solution)/shard_map/ppermute | solution.py:39
  438.6 25.0 %collective-permute-start.37 = (bf16[4,256,1024]{2,1,0:T(8,128)(2,1)}, bf16[4,256,1024]{2,1,0:T(8,128)(2,1)}, u32[]{:S(2)}, u32[]{:S(2)}) collective-permute-start(bf16[4,256,1024]{2,1,0:T(8,128)(2,1)} %pad_maximum_fusion.8), channel_id=1, source_target_pairs={{0,1},{1,0},{2,3},{3,2},{4,5},{5,4},{6,7},{7,6},{8,9},{9,8},{10,11... | collective-permute-start | bytes 6291464 | tf_op jit(solution)/shard_map/ppermute | solution.py:39
  449.9 35.2 %collective-permute-start.60 = (bf16[2,64,1024]{2,1,0:T(8,128)(2,1)}, bf16[2,64,1024]{2,1,0:T(8,128)(2,1)}, u32[]{:S(2)}, u32[]{:S(2)}) collective-permute-start(bf16[2,64,1024]{2,1,0:T(8,128)(2,1)} %get-tuple-element.189), channel_id=1, source_target_pairs={{0,16},{1,17},{2,18},{3,19},{4,20},{5,21},{6,22},{7,23},{8,24},{9,... | collective-permute-start | bytes 786440 | tf_op jit(solution)/shard_map/ppermute | solution.py:39
  453.3 35.5 %collective-permute-start.58 = (bf16[2,64,1024]{2,1,0:T(8,128)(2,1)}, bf16[2,64,1024]{2,1,0:T(8,128)(2,1)}, u32[]{:S(2)}, u32[]{:S(2)}) collective-permute-start(bf16[2,64,1024]{2,1,0:T(8,128)(2,1)} %get-tuple-element.187), channel_id=1, source_target_pairs={{0,16},{1,17},{2,18},{3,19},{4,20},{5,21},{6,22},{7,23},{8,24},{9,... | collective-permute-start | bytes 786440 | tf_op jit(solution)/shard_map/ppermute | solution.py:39
  462.4 32.6 %collective-permute-start.49 = (bf16[2,256,1024]{2,1,0:T(8,128)(2,1)}, bf16[2,256,1024]{2,1,0:T(8,128)(2,1)}, u32[]{:S(2)}, u32[]{:S(2)}) collective-permute-start(bf16[2,256,1024]{2,1,0:T(8,128)(2,1)} %pad_maximum_fusion.14), channel_id=1, source_target_pairs={{0,4},{1,5},{2,6},{3,7},{4,0},{5,1},{6,2},{7,3},{8,12},{9,13},{10,... | collective-permute-start | bytes 3145736 | tf_op jit(solution)/shard_map/ppermute | solution.py:39
  466.7 29.3 %collective-permute-start.44 = (bf16[2,256,1024]{2,1,0:T(8,128)(2,1)}, bf16[2,256,1024]{2,1,0:T(8,128)(2,1)}, u32[]{:S(2)}, u32[]{:S(2)}) collective-permute-start(bf16[2,256,1024]{2,1,0:T(8,128)(2,1)} %pad_maximum_fusion.13), channel_id=1, source_target_pairs={{0,2},{1,3},{2,0},{3,1},{4,6},{5,7},{6,4},{7,5},{8,10},{9,11},{10,... | collective-permute-start | bytes 3145736 | tf_op jit(solution)/shard_map/ppermute | solution.py:39
  486.2 58.9 %collective-permute-start.47 = (bf16[2,80,1024]{2,1,0:T(8,128)(2,1)}, bf16[2,80,1024]{2,1,0:T(8,128)(2,1)S(1)}, u32[]{:S(2)}, u32[]{:S(2)}) collective-permute-start(bf16[2,80,1024]{2,1,0:T(8,128)(2,1)} %get-tuple-element.185), channel_id=1, source_target_pairs={{0,16},{1,17},{2,18},{3,19},{4,20},{5,21},{6,22},{7,23},{8,24},{9,... | collective-permute-start | bytes 983048 | tf_op jit(solution)/shard_map/ppermute | solution.py:39
  488.8 56.1 %collective-permute-start.51 = (bf16[2,80,1024]{2,1,0:T(8,128)(2,1)}, bf16[2,80,1024]{2,1,0:T(8,128)(2,1)S(1)}, u32[]{:S(2)}, u32[]{:S(2)}) collective-permute-start(bf16[2,80,1024]{2,1,0:T(8,128)(2,1)} %get-tuple-element.183), channel_id=1, source_target_pairs={{0,16},{1,17},{2,18},{3,19},{4,20},{5,21},{6,22},{7,23},{8,24},{9,... | collective-permute-start | bytes 983048 | tf_op jit(solution)/shard_map/ppermute | solution.py:39
  492.3 45.7 %collective-permute-start.48 = (bf16[16,40,384]{2,1,0:T(8,128)(2,1)S(1)}, bf16[16,40,384]{2,1,0:T(8,128)(2,1)S(1)}, u32[]{:S(2)}, u32[]{:S(2)}) collective-permute-start(bf16[16,40,384]{2,1,0:T(8,128)(2,1)S(1)} %slice.619), channel_id=1, source_target_pairs={{0,16},{1,17},{2,18},{3,19},{4,20},{5,21},{6,22},{7,23},{8,24},{9,... | collective-permute-start | bytes 1474568 | tf_op jit(solution)/shard_map/ppermute | solution.py:39
  495.0 43.2 %collective-permute-start.59 = (bf16[64,1024]{1,0:T(8,128)(2,1)S(1)}, bf16[64,1024]{1,0:T(8,128)(2,1)S(1)}, u32[]{:S(2)}, u32[]{:S(2)}) collective-permute-start(bf16[64,1024]{1,0:T(8,128)(2,1)S(1)} %fusion.75), channel_id=1, source_target_pairs={{0,8},{1,9},{2,10},{3,11},{4,12},{5,13},{6,14},{7,15},{8,0},{9,1},... | collective-permute-start | bytes 393224 | tf_op jit(solution)/shard_map/ppermute | solution.py:39
  540.0 31.2 %collective-permute-start.52 = (bf16[1,256,1024]{2,1,0:T(8,128)(2,1)}, bf16[1,256,1024]{2,1,0:T(8,128)(2,1)}, u32[]{:S(2)}, u32[]{:S(2)}) collective-permute-start(bf16[1,256,1024]{2,1,0:T(8,128)(2,1)} %add_convert_fusion.12), channel_id=1, source_target_pairs={{0,2},{1,3},{2,0},{3,1},{4,6},{5,7},{6,4},{7,5},{8,10},{9,11},{10,... | collective-permute-start | bytes 1572872 | tf_op jit(solution)/shard_map/ppermute | solution.py:39
  541.1 30.0 %collective-permute-start.46 = (bf16[1,256,1024]{2,1,0:T(8,128)(2,1)}, bf16[1,256,1024]{2,1,0:T(8,128)(2,1)}, u32[]{:S(2)}, u32[]{:S(2)}) collective-permute-start(bf16[1,256,1024]{2,1,0:T(8,128)(2,1)} %add_convert_fusion.13), channel_id=1, source_target_pairs={{0,4},{1,5},{2,6},{3,7},{4,0},{5,1},{6,2},{7,3},{8,12},{9,13},{10,... | collective-permute-start | bytes 1572872 | tf_op jit(solution)/shard_map/ppermute | solution.py:39
  (124 other events, 969.8 us)
Sparse Core Ops, SparseCore 0:
  77.7 131.6 all-gather.2
